TPU v7x, 32 devices: a whole 2x2x4 slice. The times are simulated.
32 devices in a mesh: seq: 8 (over z, y), pipe: 4 (over x, core).
Axes of the slice: x: 2, y: 2, z: 4, core: 2. Of those that a mesh axis runs over, the one named last changes fastest.
Arguments:
- cotangent: bfloat16 [4, 4096, 4096], P('pipe', 'seq'), may hold values from -6 to 6
- input_map: bfloat16 [4, 4096, 128], P('pipe', 'seq'), may hold values from -0.30273438 to 0.30273438
- output_map: bfloat16 [4, 4096, 128], P('pipe', 'seq'), may hold values from -0.30273438 to 0.30273438
- log_decay: float32 [4, 4096, 32], P('pipe', 'seq'), may hold values from -2 to 0, as said below
- flight_starts: int32 [4, 4096], P('pipe', 'seq'), may hold values 0 or 1
- skip_gain: float32 [4, 32], P('pipe'), may hold values from 0.5 to 1.5
- in_weight: bfloat16 [4, 2048, 4096], P('pipe', 'seq'), may hold values from -0.09375 to 0.09375
Outputs:
- input_cotangent: bfloat16 [4, 4096, 2048], P('pipe', 'seq')
Inputs may be any that keep to these rules, and one draw needn't show every extreme that they name: log_decay is never positive.
All inputs are finite; a program needn't handle non-finite values. No bound on the sum of `flight_starts` on one device may be relied on, other than what follows from the above.
Results may differ from a plain program's by a relative error of at most 0.009.
Values may be sent and summed in bfloat16 or wider, within the bound.
No kernel may reach another device: no remote copies, remote signals or barrier semaphores. Data moves between devices by JAX's collectives and lax.ppermute only.
A program may use at most 192 MiB of HBM per device.

v0:
```python
import jax
import jax.numpy as jnp
from jax import lax
from jax.sharding import PartitionSpec as P

SPAN = 256


def entering(x, axis, combine, identity):
    size, mine = (lax.axis_size(axis), lax.axis_index(axis))
    everything = jax.tree.map(
        lambda part, kind: lax.all_gather(part.astype(kind), axis), x, (jnp.bfloat16, jnp.bfloat16)
    )
    start = jax.tree.map(
        lambda part, zero: jnp.broadcast_to(jnp.asarray(zero, part.dtype), part.shape), x, identity
    )

    def lap(k, before):
        at = size - 1 - k
        reached = at > mine
        new = combine(
            before, jax.tree.map(lambda part, own: part[at].astype(own.dtype), everything, x)
        )
        return jax.tree.map(lambda a, b: jnp.where(reached, a, b), new, before)

    return lax.fori_loop(0, size, lap, start)


def from_behind(block, axis, distance):
    devices = range(lax.axis_size(axis))
    route = [((i - distance) % len(devices), i) for i in devices]
    return lax.ppermute(block, axis, route)


def compose(earlier, later):
    keep_one, state_one = earlier
    keep_two, state_two = later
    return (keep_one * keep_two, state_two + keep_two[..., None, None] * state_one)


def body(cotangent, input_map, output_map, log_decay, flight_starts, skip_gain, in_weight):
    upstream = cotangent[0]
    heads = skip_gain.shape[1]
    width = input_map.shape[2]
    tokens = upstream.shape[0]
    head_size = upstream.shape[1] // heads
    blocks = tokens // SPAN
    grads = upstream.reshape(blocks, SPAN, heads, head_size)
    writes = input_map[0].reshape(blocks, SPAN, width)
    reads = output_map[0].reshape(blocks, SPAN, width)
    running = jnp.cumsum(log_decay[0].reshape(blocks, SPAN, heads), axis=1)
    counts = jnp.cumsum(flight_starts[0].reshape(blocks, SPAN), axis=1)
    keeps = jnp.where((counts[:, -1] == 0)[:, None], jnp.exp(running[:, -1, :]), 0.0)
    opened = jnp.where((counts == 0)[:, :, None], jnp.exp(running), 0.0)
    scaled_map = (opened[..., None] * reads.astype(jnp.float32)[:, :, None, :]).astype(jnp.bfloat16)
    block_states = jnp.einsum(
        "kthp,kthn->khpn", grads, scaled_map, preferred_element_type=jnp.float32
    )

    def fold_block(carry, item):
        return (compose(carry, item), None)

    start = (jnp.ones((heads,), jnp.float32), jnp.zeros((heads, head_size, width), jnp.float32))
    (device_keep, device_state), _ = lax.scan(
        fold_block, start, (keeps, block_states), reverse=True
    )
    _, after = entering((device_keep, device_state), "seq", compose, start)
    element_offset = jnp.arange(SPAN)
    upper = element_offset[:, None] <= element_offset[None, :]
    gains = skip_gain[0]

    def one_block(later, item):
        grad_block, write_block, read_block, run_block, count_block, keep_block, state_block = item
        scores = jnp.dot(write_block, read_block.T, preferred_element_type=jnp.float32)
        linked = upper & (count_block[:, None] == count_block[None, :])
        spread = run_block.T[:, None, :] - run_block.T[:, :, None]
        weight = jnp.where(
            linked[None], jnp.exp(jnp.where(linked[None], spread, 0.0)) * scores[None], 0.0
        ).astype(jnp.bfloat16)
        local = jnp.einsum("hst,thp->shp", weight, grad_block, preferred_element_type=jnp.float32)
        tail = jnp.where(
            (count_block == count_block[-1])[:, None],
            jnp.exp(run_block[-1][None, :] - run_block),
            0.0,
        )
        far = jnp.einsum(
            "hpn,sn->shp",
            later.astype(jnp.bfloat16),
            write_block,
            preferred_element_type=jnp.float32,
        )
        total = (
            local + tail[:, :, None] * far + gains[None, :, None] * grad_block.astype(jnp.float32)
        )
        earlier_state = state_block + keep_block[:, None, None] * later
        return (earlier_state, total.astype(jnp.bfloat16).reshape(SPAN, heads * head_size))

    _, pieces = lax.scan(
        one_block, after, (grads, writes, reads, running, counts, keeps, block_states), reverse=True
    )
    scan_grad = pieces.reshape(tokens, heads * head_size)
    feature_grad = lax.dot_general(
        scan_grad,
        lax.all_gather(in_weight[0], "seq", axis=0, tiled=True),
        (((1,), (1,)), ((), ())),
        preferred_element_type=jnp.float32,
    ).astype(jnp.bfloat16)
    result = feature_grad.reshape(1, tokens, feature_grad.shape[1])
    return from_behind(result, "pipe", -1)


def solution(mesh):
    placed = (
        P("pipe", "seq", None),
        P("pipe", "seq", None),
        P("pipe", "seq", None),
        P("pipe", "seq", None),
        P("pipe", "seq"),
        P("pipe", None),
        P("pipe", "seq", None),
    )
    return jax.shard_map(
        body, mesh=mesh, in_specs=placed, out_specs=P("pipe", "seq", None), check_vma=False
    )
```

profile of v0, /device:TPU:9, one launch (start us, length us, event | category | flops | bytes accessed | tf_op | source)
XLA Modules:
  0.0 434.5 jit_solution(10122095510348551693)
XLA Ops:
  6.5 1.3 reduce-window.14
  8.3 0.9 reshape_squeeze.13
  9.2 1.2 reduce-window.16
  10.8 5.5 %copy.46 = bf16[64,8,32,128]{3,2,1,0:T(8,128)(2,1)} copy(bf16[64,8,32,128]{3,1,2,0:T(8,128)(2,1)} %bitcast.134) | data formatting | bytes 8388608
  16.4 6.7 %fusion.40 = f32[2,32,128,128]{2,3,1,0:T(8,128)} fusion(bf16[2,256,32,128]{3,2,1,0:T(8,128)(2,1)} %bitcast.132, f32[2,256,128]{1,2,0:T(8,128)S(1)} %copy.34, f32[2,256,32]{1,2,0:T(8,128)S(1)} %exponential_select_fusion), kind=kOutput, calls=%fused_computation.54 | convolution fusion | flops 541065216 | bytes 8716288 | tf_op jit(solution)/shard_map/kthp,kthn->khpn/dot_general | solution.py:56
  23.1 5.6 %copy.36 = f32[2,32,128,128]{3,2,1,0:T(8,128)} copy(f32[2,32,128,128]{2,3,1,0:T(8,128)} %fusion.40) | data formatting | bytes 8388608
  29.2 4.1 while.51
  29.2 2.0 bitcast_add_fusion.6
  31.2 2.0 bitcast_add_fusion.6
  33.3 1.1 convert_element_type.87
  34.5 0.7 all-gather.8.cloned.1.call-update
  35.2 0.6 dynamic-slice
  36.8 16.3 %all-reduce = bf16[256]{0:T(256)(128)(2,1)S(1)} all-reduce(bf16[256]{0:T(256)(128)(2,1)S(1)} %dynamic-update-slice), channel_id=3, replica_groups=mesh['seq'=8,'pipe'=4] {'seq'}, use_global_device_ids=true, to_apply=%add | all-reduce | flops 256 | bytes 1024
  53.2 105.6 %all-gather.6.cloned.1.call-done = bf16[256,128,128]{2,1,0:T(8,128)(2,1)} async-done(((bf16[32,128,128]{2,1,0:T(8,128)(2,1)}), bf16[256,128,128]{2,1,0:T(8,128)(2,1)}) %all-gather.6.cloned.1.call-update) | async-done | bytes 8388624 | tf_op jit(solution)/shard_map/all_gather | solution.py:12
  158.8 18.5 %while.52 = (s32[]{:T(128)}, f32[32,128,128]{2,1,0:T(8,128)S(1)}, s32[]{:T(128)}, bf16[8,32,128,128]{3,2,1,0:T(8,128)(2,1)}, bf16[8,32]{1,0:T(8,128)(2,1)S(1)}, ...) while((s32[]{:T(128)}, f32[32,128,128]{2,1,0:T(8,128)S(1)}, s32[]{:T(128)}, ...), condition=%wide.region_7.8_spmd.clone, body=%wide.region_6.7_spmd.clone.sunk | while | flops 2621480 | bytes 5243367 | solution.py:26
  158.8 2.2 fusion.70
  161.0 2.2 fusion.70
  163.3 2.2 fusion.70
  165.6 2.2 fusion.70
  167.8 2.3 fusion.70
  170.1 2.4 fusion.70
  172.6 2.3 fusion.70
  175.0 2.2 fusion.70
  177.3 2.4 broadcast_in_dim.113.clone
  179.7 54.8 %while.50 = (s32[]{:T(128)}, f32[32,128,128]{2,1,0:T(8,128)S(1)}, bf16[2,256,4096]{2,1,0:T(8,128)(2,1)}, f32[2,32,128,128]{3,2,1,0:T(8,128)}, f32[2,32]{1,0:T(2,...) while((s32[]{:T(128)}, f32[32,128,128]{2,1,0:T(8,128)S(1)}, ...), condition=%wide.region_9.10_spmd.clone, body=%wide.region_8.9_spmd.clone.sunk | while | flops 840646912 | bytes 57678832 | solution.py:98
  180.0 3.3 constant_dynamic-slice_fusion.6
  183.4 4.3 copy.63
  187.6 5.0 %fusion.66 = f32[32,128,256]{2,1,0:T(8,128)} fusion(f32[256,256]{1,0:T(8,128)S(1)} %fusion.64, f32[32,256]{1,0:T(8,128)S(1)} %dynamic-slice_bitcast_fusion.4, pred[256,256]{1,0:T(8,128)(4,1)S(1)} %fusion.65, bf16[1,256,32,128]{1,3,2,0:T(8,128)(2,1)} %copy.63), kind=kOutput, calls=%fused_computation.10.clone.1 | convolution fusion | flops 547356672 | bytes 6651904 | tf_op jit(solution)/shard_map/while/body/eval_jaxpr/hst,thp->shp/dot_general | solution.py:80
  192.7 0.6 dynamic-slice.7
  193.2 0.6 broadcast_compare_fusion.3
  194.2 5.1 %fusion.68 = bf16[256,32,128]{0,2,1:T(8,128)(2,1)} fusion(f32[32,128,256]{2,1,0:T(8,128)} %fusion.66, bf16[1,256,32,128]{1,3,2,0:T(8,128)(2,1)} %copy.63, f32[32]{0:T(128)S(1)} %bitcast.144, f32[256,32]{0,1:T(8,128)S(1)} %fusion.67, f32[32,128,128]{2,1,0:T(8,128)S(1)} %get-tuple-element.845, bf16[2,256,128]{2,1,0:T(8,128)(2,1)S(1)} %get-tuple-element.866, ...), kind=kOutput, calls=%fused_computation.13.clone.1 | convolution fusion | flops 275251200 | bytes 10584580 | tf_op jit(solution)/shard_map/while/body/eval_jaxpr/hpn,sn->shp/dot_general | solution.py:86
  199.3 4.1 copy.64
  203.4 3.3 constant_dynamic-update-slice_fusion.2
  206.6 0.4 bitcast_add_fusion.5
  207.4 3.3 constant_dynamic-slice_fusion.6
  210.7 4.3 copy.63
  215.0 5.0 %fusion.66 = f32[32,128,256]{2,1,0:T(8,128)} fusion(f32[256,256]{1,0:T(8,128)S(1)} %fusion.64, f32[32,256]{1,0:T(8,128)S(1)} %dynamic-slice_bitcast_fusion.4, pred[256,256]{1,0:T(8,128)(4,1)S(1)} %fusion.65, bf16[1,256,32,128]{1,3,2,0:T(8,128)(2,1)} %copy.63), kind=kOutput, calls=%fused_computation.10.clone.1 | convolution fusion | flops 547356672 | bytes 6651904 | tf_op jit(solution)/shard_map/while/body/eval_jaxpr/hst,thp->shp/dot_general | solution.py:80
  220.0 0.6 dynamic-slice.7
  220.6 0.6 broadcast_compare_fusion.3
  221.6 5.1 %fusion.68 = bf16[256,32,128]{0,2,1:T(8,128)(2,1)} fusion(f32[32,128,256]{2,1,0:T(8,128)} %fusion.66, bf16[1,256,32,128]{1,3,2,0:T(8,128)(2,1)} %copy.63, f32[32]{0:T(128)S(1)} %bitcast.144, f32[256,32]{0,1:T(8,128)S(1)} %fusion.67, f32[32,128,128]{2,1,0:T(8,128)S(1)} %get-tuple-element.845, bf16[2,256,128]{2,1,0:T(8,128)(2,1)S(1)} %get-tuple-element.866, ...), kind=kOutput, calls=%fused_computation.13.clone.1 | convolution fusion | flops 275251200 | bytes 10584580 | tf_op jit(solution)/shard_map/while/body/eval_jaxpr/hpn,sn->shp/dot_general | solution.py:86
  226.7 4.1 copy.64
  230.7 3.3 constant_dynamic-update-slice_fusion.2
  234.1 0.4 bitcast_add_fusion.5
  234.5 152.2 %all-gather.8.cloned.1.call-done = bf16[1,2048,4096]{2,1,0:T(8,128)(2,1)} async-done(((bf16[1,256,4096]{2,1,0:T(8,128)(2,1)}), bf16[1,2048,4096]{2,1,0:T(8,128)(2,1)}) %all-gather.8.cloned.1.call-update) | async-done | bytes 16777232 | tf_op jit(solution)/shard_map/all_gather | solution.py:104
  386.7 13.7 %fusion.37 = bf16[1,512,2048]{2,1,0:T(8,128)(2,1)S(1)} fusion(bf16[512,4096]{1,0:T(8,128)(2,1)} %bitcast.135, bf16[1,2048,4096]{2,1,0:T(8,128)(2,1)} %all-gather.8.cloned.1.call-done), kind=kOutput, calls=%fused_computation.53 | convolution fusion | flops 8590983168 | bytes 23068672 | tf_op jit(solution)/shard_map/dot_general | solution.py:102
  400.4 1.1 collective-permute-start
  401.5 24.8 %collective-permute-done = bf16[1,512,2048]{2,1,0:T(8,128)(2,1)S(1)} collective-permute-done((bf16[1,512,2048]{2,1,0:T(8,128)(2,1)S(1)}, bf16[1,512,2048]{2,1,0:T(8,128)(2,1)S(1)}, u32[]{:S(2)}, u32[]{:S(2)}) %collective-permute-start) | collective-permute-done | bytes 2097184 | tf_op jit(solution)/shard_map/ppermute | solution.py:32
  426.3 1.3 copy.92
  (61 shorter events, 3.1 us)
Async XLA Ops:
  6.5 152.2 %all-gather.6.cloned.1.call-start = ((), (), s32[]{:S(2)}) async-start(), calls=%async_computation | async-start | bytes 9437184 | tf_op jit(solution)/shard_map/all_gather | solution.py:12
  10.8 5.5 %copy-start.2 = (bf16[1,512,128]{2,1,0:T(8,128)(2,1)S(1)}, bf16[1,512,128]{2,1,0:T(8,128)(2,1)}, u32[]{:S(2)}) copy-start(bf16[1,512,128]{2,1,0:T(8,128)(2,1)} %param.15) | copy-start | bytes 393220
  33.3 2.0 copy-start.4
  34.4 352.3 %all-gather.8.cloned.1.call-start = ((), (), s32[]{:S(2)}) async-start(), calls=%async_computation.1 | async-start | bytes 18874368 | tf_op jit(solution)/shard_map/all_gather | solution.py:104
  177.2 2.5 copy-start.1
  177.2 2.5 copy-start.3
  203.4 3.3 copy-start
  230.7 3.3 copy-start
  400.4 25.9 %collective-permute-start = (bf16[1,512,2048]{2,1,0:T(8,128)(2,1)S(1)}, bf16[1,512,2048]{2,1,0:T(8,128)(2,1)S(1)}, u32[]{:S(2)}, u32[]{:S(2)}) collective-permute-start(bf16[1,512,2048]{2,1,0:T(8,128)(2,1)S(1)} %fusion.37), channel_id=1, source_target_pairs={{1,0},{2,1},{3,2},{0,3},{5,4},{6,5},{7,6},{4,7},{9,8},{10,9},{11,1... | collective-permute-start | bytes 6291464 | tf_op jit(solution)/shard_map/ppermute | solution.py:32
Sparse Core Ops, SparseCore 0:
  34.5 124.1 all-gather.5
  160.9 225.7 all-gather.7
where the time goes:
time: 438 us; the launch traced here: 434 us
  waiting for transfers between devices  283 us (65%)
  local copies, waits for them, and re-layouts  48.9 us (11%)
  matrix products  41 us (9%)
  other arithmetic  29 us (7%)
  blocking collectives  16.3 us (4%)
  between operations  14.3 us (3%)
    all_gather x1, waiting for transfers between devices, body(): lax.all_gather(in_weight[0], 'seq', axis=0, tiled=True)  152 us
    all_gather x1, waiting for transfers between devices, entering(): lax.all_gather(part.astype(kind), axis)  106 us
    ppermute x1, waiting for transfers between devices, from_behind(): return lax.ppermute(block, axis, route)  24.8 us
    select_n x8, other arithmetic, lap(): return jax.tree.map(lambda a, b: jnp.where(reached, a, b), new, before)  18.1 us
    unnamed x1, blocking collectives  16.3 us
    dynamic_slice x6, local copies, waits for them, and re-layouts, body(): lax.scan(one_block, after, (grads, writes, reads, running, counts, keeps,...  15.2 us
    dynamic_update_slice x4, local copies, waits for them, and re-layouts, body(): lax.scan(one_block, after, (grads, writes, reads, running, counts, keeps,...  14.7 us
    dot_general x1, matrix products, body(): lax.dot_general(scan_grad, lax.all_gather(in_weight[0], 'seq', axis=0, ti...  13.7 us
  transfers between devices with their start and end apart: 3, of which 3 were waited for; matrix products, arithmetic and copies ran while one was open for 18% of the time, Pallas kernels for 0%

commit v1 on v0

v1 whole, which is shorter than its diff:
```python
import functools

import jax
import jax.numpy as jnp
from jax import lax
from jax.experimental import pallas as pl
from jax.experimental.pallas import tpu as pltpu
from jax.sharding import PartitionSpec as P

CHUNK = 128
GROUP = 4
EXTRA = 16
BF16 = jnp.bfloat16
F32 = jnp.float32


def cycle_of(n):
    columns = 1
    while (2 * columns) ** 2 <= n:
        columns *= 2
    rows = n // columns
    if columns == 1:
        return list(range(n))
    order = []
    for z in range(rows):
        ys = range(1, columns)
        order += [z * columns + y for y in (ys if z % 2 == 0 else reversed(ys))]
    return order + [z * columns for z in reversed(range(rows))]


def state_kernel(reads_ref, open_ref, cot_ref, keep_ref, out_ref):
    reads = reads_ref[...].astype(F32)
    width = reads.shape[0]
    for j in range(GROUP):
        scaled = (reads * open_ref[0, j : j + 1, :]).astype(BF16)
        state = jnp.dot(
            scaled, cot_ref[:, j * 128 : (j + 1) * 128], preferred_element_type=F32
        )
        out_ref[j, :width, :] = state.astype(BF16)
        keep = jnp.broadcast_to(keep_ref[0, j : j + 1, :], (EXTRA, 128))
        high = keep.astype(BF16)
        low = (keep - high.astype(F32)).astype(BF16)
        top = lax.broadcasted_iota(jnp.int32, (EXTRA, 128), 0) < EXTRA // 2
        out_ref[j, width:, :] = jnp.where(top, high.astype(F32), low.astype(F32)).astype(BF16)


def fold_kernel(size, width, in_ref, out_ref):
    shape = out_ref.shape[1:]
    later = jnp.zeros(shape, F32)
    for at in reversed(range(size)):
        out_ref[at] = later.astype(BF16)
        if at:
            state = in_ref[at, :, :width, :].astype(F32)
            high = in_ref[at, :, width : width + 1, :].astype(F32)
            low = in_ref[at, :, width + EXTRA // 2 : width + EXTRA // 2 + 1, :].astype(F32)
            later = state + (high + low) * later


def scan_kernel(
    chunks, writes_ref, reads_ref, readst_ref, cntc_ref, cntr_ref, cum_ref, cumt_ref, tail_ref,
    open_ref, keep_ref, gain_ref, cot_ref, later_ref, out_ref, score_ref,
):
    @pl.when(pl.program_id(0) == 0)
    def _():
        row = lax.broadcasted_iota(jnp.int32, (CHUNK, CHUNK), 0)
        col = lax.broadcasted_iota(jnp.int32, (CHUNK, CHUNK), 1)
        for c in range(chunks):
            at = slice(c * CHUNK, (c + 1) * CHUNK)
            scores = lax.dot_general(
                writes_ref[at, :], reads_ref[at, :], (((1,), (1,)), ((), ())),
                preferred_element_type=F32,
            )
            linked = (row <= col) & (cntc_ref[at, :] == cntr_ref[:, at])
            score_ref[at, :] = jnp.where(linked, scores, 0.0)

    for j in range(GROUP):
        lane = slice(j * 128, (j + 1) * 128)
        later = later_ref[j].astype(F32)
        gain = gain_ref[0, j : j + 1, :]
        for c in reversed(range(chunks)):
            at = slice(c * CHUNK, (c + 1) * CHUNK)
            cot = cot_ref[at, lane]
            spread = cumt_ref[0, j : j + 1, at] - cum_ref[0, at, j : j + 1]
            weight = (jnp.exp(jnp.minimum(spread, 0.0)) * score_ref[at, :]).astype(BF16)
            reach = (tail_ref[0, at, j : j + 1] * writes_ref[at, :].astype(F32)).astype(BF16)
            total = jnp.dot(
                jnp.concatenate([weight, reach], axis=1),
                jnp.concatenate([cot, later.astype(BF16)], axis=0),
                preferred_element_type=F32,
            )
            out_ref[at, lane] = (total + gain * cot.astype(F32)).astype(BF16)
            if c:
                scaled = (readst_ref[:, at].astype(F32) * open_ref[0, j : j + 1, at]).astype(BF16)
                state = jnp.dot(scaled, cot, preferred_element_type=F32)
                later = state + keep_ref[0, c * GROUP + j : c * GROUP + j + 1, :] * later


def body(n, cotangent, input_map, output_map, log_decay, flight_starts, skip_gain, in_weight):
    cot = cotangent[0]
    writes, reads = input_map[0], output_map[0]
    heads = skip_gain.shape[1]
    width = writes.shape[1]
    tokens = cot.shape[0]
    size = cot.shape[1] // heads
    chunks = tokens // CHUNK
    groups = heads // GROUP
    mine = lax.axis_index("seq")

    cum = jnp.cumsum(log_decay[0].reshape(chunks, CHUNK, heads), axis=1)
    cnt = jnp.cumsum(flight_starts[0].reshape(chunks, CHUNK), axis=1)
    last, ends = cum[:, -1, :], cnt[:, -1]
    clear = (ends == 0)[:, None]
    keep = jnp.where(clear, jnp.exp(last), 0.0)
    tail = jnp.where((cnt == ends[:, None])[..., None], jnp.exp(last[:, None, :] - cum), 0.0)
    opened = jnp.where((cnt == 0)[..., None], jnp.exp(cum), 0.0)
    before = jnp.cumsum(last, axis=0) - last
    blocked = jnp.cumsum(ends) - ends
    whole = jnp.where(
        ((cnt == 0) & (blocked == 0)[:, None])[..., None], jnp.exp(cum + before[:, None, :]), 0.0
    )
    device_keep = jnp.where(jnp.sum(ends) == 0, jnp.exp(jnp.sum(last, axis=0)), 0.0)

    def rows_of(x):
        return x.reshape(tokens, groups, GROUP).transpose(1, 2, 0)

    def columns_of(x):
        return x.reshape(tokens, groups, GROUP).transpose(1, 0, 2)

    def wide(x):
        return jnp.broadcast_to(x[..., None], x.shape + (128,))

    reads_t = reads.T
    step3 = lambda g: (g, 0, 0)
    whole2 = lambda g: (0, 0)
    states = pl.pallas_call(
        state_kernel,
        grid=(groups,),
        in_specs=[
            pl.BlockSpec((width, tokens), whole2),
            pl.BlockSpec((1, GROUP, tokens), step3),
            pl.BlockSpec((tokens, GROUP * size), lambda g: (0, g)),
            pl.BlockSpec((1, GROUP, 128), step3),
        ],
        out_specs=pl.BlockSpec((GROUP, width + EXTRA, size), step3),
        out_shape=jax.ShapeDtypeStruct((heads, width + EXTRA, size), BF16),
        cost_estimate=pl.CostEstimate(
            flops=2 * tokens * width * heads * size,
            bytes_accessed=2 * tokens * heads * size,
            transcendentals=0,
        ),
        name="states",
    )(reads_t, rows_of(whole), cot, wide(device_keep.reshape(groups, GROUP)))

    held = lax.all_to_all(states, "seq", 0, 0, tiled=True)
    part = heads // n
    held = held.reshape(n, part, width + EXTRA, size)
    entering = pl.pallas_call(
        functools.partial(fold_kernel, n, width),
        out_shape=jax.ShapeDtypeStruct((n, part, width, size), BF16),
        cost_estimate=pl.CostEstimate(
            flops=2 * heads * width * size, bytes_accessed=4 * heads * width * size,
            transcendentals=0,
        ),
        name="fold",
    )(held)
    later = lax.all_to_all(entering.reshape(heads, width, size), "seq", 0, 0, tiled=True)

    scan_grad = pl.pallas_call(
        functools.partial(scan_kernel, chunks),
        grid=(groups,),
        in_specs=[
            pl.BlockSpec((tokens, width), whole2),
            pl.BlockSpec((tokens, width), whole2),
            pl.BlockSpec((width, tokens), whole2),
            pl.BlockSpec((tokens, 1), whole2),
            pl.BlockSpec((1, tokens), whole2),
            pl.BlockSpec((1, tokens, GROUP), step3),
            pl.BlockSpec((1, GROUP, tokens), step3),
            pl.BlockSpec((1, tokens, GROUP), step3),
            pl.BlockSpec((1, GROUP, tokens), step3),
            pl.BlockSpec((1, chunks * GROUP, 128), step3),
            pl.BlockSpec((1, GROUP, 128), step3),
            pl.BlockSpec((tokens, GROUP * size), lambda g: (0, g)),
            pl.BlockSpec((GROUP, width, size), step3),
        ],
        out_specs=pl.BlockSpec((tokens, GROUP * size), lambda g: (0, g)),
        out_shape=jax.ShapeDtypeStruct((tokens, heads * size), BF16),
        scratch_shapes=[pltpu.VMEM((tokens, CHUNK), F32)],
        cost_estimate=pl.CostEstimate(
            flops=6 * tokens * CHUNK * heads * size,
            bytes_accessed=4 * tokens * heads * size,
            transcendentals=tokens * CHUNK * heads,
        ),
        name="scan",
    )(
        writes, reads, reads_t, cnt.reshape(tokens, 1), cnt.reshape(1, tokens),
        columns_of(cum.reshape(tokens, heads)), rows_of(cum), columns_of(tail),
        rows_of(opened),
        wide(keep.reshape(chunks, groups, GROUP).transpose(1, 0, 2).reshape(groups, -1)),
        wide(skip_gain[0].reshape(groups, GROUP)), cot, later,
    )

    order = cycle_of(n)
    place = [order.index(s) for s in range(n)]
    forth = [(order[i], order[(i + 1) % n]) for i in range(n)]
    back = [(b, a) for a, b in forth]
    pipes = lax.axis_size("pipe")
    route = [(i, (i - 1) % pipes) for i in range(pipes)]
    weight = in_weight[0]
    rows = weight.shape[0]
    half = rows // 2
    table = jnp.array(
        [[order[(place[s] - k) % n] for k in range(n)] for s in range(n)], jnp.int32
    )[mine]
    result = jnp.zeros((tokens, n * rows), BF16)

    def finish(result, block, source, offset):
        piece = lax.dot_general(
            scan_grad, block, (((1,), (1,)), ((), ())), preferred_element_type=F32
        ).astype(BF16)
        piece = lax.ppermute(piece, "pipe", route)
        return lax.dynamic_update_slice(result, piece, (0, source * rows + offset))

    result = finish(result, weight, mine, 0)
    streams = []
    for h in range(2):
        for way in (1, -1):
            steps = n // 2 - (0 if (h == 0) == (way == 1) else 1)
            streams.append([weight[h * half : (h + 1) * half], h * half, way, steps])
    for k in range(1, n // 2 + 1):
        for stream in streams:
            block, offset, way, steps = stream
            if k <= steps:
                block = lax.ppermute(block, "seq", forth if way == 1 else back)
                stream[0] = block
                result = finish(result, block, table[(way * k) % n], offset)
    return result[None]


def solution(mesh):
    n = mesh.shape["seq"]
    placed = (
        P("pipe", "seq", None),
        P("pipe", "seq", None),
        P("pipe", "seq", None),
        P("pipe", "seq", None),
        P("pipe", "seq"),
        P("pipe", None),
        P("pipe", "seq", None),
    )
    return jax.shard_map(
        functools.partial(body, n),
        mesh=mesh,
        in_specs=placed,
        out_specs=P("pipe", "seq", None),
        check_vma=False,
    )
```

time: 438 us -> 290 us (0.66)
  waiting for transfers between devices: 283 us -> 168 us
  local copies, waits for them, and re-layouts: 48.9 us -> 16.5 us
  starting transfers between devices: 1.17 us -> 29 us
  Pallas kernels: 0 us -> 25.6 us
  other arithmetic: 29 us -> 3.82 us
  blocking collectives: 16.3 us -> 0 us
  between operations: 14.3 us -> 5.55 us
    all_gather x2 -> x0, waiting for transfers between devices: 258 us -> none  [the longest x1 152 us: body(): lax.all_gather(in_weight[0], 'seq', axis=0, tiled=True)]
    ppermute x1 -> x29, waiting for transfers between devices: 24.8 us -> 168 us  [the longest x14 129 us: body(): block = lax.ppermute(block, 'seq', forth if way == 1 else back)]
    pallas_call x0 -> x3, Pallas kernels: none -> 25.6 us  [the longest x1 16 us: body(): pl.pallas_call(functools.partial(scan_kernel, chunks), grid=(groups,), in...]
    select_n x12 -> x1, other arithmetic: 18.4 us -> 0.01 us  [body(): jnp.where(jnp.sum(ends) == 0, jnp.exp(jnp.sum(last, axis=0)), 0.0)]
    ppermute x1 -> x29, starting transfers between devices: 1.12 us -> 19.2 us  [the longest x14 13.2 us: body(): block = lax.ppermute(block, 'seq', forth if way == 1 else back)]
    unnamed x1 -> x0, blocking collectives: 16.3 us -> none
    dynamic_slice x6 -> x1, local copies, waits for them, and re-layouts: 15.2 us -> 0.69 us  [body(): jnp.array([[order[(place[s] - k) % n] for k in range(n)] for s in range(n...]
    dynamic_update_slice x4 -> x15, local copies, waits for them, and re-layouts: 14.7 us -> 1.17 us  [finish(): return lax.dynamic_update_slice(result, piece, (0, source * rows + offset))]
  transfers between devices with their start and end apart: 3 -> 31, of which waited for: 3 -> 15; matrix products, arithmetic and copies ran while one was open for 18% -> 17% of each run, Pallas kernels for 0% -> 6%
where the time goes in v1:
time: 290 us; the launch traced here: 287 us
  waiting for transfers between devices  168 us (58%)
  matrix products  38.3 us (13%)
  starting transfers between devices  29 us (10%)
  Pallas kernels  25.6 us (9%)
  local copies, waits for them, and re-layouts  16.5 us (6%)
  between operations  5.55 us (2%)
  other arithmetic  3.82 us (1%)
    ppermute x14, waiting for transfers between devices, body(): block = lax.ppermute(block, 'seq', forth if way == 1 else back)  129 us
    ppermute x15, waiting for transfers between devices, finish(): piece = lax.ppermute(piece, 'pipe', route)  39.5 us
    dot_general x15, matrix products, finish(): lax.dot_general(scan_grad, block, (((1,), (1,)), ((), ())), preferred_ele...  38.3 us
    pallas_call x1, Pallas kernels, body(): pl.pallas_call(functools.partial(scan_kernel, chunks), grid=(groups,), in...  16 us
    ppermute x14, starting transfers between devices, body(): block = lax.ppermute(block, 'seq', forth if way == 1 else back)  13.2 us
    pallas_call x1, Pallas kernels, body(): pl.pallas_call(state_kernel, grid=(groups,), in_specs=[pl.BlockSpec((widt...  7.15 us
    ppermute x15, starting transfers between devices, finish(): piece = lax.ppermute(piece, 'pipe', route)  6.01 us
    all_to_all x1, starting transfers between devices, body(): held = lax.all_to_all(states, 'seq', 0, 0, tiled=True)  5.85 us
  transfers between devices with their start and end apart: 31, of which 15 were waited for; matrix products, arithmetic and copies ran while one was open for 17% of the time, Pallas kernels for 6%

profile of v1, /device:TPU:9, one launch (start us, length us, event | category | flops | bytes accessed | tf_op | source)
XLA Modules:
  0.0 287.1 jit_solution(354567753742383660)
XLA Ops:
  4.1 1.7 copy.19
  7.8 7.2 %states.1 = bf16[32,144,128]{2,1,0:T(8,128)(2,1)} custom-call(bf16[128,512]{1,0:T(8,128)(2,1)} %bitcast.117, f32[8,4,512]{2,1,0:T(4,128)} %get-tuple-element.16.open_ref, bf16[512,4096]{1,0:T(8,128)(2,1)} %bitcast.113, f32[8,4,128]{2,1,0:T(4,128)} %broadcast_in_dim.114.keep_ref), custom_call_target="tpu_custom_call" | custom-call | flops 536870912 | bytes 4194304 | tf_op jit(solution)/shard_map/states/pallas_call | solution.py:135
  14.9 5.9 %all-to-all-start = ((bf16[32,144,128]{2,1,0:T(8,128)(2,1)}), bf16[32,144,128]{2,1,0:T(8,128)(2,1)S(1)}, u32[]{:S(2)}, u32[]{:S(2)}) async-start(bf16[32,144,128]{2,1,0:T(8,128)(2,1)} %states.1), calls=%async_computation | async-start | bytes 2359296 | tf_op jit(solution)/shard_map/all_to_all | solution.py:154
  20.8 1.5 slice_bitcast_fusion
  22.3 1.2 collective-permute-start.7
  23.8 1.4 collective-permute-start.3
  25.3 44.1 %collective-permute-done.7 = bf16[128,4096]{1,0:T(8,128)(2,1)} collective-permute-done((bf16[128,4096]{1,0:T(8,128)(2,1)}, bf16[128,4096]{1,0:T(8,128)(2,1)}, u32[]{:S(2)}, u32[]{:S(2)}) %collective-permute-start.7) | collective-permute-done | bytes 1048608 | tf_op jit(solution)/shard_map/ppermute | solution.py:234
  69.3 2.2 collective-permute-start.15
  72.6 2.5 fold.1
  75.1 3.9 %all-to-all-start.1 = ((bf16[32,128,128]{2,1,0:T(8,128)(2,1)}), bf16[32,128,128]{2,1,0:T(8,128)(2,1)S(1)}, u32[]{:S(2)}, u32[]{:S(2)}) async-start(bf16[32,128,128]{2,1,0:T(8,128)(2,1)} %bitcast.116), calls=%async_computation.1 | async-start | bytes 2097152 | tf_op jit(solution)/shard_map/all_to_all | solution.py:166
  79.0 13.4 %collective-permute-done.5 = bf16[128,4096]{1,0:T(8,128)(2,1)} collective-permute-done((bf16[128,4096]{1,0:T(8,128)(2,1)}, bf16[128,4096]{1,0:T(8,128)(2,1)}, u32[]{:S(2)}, u32[]{:S(2)}) %collective-permute-start.5) | collective-permute-done | bytes 1048608 | tf_op jit(solution)/shard_map/ppermute | solution.py:234
  92.4 1.6 collective-permute-start.11
  94.0 30.4 %collective-permute-done.15 = bf16[128,4096]{1,0:T(8,128)(2,1)} collective-permute-done((bf16[128,4096]{1,0:T(8,128)(2,1)}, bf16[128,4096]{1,0:T(8,128)(2,1)}, u32[]{:S(2)}, u32[]{:S(2)}) %collective-permute-start.15) | collective-permute-done | bytes 1048608 | tf_op jit(solution)/shard_map/ppermute | solution.py:234
  124.4 2.7 collective-permute-start.23
  135.4 2.0 copy.29.tail_ref
  137.4 2.0 copy.28.cum_ref
  139.4 20.5 %collective-permute-done.13 = bf16[128,4096]{1,0:T(8,128)(2,1)} collective-permute-done((bf16[128,4096]{1,0:T(8,128)(2,1)}, bf16[128,4096]{1,0:T(8,128)(2,1)}, u32[]{:S(2)}, u32[]{:S(2)}) %collective-permute-start.13) | collective-permute-done | bytes 1048608 | tf_op jit(solution)/shard_map/ppermute | solution.py:234
  159.9 1.6 collective-permute-start.19
  161.5 20.3 %collective-permute-done.23 = bf16[128,4096]{1,0:T(8,128)(2,1)} collective-permute-done((bf16[128,4096]{1,0:T(8,128)(2,1)}, bf16[128,4096]{1,0:T(8,128)(2,1)}, u32[]{:S(2)}, u32[]{:S(2)}) %collective-permute-start.23) | collective-permute-done | bytes 1048608 | tf_op jit(solution)/shard_map/ppermute | solution.py:234
  181.7 2.2 collective-permute-start.27
  185.4 16.0 %scan.1 = bf16[512,4096]{1,0:T(8,128)(2,1)} custom-call(bf16[512,128]{1,0:T(8,128)(2,1)} %bitcast.123, bf16[512,128]{1,0:T(8,128)(2,1)} %bitcast.122, bf16[128,512]{1,0:T(8,128)(2,1)} %bitcast.118, s32[512,1]{1,0:T(8,128)} %copy.27.cntc_ref, s32[1,512]{1,0:T(1,128)} %bitcast.125, f32[8,512,4]{2,1,0:T(8,128)} %copy.28.cum_ref, f32[8,4,512]{2,1,0:T(4,128)} %bitcast.120, ...), custom_call_target="tpu_custom_call" | custom-call | flops 1610612736 | bytes 8388608 | tf_op jit(solution)/shard_map/scan/pallas_call | solution.py:168
  201.4 3.6 %fusion.2 = bf16[512,256]{1,0:T(8,128)(2,1)S(1)} fusion(bf16[512,4096]{1,0:T(8,128)(2,1)} %scan.1, bf16[1,256,4096]{2,1,0:T(8,128)(2,1)S(1)} %copy-done.4), kind=kOutput, calls=%fused_computation.2 | convolution fusion | flops 1073872896 | bytes 6553600 | tf_op jit(solution)/shard_map/dot_general | solution.py:218
  205.1 1.9 collective-permute-start
  206.9 2.5 convolution_convert_fusion.10
  209.4 2.5 convolution_convert_fusion.6
  211.9 2.5 convolution_convert_fusion.2
  214.4 2.5 convolution_convert_fusion.11
  216.9 2.5 convolution_convert_fusion.7
  219.4 2.5 convolution_convert_fusion.12
  221.9 2.5 convolution_convert_fusion.8
  224.3 2.5 convolution_convert_fusion.13
  226.8 2.5 convolution_convert_fusion.9
  229.3 2.5 convolution_convert_fusion.5
  232.1 2.5 convolution_convert_fusion.3
  234.6 1.6 collective-permute-start.16
  236.2 2.5 convolution_convert_fusion.4
  239.1 4.1 %collective-permute-done.2 = bf16[512,128]{1,0:T(8,128)(2,1)S(1)} collective-permute-done((bf16[512,128]{1,0:T(8,128)(2,1)S(1)}, bf16[512,128]{1,0:T(8,128)(2,1)S(1)}, u32[]{:S(2)}, u32[]{:S(2)}) %collective-permute-start.2) | collective-permute-done | bytes 131104 | tf_op jit(solution)/shard_map/ppermute | solution.py:221
  243.2 4.3 %collective-permute-done.4 = bf16[512,128]{1,0:T(8,128)(2,1)S(1)} collective-permute-done((bf16[512,128]{1,0:T(8,128)(2,1)S(1)}, bf16[512,128]{1,0:T(8,128)(2,1)S(1)}, u32[]{:S(2)}, u32[]{:S(2)}) %collective-permute-start.4) | collective-permute-done | bytes 131104 | tf_op jit(solution)/shard_map/ppermute | solution.py:221
  247.6 4.3 %collective-permute-done.6 = bf16[512,128]{1,0:T(8,128)(2,1)S(1)} collective-permute-done((bf16[512,128]{1,0:T(8,128)(2,1)S(1)}, bf16[512,128]{1,0:T(8,128)(2,1)S(1)}, u32[]{:S(2)}, u32[]{:S(2)}) %collective-permute-start.6) | collective-permute-done | bytes 131104 | tf_op jit(solution)/shard_map/ppermute | solution.py:221
  252.8 5.0 %collective-permute-done.10 = bf16[512,128]{1,0:T(8,128)(2,1)S(1)} collective-permute-done((bf16[512,128]{1,0:T(8,128)(2,1)S(1)}, bf16[512,128]{1,0:T(8,128)(2,1)S(1)}, u32[]{:S(2)}, u32[]{:S(2)}) %collective-permute-start.10) | collective-permute-done | bytes 131104 | tf_op jit(solution)/shard_map/ppermute | solution.py:221
  257.8 4.3 %collective-permute-done.12 = bf16[512,128]{1,0:T(8,128)(2,1)S(1)} collective-permute-done((bf16[512,128]{1,0:T(8,128)(2,1)S(1)}, bf16[512,128]{1,0:T(8,128)(2,1)S(1)}, u32[]{:S(2)}, u32[]{:S(2)}) %collective-permute-start.12) | collective-permute-done | bytes 131104 | tf_op jit(solution)/shard_map/ppermute | solution.py:221
  262.2 4.3 %collective-permute-done.14 = bf16[512,128]{1,0:T(8,128)(2,1)S(1)} collective-permute-done((bf16[512,128]{1,0:T(8,128)(2,1)S(1)}, bf16[512,128]{1,0:T(8,128)(2,1)S(1)}, u32[]{:S(2)}, u32[]{:S(2)}) %collective-permute-start.14) | collective-permute-done | bytes 131104 | tf_op jit(solution)/shard_map/ppermute | solution.py:221
  267.3 5.0 %collective-permute-done.18 = bf16[512,128]{1,0:T(8,128)(2,1)S(1)} collective-permute-done((bf16[512,128]{1,0:T(8,128)(2,1)S(1)}, bf16[512,128]{1,0:T(8,128)(2,1)S(1)}, u32[]{:S(2)}, u32[]{:S(2)}) %collective-permute-start.18) | collective-permute-done | bytes 131104 | tf_op jit(solution)/shard_map/ppermute | solution.py:221
  272.4 4.3 %collective-permute-done.20 = bf16[512,128]{1,0:T(8,128)(2,1)S(1)} collective-permute-done((bf16[512,128]{1,0:T(8,128)(2,1)S(1)}, bf16[512,128]{1,0:T(8,128)(2,1)S(1)}, u32[]{:S(2)}, u32[]{:S(2)}) %collective-permute-start.20) | collective-permute-done | bytes 131104 | tf_op jit(solution)/shard_map/ppermute | solution.py:221
  276.9 2.5 convolution_convert_fusion.1
  279.5 2.5 convolution_convert_fusion
  282.6 1.2 collective-permute-done.26
  283.9 2.5 collective-permute-done.28
  (102 shorter events, 16.0 us)
Async XLA Ops:
  2.4 131.8 %copy-start.6 = (s32[4,128]{1,0:T(4,128)}, s32[4,128]{1,0:T(4,128)S(1)}, u32[]{:S(2)}) copy-start(s32[4,128]{1,0:T(4,128)S(1)} %reduce_window_sum.40) | copy-start | bytes 6148
  5.8 131.6 %copy-start.5 = (f32[512,8,4]{0,2,1:T(4,128)}, f32[512,8,4]{0,2,1:T(4,128)S(1)}, u32[]{:S(2)}) copy-start(f32[512,8,4]{0,2,1:T(4,128)S(1)} %reshape_reshape.3) | copy-start | bytes 196612
  14.9 5.9 %copy-start.4 = (bf16[1,256,4096]{2,1,0:T(8,128)(2,1)S(1)}, bf16[1,256,4096]{2,1,0:T(8,128)(2,1)}, u32[]{:S(2)}) copy-start(bf16[1,256,4096]{2,1,0:T(8,128)(2,1)} %param.14) | copy-start | bytes 6291460
  14.9 56.6 %all-to-all-start = ((bf16[32,144,128]{2,1,0:T(8,128)(2,1)}), bf16[32,144,128]{2,1,0:T(8,128)(2,1)S(1)}, u32[]{:S(2)}, u32[]{:S(2)}) async-start(bf16[32,144,128]{2,1,0:T(8,128)(2,1)} %states.1), calls=%async_computation | async-start | bytes 2359296 | tf_op jit(solution)/shard_map/all_to_all | solution.py:154
  22.3 47.0 %collective-permute-start.7 = (bf16[128,4096]{1,0:T(8,128)(2,1)}, bf16[128,4096]{1,0:T(8,128)(2,1)}, u32[]{:S(2)}, u32[]{:S(2)}) collective-permute-start(bf16[128,4096]{1,0:T(8,128)(2,1)} %get-tuple-element.13), channel_id=1, source_target_pairs={{12,4},{20,12},{28,20},{24,28},{16,24},{8,16},{0,8},{4,0},{13,5},{... | collective-permute-start | bytes 3145736 | tf_op jit(solution)/shard_map/ppermute | solution.py:234
  23.5 48.0 %collective-permute-start.1 = (bf16[128,4096]{1,0:T(8,128)(2,1)}, bf16[128,4096]{1,0:T(8,128)(2,1)}, u32[]{:S(2)}, u32[]{:S(2)}) collective-permute-start(bf16[128,4096]{1,0:T(8,128)(2,1)} %get-tuple-element.14), channel_id=1, source_target_pairs={{4,12},{12,20},{20,28},{28,24},{24,16},{16,8},{8,0},{0,4},{5,13},{... | collective-permute-start | bytes 3145736 | tf_op jit(solution)/shard_map/ppermute | solution.py:234
  23.8 68.6 %collective-permute-start.5 = (bf16[128,4096]{1,0:T(8,128)(2,1)}, bf16[128,4096]{1,0:T(8,128)(2,1)}, u32[]{:S(2)}, u32[]{:S(2)}) collective-permute-start(bf16[128,4096]{1,0:T(8,128)(2,1)} %get-tuple-element.13), channel_id=1, source_target_pairs={{4,12},{12,20},{20,28},{28,24},{24,16},{16,8},{8,0},{0,4},{5,13},{... | collective-permute-start | bytes 3145736 | tf_op jit(solution)/shard_map/ppermute | solution.py:234
  23.8 68.6 %collective-permute-start.3 = (bf16[128,4096]{1,0:T(8,128)(2,1)}, bf16[128,4096]{1,0:T(8,128)(2,1)}, u32[]{:S(2)}, u32[]{:S(2)}) collective-permute-start(bf16[128,4096]{1,0:T(8,128)(2,1)} %get-tuple-element.14), channel_id=1, source_target_pairs={{12,4},{20,12},{28,20},{24,28},{16,24},{8,16},{0,8},{4,0},{13,5},{... | collective-permute-start | bytes 3145736 | tf_op jit(solution)/shard_map/ppermute | solution.py:234
  69.3 55.1 %collective-permute-start.15 = (bf16[128,4096]{1,0:T(8,128)(2,1)}, bf16[128,4096]{1,0:T(8,128)(2,1)}, u32[]{:S(2)}, u32[]{:S(2)}) collective-permute-start(bf16[128,4096]{1,0:T(8,128)(2,1)} %collective-permute-done.7), channel_id=1, source_target_pairs={{12,4},{20,12},{28,20},{24,28},{16,24},{8,16},{0,8},{4,0},{13,5},{... | collective-permute-start | bytes 3145736 | tf_op jit(solution)/shard_map/ppermute | solution.py:234
  71.5 55.6 %collective-permute-start.9 = (bf16[128,4096]{1,0:T(8,128)(2,1)}, bf16[128,4096]{1,0:T(8,128)(2,1)}, u32[]{:S(2)}, u32[]{:S(2)}) collective-permute-start(bf16[128,4096]{1,0:T(8,128)(2,1)} %collective-permute-done.1), channel_id=1, source_target_pairs={{4,12},{12,20},{20,28},{28,24},{24,16},{16,8},{8,0},{0,4},{5,13},{... | collective-permute-start | bytes 3145736 | tf_op jit(solution)/shard_map/ppermute | solution.py:234
  71.5 1.0 copy-start
  72.6 60.9 %copy-start.7 = (f32[1,32]{1,0:T(1,128)S(1)}, f32[1,32]{1,0:T(1,128)}, u32[]{:S(2)}) copy-start(f32[1,32]{1,0:T(1,128)} %param.13) | copy-start | bytes 388
  75.1 108.9 %all-to-all-start.1 = ((bf16[32,128,128]{2,1,0:T(8,128)(2,1)}), bf16[32,128,128]{2,1,0:T(8,128)(2,1)S(1)}, u32[]{:S(2)}, u32[]{:S(2)}) async-start(bf16[32,128,128]{2,1,0:T(8,128)(2,1)} %bitcast.116), calls=%async_computation.1 | async-start | bytes 2097152 | tf_op jit(solution)/shard_map/all_to_all | solution.py:166
  92.4 67.5 %collective-permute-start.13 = (bf16[128,4096]{1,0:T(8,128)(2,1)}, bf16[128,4096]{1,0:T(8,128)(2,1)}, u32[]{:S(2)}, u32[]{:S(2)}) collective-permute-start(bf16[128,4096]{1,0:T(8,128)(2,1)} %collective-permute-done.5), channel_id=1, source_target_pairs={{4,12},{12,20},{20,28},{28,24},{24,16},{16,8},{8,0},{0,4},{5,13},{... | collective-permute-start | bytes 3145736 | tf_op jit(solution)/shard_map/ppermute | solution.py:234
  92.4 67.5 %collective-permute-start.11 = (bf16[128,4096]{1,0:T(8,128)(2,1)}, bf16[128,4096]{1,0:T(8,128)(2,1)}, u32[]{:S(2)}, u32[]{:S(2)}) collective-permute-start(bf16[128,4096]{1,0:T(8,128)(2,1)} %collective-permute-done.3), channel_id=1, source_target_pairs={{12,4},{20,12},{28,20},{24,28},{16,24},{8,16},{0,8},{4,0},{13,5},{... | collective-permute-start | bytes 3145736 | tf_op jit(solution)/shard_map/ppermute | solution.py:234
  124.4 57.3 %collective-permute-start.23 = (bf16[128,4096]{1,0:T(8,128)(2,1)}, bf16[128,4096]{1,0:T(8,128)(2,1)}, u32[]{:S(2)}, u32[]{:S(2)}) collective-permute-start(bf16[128,4096]{1,0:T(8,128)(2,1)} %collective-permute-done.15), channel_id=1, source_target_pairs={{12,4},{20,12},{28,20},{24,28},{16,24},{8,16},{0,8},{4,0},{13,5},{... | collective-permute-start | bytes 3145736 | tf_op jit(solution)/shard_map/ppermute | solution.py:234
  127.1 56.8 %collective-permute-start.17 = (bf16[128,4096]{1,0:T(8,128)(2,1)}, bf16[128,4096]{1,0:T(8,128)(2,1)}, u32[]{:S(2)}, u32[]{:S(2)}) collective-permute-start(bf16[128,4096]{1,0:T(8,128)(2,1)} %collective-permute-done.9), channel_id=1, source_target_pairs={{4,12},{12,20},{20,28},{28,24},{24,16},{16,8},{8,0},{0,4},{5,13},{... | collective-permute-start | bytes 3145736 | tf_op jit(solution)/shard_map/ppermute | solution.py:234
  159.9 71.9 %collective-permute-start.21 = (bf16[128,4096]{1,0:T(8,128)(2,1)}, bf16[128,4096]{1,0:T(8,128)(2,1)}, u32[]{:S(2)}, u32[]{:S(2)}) collective-permute-start(bf16[128,4096]{1,0:T(8,128)(2,1)} %collective-permute-done.13), channel_id=1, source_target_pairs={{4,12},{12,20},{20,28},{28,24},{24,16},{16,8},{8,0},{0,4},{5,13},{... | collective-permute-start | bytes 3145736 | tf_op jit(solution)/shard_map/ppermute | solution.py:234
  159.9 74.7 %collective-permute-start.19 = (bf16[128,4096]{1,0:T(8,128)(2,1)}, bf16[128,4096]{1,0:T(8,128)(2,1)}, u32[]{:S(2)}, u32[]{:S(2)}) collective-permute-start(bf16[128,4096]{1,0:T(8,128)(2,1)} %collective-permute-done.11), channel_id=1, source_target_pairs={{12,4},{20,12},{28,20},{24,28},{16,24},{8,16},{0,8},{4,0},{13,5},{... | collective-permute-start | bytes 3145736 | tf_op jit(solution)/shard_map/ppermute | solution.py:234
  181.7 97.7 %collective-permute-start.27 = (bf16[128,4096]{1,0:T(8,128)(2,1)}, bf16[128,4096]{1,0:T(8,128)(2,1)}, u32[]{:S(2)}, u32[]{:S(2)}) collective-permute-start(bf16[128,4096]{1,0:T(8,128)(2,1)} %collective-permute-done.23), channel_id=1, source_target_pairs={{12,4},{20,12},{28,20},{24,28},{16,24},{8,16},{0,8},{4,0},{13,5},{... | collective-permute-start | bytes 3145736 | tf_op jit(solution)/shard_map/ppermute | solution.py:234
  183.9 93.0 %collective-permute-start.25 = (bf16[128,4096]{1,0:T(8,128)(2,1)}, bf16[128,4096]{1,0:T(8,128)(2,1)}, u32[]{:S(2)}, u32[]{:S(2)}) collective-permute-start(bf16[128,4096]{1,0:T(8,128)(2,1)} %collective-permute-done.17), channel_id=1, source_target_pairs={{4,12},{12,20},{20,28},{28,24},{24,16},{16,8},{8,0},{0,4},{5,13},{... | collective-permute-start | bytes 3145736 | tf_op jit(solution)/shard_map/ppermute | solution.py:234
  183.9 1.5 copy-start.2
  201.4 5.5 %copy-start.1 = (bf16[512,4096]{1,0:T(8,128)(2,1)S(1)}, bf16[512,4096]{1,0:T(8,128)(2,1)}, u32[]{:S(2)}) copy-start(bf16[512,4096]{1,0:T(8,128)(2,1)} %scan.1) | copy-start | bytes 12582916
  205.1 33.7 %collective-permute-start = (bf16[512,256]{1,0:T(8,128)(2,1)S(1)}, bf16[512,256]{1,0:T(8,128)(2,1)S(1)}, u32[]{:S(2)}, u32[]{:S(2)}) collective-permute-start(bf16[512,256]{1,0:T(8,128)(2,1)S(1)} %fusion.2), channel_id=1, source_target_pairs={{0,3},{1,0},{2,1},{3,2},{4,7},{5,4},{6,5},{7,6},{8,11},{9,8},{10,9... | collective-permute-start | bytes 786440 | tf_op jit(solution)/shard_map/ppermute | solution.py:221
  231.8 20.2 %collective-permute-start.8 = (bf16[512,128]{1,0:T(8,128)(2,1)S(1)}, bf16[512,128]{1,0:T(8,128)(2,1)S(1)}, u32[]{:S(2)}, u32[]{:S(2)}) collective-permute-start(bf16[512,128]{1,0:T(8,128)(2,1)S(1)} %convolution_convert_fusion.10), channel_id=1, source_target_pairs={{0,3},{1,0},{2,1},{3,2},{4,7},{5,4},{6,5},{7,6},{8,11},{9,8},{10,9... | collective-permute-start | bytes 393224 | tf_op jit(solution)/shard_map/ppermute | solution.py:221
  234.6 32.0 %collective-permute-start.16 = (bf16[512,128]{1,0:T(8,128)(2,1)S(1)}, bf16[512,128]{1,0:T(8,128)(2,1)S(1)}, u32[]{:S(2)}, u32[]{:S(2)}) collective-permute-start(bf16[512,128]{1,0:T(8,128)(2,1)S(1)} %convolution_convert_fusion.6), channel_id=1, source_target_pairs={{0,3},{1,0},{2,1},{3,2},{4,7},{5,4},{6,5},{7,6},{8,11},{9,8},{10,9... | collective-permute-start | bytes 393224 | tf_op jit(solution)/shard_map/ppermute | solution.py:221
  238.7 4.4 %collective-permute-start.2 = (bf16[512,128]{1,0:T(8,128)(2,1)S(1)}, bf16[512,128]{1,0:T(8,128)(2,1)S(1)}, u32[]{:S(2)}, u32[]{:S(2)}) collective-permute-start(bf16[512,128]{1,0:T(8,128)(2,1)S(1)} %convolution_convert_fusion.13), channel_id=1, source_target_pairs={{0,3},{1,0},{2,1},{3,2},{4,7},{5,4},{6,5},{7,6},{8,11},{9,8},{10,9... | collective-permute-start | bytes 393224 | tf_op jit(solution)/shard_map/ppermute | solution.py:221
  243.2 4.4 %collective-permute-start.4 = (bf16[512,128]{1,0:T(8,128)(2,1)S(1)}, bf16[512,128]{1,0:T(8,128)(2,1)S(1)}, u32[]{:S(2)}, u32[]{:S(2)}) collective-permute-start(bf16[512,128]{1,0:T(8,128)(2,1)S(1)} %convolution_convert_fusion.12), channel_id=1, source_target_pairs={{0,3},{1,0},{2,1},{3,2},{4,7},{5,4},{6,5},{7,6},{8,11},{9,8},{10,9... | collective-permute-start | bytes 393224 | tf_op jit(solution)/shard_map/ppermute | solution.py:221
  247.6 4.4 %collective-permute-start.6 = (bf16[512,128]{1,0:T(8,128)(2,1)S(1)}, bf16[512,128]{1,0:T(8,128)(2,1)S(1)}, u32[]{:S(2)}, u32[]{:S(2)}) collective-permute-start(bf16[512,128]{1,0:T(8,128)(2,1)S(1)} %convolution_convert_fusion.11), channel_id=1, source_target_pairs={{0,3},{1,0},{2,1},{3,2},{4,7},{5,4},{6,5},{7,6},{8,11},{9,8},{10,9... | collective-permute-start | bytes 393224 | tf_op jit(solution)/shard_map/ppermute | solution.py:221
  252.0 24.9 %collective-permute-start.24 = (bf16[512,128]{1,0:T(8,128)(2,1)S(1)}, bf16[512,128]{1,0:T(8,128)(2,1)S(1)}, u32[]{:S(2)}, u32[]{:S(2)}) collective-permute-start(bf16[512,128]{1,0:T(8,128)(2,1)S(1)} %convolution_convert_fusion.2), channel_id=1, source_target_pairs={{0,3},{1,0},{2,1},{3,2},{4,7},{5,4},{6,5},{7,6},{8,11},{9,8},{10,9... | collective-permute-start | bytes 393224 | tf_op jit(solution)/shard_map/ppermute | solution.py:221
  252.0 5.7 %collective-permute-start.10 = (bf16[512,128]{1,0:T(8,128)(2,1)S(1)}, bf16[512,128]{1,0:T(8,128)(2,1)S(1)}, u32[]{:S(2)}, u32[]{:S(2)}) collective-permute-start(bf16[512,128]{1,0:T(8,128)(2,1)S(1)} %convolution_convert_fusion.9), channel_id=1, source_target_pairs={{0,3},{1,0},{2,1},{3,2},{4,7},{5,4},{6,5},{7,6},{8,11},{9,8},{10,9... | collective-permute-start | bytes 393224 | tf_op jit(solution)/shard_map/ppermute | solution.py:221
  257.8 4.4 %collective-permute-start.12 = (bf16[512,128]{1,0:T(8,128)(2,1)S(1)}, bf16[512,128]{1,0:T(8,128)(2,1)S(1)}, u32[]{:S(2)}, u32[]{:S(2)}) collective-permute-start(bf16[512,128]{1,0:T(8,128)(2,1)S(1)} %convolution_convert_fusion.8), channel_id=1, source_target_pairs={{0,3},{1,0},{2,1},{3,2},{4,7},{5,4},{6,5},{7,6},{8,11},{9,8},{10,9... | collective-permute-start | bytes 393224 | tf_op jit(solution)/shard_map/ppermute | solution.py:221
  262.2 4.4 %collective-permute-start.14 = (bf16[512,128]{1,0:T(8,128)(2,1)S(1)}, bf16[512,128]{1,0:T(8,128)(2,1)S(1)}, u32[]{:S(2)}, u32[]{:S(2)}) collective-permute-start(bf16[512,128]{1,0:T(8,128)(2,1)S(1)} %convolution_convert_fusion.7), channel_id=1, source_target_pairs={{0,3},{1,0},{2,1},{3,2},{4,7},{5,4},{6,5},{7,6},{8,11},{9,8},{10,9... | collective-permute-start | bytes 393224 | tf_op jit(solution)/shard_map/ppermute | solution.py:221
  266.5 10.2 %collective-permute-start.22 = (bf16[512,128]{1,0:T(8,128)(2,1)S(1)}, bf16[512,128]{1,0:T(8,128)(2,1)S(1)}, u32[]{:S(2)}, u32[]{:S(2)}) collective-permute-start(bf16[512,128]{1,0:T(8,128)(2,1)S(1)} %convolution_convert_fusion.3), channel_id=1, source_target_pairs={{0,3},{1,0},{2,1},{3,2},{4,7},{5,4},{6,5},{7,6},{8,11},{9,8},{10,9... | collective-permute-start | bytes 393224 | tf_op jit(solution)/shard_map/ppermute | solution.py:221
  266.6 5.7 %collective-permute-start.18 = (bf16[512,128]{1,0:T(8,128)(2,1)S(1)}, bf16[512,128]{1,0:T(8,128)(2,1)S(1)}, u32[]{:S(2)}, u32[]{:S(2)}) collective-permute-start(bf16[512,128]{1,0:T(8,128)(2,1)S(1)} %convolution_convert_fusion.5), channel_id=1, source_target_pairs={{0,3},{1,0},{2,1},{3,2},{4,7},{5,4},{6,5},{7,6},{8,11},{9,8},{10,9... | collective-permute-start | bytes 393224 | tf_op jit(solution)/shard_map/ppermute | solution.py:221
  272.3 4.4 %collective-permute-start.20 = (bf16[512,128]{1,0:T(8,128)(2,1)S(1)}, bf16[512,128]{1,0:T(8,128)(2,1)S(1)}, u32[]{:S(2)}, u32[]{:S(2)}) collective-permute-start(bf16[512,128]{1,0:T(8,128)(2,1)S(1)} %convolution_convert_fusion.4), channel_id=1, source_target_pairs={{0,3},{1,0},{2,1},{3,2},{4,7},{5,4},{6,5},{7,6},{8,11},{9,8},{10,9... | collective-permute-start | bytes 393224 | tf_op jit(solution)/shard_map/ppermute | solution.py:221
  279.4 4.4 %collective-permute-start.26 = (bf16[512,128]{1,0:T(8,128)(2,1)S(1)}, bf16[512,128]{1,0:T(8,128)(2,1)S(1)}, u32[]{:S(2)}, u32[]{:S(2)}) collective-permute-start(bf16[512,128]{1,0:T(8,128)(2,1)S(1)} %convolution_convert_fusion.1), channel_id=1, source_target_pairs={{0,3},{1,0},{2,1},{3,2},{4,7},{5,4},{6,5},{7,6},{8,11},{9,8},{10,9... | collective-permute-start | bytes 393224 | tf_op jit(solution)/shard_map/ppermute | solution.py:221
  282.0 4.4 %collective-permute-start.28 = (bf16[512,128]{1,0:T(8,128)(2,1)S(1)}, bf16[512,128]{1,0:T(8,128)(2,1)S(1)}, u32[]{:S(2)}, u32[]{:S(2)}) collective-permute-start(bf16[512,128]{1,0:T(8,128)(2,1)S(1)} %convolution_convert_fusion), channel_id=1, source_target_pairs={{0,3},{1,0},{2,1},{3,2},{4,7},{5,4},{6,5},{7,6},{8,11},{9,8},{10,9... | collective-permute-start | bytes 393224 | tf_op jit(solution)/shard_map/ppermute | solution.py:221
  283.9 2.5 copy-start.3

commit v2 on v0

v2 whole, which is shorter than its diff:
```python
import functools

import jax
import jax.numpy as jnp
from jax import lax
from jax.experimental import pallas as pl
from jax.experimental.pallas import tpu as pltpu
from jax.sharding import PartitionSpec as P

CHUNK = 128
GROUP = 4
EXTRA = 16
BF16 = jnp.bfloat16
F32 = jnp.float32
COST = pl.CostEstimate(flops=0, bytes_accessed=0, transcendentals=0)


def near_kernel(
    chunks, maps_ref, readst_ref, cntc_ref, cntr_ref, cum_ref, cumt_ref, tail_ref,
    open_ref, keep_ref, whole_ref, gain_ref, cot_ref, out_ref, state_ref, score_ref,
):
    @pl.when(pl.program_id(0) == 0)
    def _():
        row = lax.broadcasted_iota(jnp.int32, (CHUNK, CHUNK), 0)
        col = lax.broadcasted_iota(jnp.int32, (CHUNK, CHUNK), 1)
        for c in range(chunks):
            at = slice(c * CHUNK, (c + 1) * CHUNK)
            scores = lax.dot_general(
                maps_ref[0, at, :], maps_ref[1, at, :], (((1,), (1,)), ((), ())),
                preferred_element_type=F32,
            )
            linked = (row <= col) & (cntc_ref[at, :] == cntr_ref[:, at])
            score_ref[at, :] = jnp.where(linked, scores, 0.0)

    width = readst_ref.shape[0]
    for j in range(GROUP):
        lane = slice(j * 128, (j + 1) * 128)
        gain = gain_ref[0, j : j + 1, :]
        later = None
        for c in reversed(range(chunks)):
            at = slice(c * CHUNK, (c + 1) * CHUNK)
            cot = cot_ref[at, lane]
            spread = cumt_ref[0, j : j + 1, at] - cum_ref[0, at, j : j + 1]
            weight = (jnp.exp(jnp.minimum(spread, 0.0)) * score_ref[at, :]).astype(BF16)
            if later is None:
                total = jnp.dot(weight, cot, preferred_element_type=F32)
            else:
                reach = (tail_ref[0, at, j : j + 1] * maps_ref[0, at, :].astype(F32)).astype(BF16)
                total = jnp.dot(
                    jnp.concatenate([weight, reach], axis=1),
                    jnp.concatenate([cot, later.astype(BF16)], axis=0),
                    preferred_element_type=F32,
                )
            out_ref[at, lane] = (total + gain * cot.astype(F32)).astype(BF16)
            scaled = (readst_ref[:, at].astype(F32) * open_ref[0, j : j + 1, at]).astype(BF16)
            state = jnp.dot(scaled, cot, preferred_element_type=F32)
            if later is not None:
                state = state + keep_ref[0, c * GROUP + j : c * GROUP + j + 1, :] * later
            later = state
        state_ref[j, :width, :] = later.astype(BF16)
        keep = jnp.broadcast_to(whole_ref[0, j : j + 1, :], (EXTRA, 128))
        high = keep.astype(BF16)
        low = (keep - high.astype(F32)).astype(BF16)
        top = lax.broadcasted_iota(jnp.int32, (EXTRA, 128), 0) < EXTRA // 2
        state_ref[j, width:, :] = jnp.where(top, high.astype(F32), low.astype(F32)).astype(BF16)


def far_kernel(*refs):
    near, writes, reach, later, out_ref = refs[0:2], refs[2:4], refs[4:6], refs[6:8], refs[8]
    tokens = near[0].shape[0]
    for side in range(2):
        for j in range(GROUP):
            lane = slice(j * 128, (j + 1) * 128)
            far = jnp.dot(writes[side][0], later[side][j], preferred_element_type=F32)
            total = near[side][:, lane].astype(F32) + reach[side][0, :, j : j + 1] * far
            out_ref[side * tokens : (side + 1) * tokens, lane] = total.astype(BF16)


def gate(x, *after):
    return lax.optimization_barrier((x,) + after)[0]


def step3(g):
    return (g, 0, 0)


def whole2(g):
    return (0, 0)


def columns2(g):
    return (0, g)


def prep_kernel(
    chunks, heads, ext_ref, maps_ref, cumc_ref, tailc_ref, reachc_ref, cumr_ref, openr_ref,
    keep_ref, whole_ref, cntc_ref, cntr_ref, readst_ref,
):
    rows = ext_ref.shape[0]
    groups = heads // GROUP
    col = lax.broadcasted_iota(jnp.int32, (rows, CHUNK), 1)
    after = jnp.zeros((rows, 1), F32)
    for c in reversed(range(chunks)):
        at = slice(c * CHUNK, (c + 1) * CHUNK)
        cum = ext_ref[:, at]
        shift = 1
        while shift < CHUNK:
            cum = cum + jnp.where(col >= shift, pltpu.roll(cum, shift, axis=1), 0.0)
            shift *= 2
        last = cum[:, CHUNK - 1 :]
        cnt, end = cum[heads : heads + 1], last[heads : heads + 1]
        linked = jnp.where(cnt == end, 1.0, 0.0)
        tail = jnp.exp(jnp.minimum(last - cum, 0.0)) * linked
        later = jnp.where(after[heads : heads + 1] == 0.0, jnp.exp(after), 0.0)
        reach = tail * later
        opened = jnp.exp(cum) * jnp.where(cnt == 0.0, 1.0, 0.0)
        keep = jnp.where(end == 0.0, jnp.exp(last), 0.0)
        after = after + last
        cntr_ref[:, at] = cnt
        columns = cum.T
        cntc_ref[at, :] = columns[:, heads : heads + 1]
        tails, reaches = tail.T, reach.T
        for g in range(groups):
            lane = slice(g * GROUP, (g + 1) * GROUP)
            cumr_ref[g, :, at] = cum[lane]
            openr_ref[g, :, at] = opened[lane]
            keep_ref[g, c * GROUP : (c + 1) * GROUP, :] = jnp.broadcast_to(
                keep[lane], (GROUP, 128)
            )
            cumc_ref[g, at, :] = columns[:, lane]
            tailc_ref[g, at, :] = tails[:, lane]
            reachc_ref[g, at, :] = reaches[:, lane]
    whole = jnp.where(after[heads : heads + 1] == 0.0, jnp.exp(after), 0.0)
    for g in range(groups):
        whole_ref[g] = jnp.broadcast_to(whole[g * GROUP : (g + 1) * GROUP], (GROUP, 128))
    readst_ref[...] = maps_ref[1].astype(F32).T.astype(BF16)


def near_part(cot, maps, ext, gains):
    heads = gains.shape[0]
    tokens, width = maps.shape[1:]
    size = cot.shape[1] // heads
    chunks = tokens // CHUNK
    groups = heads // GROUP

    def like(*shape):
        return jax.ShapeDtypeStruct(shape, F32)

    def wide(x):
        return jnp.broadcast_to(x[..., None], x.shape + (128,))

    cumc, tailc, reachc, cumr, openr, keep, whole, cntc, cntr, reads_t = pl.pallas_call(
        functools.partial(prep_kernel, chunks, heads),
        out_shape=[like(groups, tokens, GROUP)] * 3
        + [like(groups, GROUP, tokens)] * 2
        + [like(groups, chunks * GROUP, 128), like(groups, GROUP, 128), like(tokens, 1)]
        + [like(1, tokens), jax.ShapeDtypeStruct((width, tokens), BF16)],
        cost_estimate=COST,
        name="prep",
    )(ext, maps)
    near, state = pl.pallas_call(
        functools.partial(near_kernel, chunks),
        grid=(groups,),
        in_specs=[
            pl.BlockSpec((2, tokens, width), lambda g: (0, 0, 0)),
            pl.BlockSpec((width, tokens), whole2),
            pl.BlockSpec((tokens, 1), whole2),
            pl.BlockSpec((1, tokens), whole2),
            pl.BlockSpec((1, tokens, GROUP), step3),
            pl.BlockSpec((1, GROUP, tokens), step3),
            pl.BlockSpec((1, tokens, GROUP), step3),
            pl.BlockSpec((1, GROUP, tokens), step3),
            pl.BlockSpec((1, chunks * GROUP, 128), step3),
            pl.BlockSpec((1, GROUP, 128), step3),
            pl.BlockSpec((1, GROUP, 128), step3),
            pl.BlockSpec((tokens, GROUP * size), columns2),
        ],
        out_specs=[
            pl.BlockSpec((tokens, GROUP * size), columns2),
            pl.BlockSpec((GROUP, width + EXTRA, size), step3),
        ],
        out_shape=[
            jax.ShapeDtypeStruct((tokens, heads * size), BF16),
            jax.ShapeDtypeStruct((heads, width + EXTRA, size), BF16),
        ],
        scratch_shapes=[pltpu.VMEM((tokens, CHUNK), F32)],
        cost_estimate=COST,
        name="near",
    )(
        maps, reads_t, cntc, cntr, cumc, cumr, tailc, openr, keep, whole,
        wide(gains.reshape(groups, GROUP)), cot,
    )
    return near, state, reachc


def arrivals(m):
    plan = []
    for q in range(m):
        order = [(0, 0)]
        for k in range(1, m):
            order += [(1, k)] * (q >= k) + [(-1, k)] * (q + k < m)
        plan.append(order)
    return plan


def product_kernel(which, tiles, slab_ref, x_ref, *refs):
    blocks, (own_ref, other_ref, held, sem) = refs[:-4], refs[-4:]
    step = pl.program_id(0)

    @pl.when(step == 0)
    def _():
        for b, block in enumerate(blocks):
            chosen = functools.reduce(
                jnp.logical_or, [slab_ref[0] == q for q, w in enumerate(which) if w == b]
            )

            @pl.when(chosen)
            def _():
                copy = pltpu.make_async_copy(block, held, sem)
                copy.start()
                copy.wait()

    piece = lax.dot_general(
        x_ref[...], held[...], (((1,), (1,)), ((), ())), preferred_element_type=F32
    ).astype(BF16)

    @pl.when(step < tiles)
    def _():
        own_ref[...] = piece

    @pl.when(step >= tiles)
    def _():
        other_ref[...] = piece


def product(x, picked, slab, tokens):
    distinct, which = [], []
    for p in picked:
        at = [i for i, d in enumerate(distinct) if d is p]
        which.append(at[0] if at else len(distinct))
        if not at:
            distinct.append(p)
    rows, depth = picked[0].shape
    tile = 256
    tiles = tokens // tile
    return pl.pallas_call(
        functools.partial(product_kernel, which, tiles),
        grid_spec=pltpu.PrefetchScalarGridSpec(
            num_scalar_prefetch=1,
            grid=(2 * tiles,),
            in_specs=[pl.BlockSpec((tile, depth), lambda i, slab: (i, 0))]
            + [pl.BlockSpec(memory_space=pl.ANY)] * len(distinct),
            out_specs=[
                pl.BlockSpec((tile, rows), lambda i, slab: (jnp.minimum(i, tiles - 1), 0)),
                pl.BlockSpec((tile, rows), lambda i, slab: (jnp.maximum(i - tiles, 0), 0)),
            ],
            scratch_shapes=[pltpu.VMEM((rows, depth), BF16), pltpu.SemaphoreType.DMA],
        ),
        out_shape=[jax.ShapeDtypeStruct((tokens, rows), BF16)] * 2,
        cost_estimate=COST,
        name="product",
    )(slab.reshape(1), x, *distinct)


def parts_of(packed, width):
    state = packed[:, :width, :].astype(F32)
    high = packed[:, width : width + 1, :].astype(F32)
    low = packed[:, width + EXTRA // 2 : width + EXTRA // 2 + 1, :].astype(F32)
    return state, high + low


def body(n, pipes, cotangent, input_map, output_map, log_decay, flight_starts, skip_gain, in_weight):
    cot = cotangent[0]
    gains = skip_gain[0]
    heads = gains.shape[0]
    tokens, width = input_map.shape[1:]
    maps = jnp.concatenate([input_map, output_map], axis=0)
    starts = jnp.broadcast_to(flight_starts.astype(F32), (8, tokens))
    ext = jnp.concatenate([log_decay[0].T, starts], axis=0)
    size = cot.shape[1] // heads
    groups = heads // GROUP
    m = n // 2
    mine = lax.axis_index("seq")
    slab, side = mine // 2, mine % 2
    first = side == 0

    pair = [(s, s ^ 1) for s in range(n)]

    def swap(x):
        return lax.ppermute(x, "seq", pair)

    ext_b, maps_b = swap(ext), swap(maps)
    cot_b = swap(cot)

    weight = in_weight[0]
    blocks = {(0, 0): weight}
    for k in range(1, m):
        blocks[1, k] = lax.ppermute(
            blocks.get((1, k - 1), weight), "seq",
            [(s, s + 2) for s in range(2 * (k - 1), n - 2)],
        )
        blocks[-1, k] = lax.ppermute(
            blocks.get((-1, k - 1), weight), "seq",
            [(s, s - 2) for s in range(2, n - 2 * (k - 1))],
        )

    near_a, state_a, reach_a = near_part(gate(cot, ext_b, maps_b), maps, ext, gains)
    half = heads // 2
    got = swap(lax.dynamic_slice_in_dim(state_a, (1 - side) * half, half, 0))
    kept = lax.dynamic_slice_in_dim(state_a, side * half, half, 0)
    state_0, keep_0 = parts_of(jnp.where(first, kept, got), width)
    state_1, keep_1 = parts_of(jnp.where(first, got, kept), width)
    slab_state, slab_keep = state_0 + keep_0 * state_1, keep_0 * keep_1
    later = jnp.zeros((half, width, size), BF16)
    for at in reversed(range(1, m)):
        leaving = (slab_state + slab_keep * later.astype(F32)).astype(BF16)
        if at == m - 1:
            leaving = gate(leaving, blocks[1, 1], blocks[-1, 1])
        later = later + lax.ppermute(
            leaving, "seq", [(2 * at + y, 2 * at - 2 + y) for y in range(2)]
        )
    other = swap(later)
    last = jnp.where(first, jnp.stack([later, other]), jnp.stack([other, later]))
    last = last.reshape(heads, width, size)

    near_b, state_b, reach_b = near_part(cot_b, maps_b, ext_b, gains)
    state_1, keep_1 = parts_of(jnp.where(first, state_b, state_a), width)
    early = (state_1 + keep_1 * last.astype(F32)).astype(BF16)
    later_a = jnp.where(first, early, last)
    later_b = jnp.where(first, last, early)

    block2 = pl.BlockSpec((tokens, GROUP * size), columns2)
    scan_grad = pl.pallas_call(
        far_kernel,
        grid=(groups,),
        in_specs=[block2] * 2
        + [pl.BlockSpec((1, tokens, width), lambda g: (0, 0, 0))] * 2
        + [pl.BlockSpec((1, tokens, GROUP), step3)] * 2
        + [pl.BlockSpec((GROUP, width, size), step3)] * 2,
        out_specs=pl.BlockSpec((2 * tokens, GROUP * size), columns2),
        out_shape=jax.ShapeDtypeStruct((2 * tokens, heads * size), BF16),
        cost_estimate=COST,
        name="far",
    )(near_a, near_b, maps, maps_b, reach_a, reach_b, later_a, later_b)

    rows = weight.shape[0]
    result = jnp.zeros((tokens, n * rows), BF16)
    plan = arrivals(m)
    for slot in range(m):
        picks = [plan[q][slot] for q in range(m)]
        got = product(scan_grad, [blocks[p] for p in picks], slab, tokens)
        source = jnp.array([q - way * k for q, (way, k) in enumerate(picks)], jnp.int32)[slab]
        for flip in range(2):
            route = [
                (s * pipes + p, (s ^ flip) * pipes + (p - 1) % pipes)
                for s in range(n) for p in range(pipes)
            ]
            piece = lax.ppermute(got[flip], ("seq", "pipe"), route)
            column = (2 * source + (side ^ flip)) * rows
            result = lax.dynamic_update_slice(result, piece, (0, column))
    return result[None]


def solution(mesh):
    n, pipes = mesh.shape["seq"], mesh.shape["pipe"]
    placed = (
        P("pipe", "seq", None),
        P("pipe", "seq", None),
        P("pipe", "seq", None),
        P("pipe", "seq", None),
        P("pipe", "seq"),
        P("pipe", None),
        P("pipe", "seq", None),
    )
    return jax.shard_map(
        functools.partial(body, n, pipes),
        mesh=mesh,
        in_specs=placed,
        out_specs=P("pipe", "seq", None),
        check_vma=False,
    )
```

time: 438 us -> 247 us (0.56)
  waiting for transfers between devices: 283 us -> 98.8 us
  Pallas kernels: 0 us -> 90.9 us
  local copies, waits for them, and re-layouts: 48.9 us -> 7.67 us
  matrix products: 41 us -> 0 us
  starting transfers between devices: 1.17 us -> 35.3 us
  other arithmetic: 29 us -> 8.77 us
  blocking collectives: 16.3 us -> 0 us
  between operations: 14.3 us -> 2.29 us
    all_gather x2 -> x0, waiting for transfers between devices: 258 us -> none  [the longest x1 152 us: body(): lax.all_gather(in_weight[0], 'seq', axis=0, tiled=True)]
    pallas_call x0 -> x9, Pallas kernels: none -> 90.9 us  [the longest x4 32.7 us: product(): pl.pallas_call(functools.partial(product_kernel, which, tiles), grid_spec...]
    ppermute x1 -> x22, waiting for transfers between devices: 24.8 us -> 98.8 us  [the longest x3 52.5 us: body(): lax.ppermute(leaving, 'seq', [(2 * at + y, 2 * at - 2 + y) for y in range...]
    dot_general x8 -> x0, matrix products: 41 us -> none  [the longest x1 13.7 us: body(): lax.dot_general(scan_grad, lax.all_gather(in_weight[0], 'seq', axis=0, ti...]
    ppermute x1 -> x22, starting transfers between devices: 1.12 us -> 35.3 us  [the longest x3 11 us: body(): lax.ppermute(blocks.get((-1, k - 1), weight), 'seq', [(s, s - 2) for s in...]
    unnamed x1 -> x0, blocking collectives: 16.3 us -> none
    dynamic_update_slice x4 -> x8, local copies, waits for them, and re-layouts: 14.7 us -> 0.89 us  [body(): result = lax.dynamic_update_slice(result, piece, (0, column))]
    select_n x12 -> x4, other arithmetic: 18.4 us -> 4.84 us  [the longest x1 2.12 us: body(): later_b = jnp.where(first, last, early)]
  transfers between devices with their start and end apart: 3 -> 22, of which waited for: 3 -> 8; matrix products, arithmetic and copies ran while one was open for 18% -> 6% of each run, Pallas kernels for 0% -> 37%
where the time goes in v2:
time: 247 us; the launch traced here: 244 us
  waiting for transfers between devices  98.8 us (40%)
  Pallas kernels  90.9 us (37%)
  starting transfers between devices  35.3 us (14%)
  other arithmetic  8.77 us (4%)
  local copies, waits for them, and re-layouts  7.67 us (3%)
    ppermute x3, waiting for transfers between devices, body(): lax.ppermute(leaving, 'seq', [(2 * at + y, 2 * at - 2 + y) for y in range...  52.5 us
    pallas_call x4, Pallas kernels, product(): pl.pallas_call(functools.partial(product_kernel, which, tiles), grid_spec...  32.7 us
    ppermute x5, waiting for transfers between devices, swap(): return lax.ppermute(x, 'seq', pair)  31.6 us
    pallas_call x2, Pallas kernels, near_part(): pl.pallas_call(functools.partial(near_kernel, chunks), grid=(groups,), in...  30.7 us
    ppermute x8, waiting for transfers between devices, body(): piece = lax.ppermute(got[flip], ('seq', 'pipe'), route)  14.6 us
    pallas_call x2, Pallas kernels, near_part(): pl.pallas_call(functools.partial(prep_kernel, chunks, heads), out_shape=[...  14.6 us
    pallas_call x1, Pallas kernels, body(): pl.pallas_call(far_kernel, grid=(groups,), in_specs=[block2] * 2 + [pl.Bl...  12.9 us
    ppermute x3, starting transfers between devices, body(): lax.ppermute(blocks.get((-1, k - 1), weight), 'seq', [(s, s - 2) for s in...  11 us
  transfers between devices with their start and end apart: 22, of which 8 were waited for; matrix products, arithmetic and copies ran while one was open for 6% of the time, Pallas kernels for 37%

profile of v2, /device:TPU:9, one launch (start us, length us, event | category | flops | bytes accessed | tf_op | source)
XLA Modules:
  0.0 243.7 jit_solution(1832687190030962078)
XLA Ops:
  0.0 1.9 collective-permute-start.5
  1.9 3.4 %collective-permute-start.4 = (bf16[256,4096]{1,0:T(8,128)(2,1)}, bf16[256,4096]{1,0:T(8,128)(2,1)}, u32[]{:S(2)}, u32[]{:S(2)}) collective-permute-start(bf16[256,4096]{1,0:T(8,128)(2,1)} %bitcast.38), channel_id=1, source_target_pairs={{0,8},{4,12},{8,16},{12,20},{16,24},{20,28},{1,9},{5,13},{9,17},{1... | collective-permute-start | bytes 6291464 | tf_op jit(solution)/shard_map/ppermute | solution.py:298
  5.3 0.9 constant_dynamic-update-slice_fusion.1
  6.2 0.9 constant_dynamic-update-slice_fusion.maps_ref.refs_2_
  7.1 1.3 collective-permute-start.1
  8.5 0.7 convert_element_type.53
  9.1 0.8 pad_maximum_fusion.ext_ref
  10.6 7.3 %prep.2 = (f32[8,512,4]{2,1,0:T(8,128)}, f32[8,512,4]{2,1,0:T(8,128)}, f32[8,512,4]{2,1,0:T(8,128)}, f32[8,4,512]{2,1,0:T(4,128)}, f32[8,4,512]{2,1,0:T(4,128)},...) custom-call(f32[40,512]{1,0:T(8,128)} %copy-done.5, ...), custom_call_target="tpu_custom_call" | custom-call | tf_op jit(solution)/shard_map/prep/pallas_call | solution.py:152
  18.4 1.3 reduce.3
  19.9 0.7 broadcast_in_dim.44.gain_ref
  20.6 15.3 %near.2 = (bf16[512,4096]{1,0:T(8,128)(2,1)}, bf16[32,144,128]{2,1,0:T(8,128)(2,1)}) custom-call(bf16[2,512,128]{2,1,0:T(8,128)(2,1)} %copy-done.2, bf16[128,512]{1,0:T(8,128)(2,1)} %get-tuple-element.39.readst_ref, f32[512,1]{1,0:T(8,128)} %get-tuple-element.40.cntc_ref, f32[1,512]{1,0:T(1,128)} %get-tuple-element.41.cntr_ref, ...), custom_call_target="tpu_custom_call" | custom-call | tf_op jit(solution)/shard_map/near/pallas_call | solution.py:161
  35.9 1.1 constant_dynamic-slice_fusion
  37.0 0.9 collective-permute-start.3
  37.9 0.6 collective-permute-start.2
  38.5 11.9 %collective-permute-done.3 = bf16[16,144,128]{2,1,0:T(8,128)(2,1)S(1)} collective-permute-done((bf16[16,144,128]{2,1,0:T(8,128)(2,1)S(1)}, bf16[16,144,128]{2,1,0:T(8,128)(2,1)S(1)}, u32[]{:S(2)}, u32[]{:S(2)}) %collective-permute-start.3) | collective-permute-done | bytes 589856 | tf_op jit(solution)/shard_map/ppermute | solution.py:290
  50.5 1.1 broadcast_select_fusion.2
  51.9 0.7 collective-permute-start.6
  52.6 3.3 %collective-permute-start.14 = (bf16[256,4096]{1,0:T(8,128)(2,1)S(1)}, bf16[256,4096]{1,0:T(8,128)(2,1)}, u32[]{:S(2)}, u32[]{:S(2)}) collective-permute-start(bf16[256,4096]{1,0:T(8,128)(2,1)S(1)} %collective-permute-done.5.refs_0_.refs_1_), channel_id=1, source_target_pairs={{8,0},{12,4},{16,8},{20,12},{9,1},{13,5},{17,9},{21,13},{10,2},{14... | collective-permute-start | bytes 6291464 | tf_op jit(solution)/shard_map/ppermute | solution.py:302
  56.0 4.7 %collective-permute-start.15 = (bf16[256,4096]{1,0:T(8,128)(2,1)}, bf16[256,4096]{1,0:T(8,128)(2,1)}, u32[]{:S(2)}, u32[]{:S(2)}) collective-permute-start(bf16[256,4096]{1,0:T(8,128)(2,1)} %collective-permute-done.4.refs_1_), channel_id=1, source_target_pairs={{8,16},{12,20},{16,24},{20,28},{9,17},{13,21},{17,25},{21,29},{10,... | collective-permute-start | bytes 6291464 | tf_op jit(solution)/shard_map/ppermute | solution.py:298
  60.9 1.3 collective-permute-start.7
  62.2 46.4 %collective-permute-done.7 = bf16[16,128,128]{2,1,0:T(8,128)(2,1)S(1)} collective-permute-done((bf16[16,128,128]{2,1,0:T(8,128)(2,1)S(1)}, bf16[16,128,128]{2,1,0:T(8,128)(2,1)S(1)}, u32[]{:S(2)}, u32[]{:S(2)}) %collective-permute-start.7) | collective-permute-done | bytes 524320 | tf_op jit(solution)/shard_map/ppermute | solution.py:319
  109.0 1.3 collective-permute-start.8
  110.4 6.1 %collective-permute-done.8 = bf16[16,128,128]{2,1,0:T(8,128)(2,1)S(1)} collective-permute-done((bf16[16,128,128]{2,1,0:T(8,128)(2,1)S(1)}, bf16[16,128,128]{2,1,0:T(8,128)(2,1)S(1)}, u32[]{:S(2)}, u32[]{:S(2)}) %collective-permute-start.8) | collective-permute-done | bytes 524320 | tf_op jit(solution)/shard_map/ppermute | solution.py:319
  116.7 7.3 %prep.3 = (f32[8,512,4]{2,1,0:T(8,128)}, f32[8,512,4]{2,1,0:T(8,128)}, f32[8,512,4]{2,1,0:T(8,128)}, f32[8,4,512]{2,1,0:T(4,128)}, f32[8,4,512]{2,1,0:T(4,128)},...) custom-call(f32[40,512]{1,0:T(8,128)} %copy-done.6, ...), custom_call_target="tpu_custom_call" | custom-call | tf_op jit(solution)/shard_map/prep/pallas_call | solution.py:152
  124.0 5.8 %collective-permute-start.18 = (bf16[256,4096]{1,0:T(8,128)(2,1)}, bf16[256,4096]{1,0:T(8,128)(2,1)}, u32[]{:S(2)}, u32[]{:S(2)}) collective-permute-start(bf16[256,4096]{1,0:T(8,128)(2,1)} %collective-permute-done.14.refs_0_.refs_1_), channel_id=1, source_target_pairs={{8,0},{12,4},{9,1},{13,5},{10,2},{14,6},{11,3},{15,7}} | collective-permute-start | bytes 6291464 | tf_op jit(solution)/shard_map/ppermute | solution.py:302
  129.8 2.0 collective-permute-start.19
  131.8 19.7 %collective-permute-done.9 = bf16[16,128,128]{2,1,0:T(8,128)(2,1)S(1)} collective-permute-done((bf16[16,128,128]{2,1,0:T(8,128)(2,1)S(1)}, bf16[16,128,128]{2,1,0:T(8,128)(2,1)S(1)}, u32[]{:S(2)}, u32[]{:S(2)}) %collective-permute-start.9) | collective-permute-done | bytes 524320 | tf_op jit(solution)/shard_map/ppermute | solution.py:290
  151.7 15.4 %near.3 = (bf16[512,4096]{1,0:T(8,128)(2,1)}, bf16[32,144,128]{2,1,0:T(8,128)(2,1)}) custom-call(bf16[2,512,128]{2,1,0:T(8,128)(2,1)} %copy-done.3, bf16[128,512]{1,0:T(8,128)(2,1)} %get-tuple-element.50.readst_ref, f32[512,1]{1,0:T(8,128)} %get-tuple-element.51.cntc_ref, f32[1,512]{1,0:T(1,128)} %get-tuple-element.52.cntr_ref, ...), custom_call_target="tpu_custom_call" | custom-call | tf_op jit(solution)/shard_map/near/pallas_call | solution.py:161
  167.1 1.4 broadcast_select_fusion
  168.6 2.1 fusion
  170.7 12.9 %far.1.x_ref = bf16[1024,4096]{1,0:T(8,128)(2,1)} custom-call(bf16[512,4096]{1,0:T(8,128)(2,1)} %get-tuple-element.49.refs_0_, bf16[512,4096]{1,0:T(8,128)(2,1)} %get-tuple-element.59.refs_1_, bf16[2,512,128]{2,1,0:T(8,128)(2,1)} %copy-done.2, bf16[2,512,128]{2,1,0:T(8,128)(2,1)} %copy-done.3, f32[8,512,4]{2,1,0:T(8,128)} %get-tuple-element.60.refs_4_, ...), custom_call_target="tpu_custom_call" | custom-call | tf_op jit(solution)/shard_map/far/pallas_call | solution.py:333
  183.6 8.1 %product.4 = (bf16[512,256]{1,0:T(8,128)(2,1)}, bf16[512,256]{1,0:T(8,128)(2,1)}) custom-call(s32[1]{0:T(128)} %bitcast.slab_ref, bf16[1024,4096]{1,0:T(8,128)(2,1)} %far.1.x_ref, bf16[256,4096]{1,0:T(8,128)(2,1)} %bitcast.39), custom_call_target="tpu_custom_call" | custom-call | tf_op jit(solution)/shard_map/product/pallas_call | solution.py:246
  191.8 2.5 %collective-permute-start.10 = (bf16[512,256]{1,0:T(8,128)(2,1)}, bf16[512,256]{1,0:T(8,128)(2,1)S(1)}, u32[]{:S(2)}, u32[]{:S(2)}) collective-permute-start(bf16[512,256]{1,0:T(8,128)(2,1)} %get-tuple-element.65), channel_id=1, source_target_pairs={{0,3},{1,0},{2,1},{3,2},{4,7},{5,4},{6,5},{7,6},{8,11},{9,8},{10,9... | collective-permute-start | bytes 786440 | tf_op jit(solution)/shard_map/ppermute | solution.py:358
  194.3 0.6 dynamic_slice.21
  195.4 0.6 dynamic_slice.22
  196.6 0.6 dynamic_slice.23
  197.9 8.2 %product.6 = (bf16[512,256]{1,0:T(8,128)(2,1)}, bf16[512,256]{1,0:T(8,128)(2,1)}) custom-call(s32[1]{0:T(128)} %bitcast.slab_ref, bf16[1024,4096]{1,0:T(8,128)(2,1)} %far.1.x_ref, bf16[256,4096]{1,0:T(8,128)(2,1)} %collective-permute-done.14.refs_0_.refs_1_, bf16[256,4096]{1,0:T(8,128)(2,1)} %copy-done, bf16[256,4096]{1,0:T(8,128)(2,1)} %collective-permute-done.15.refs_2_), custom_call_target="tpu_custom_call" | custom-call | tf_op jit(solution)/shard_map/product/pallas_call | solution.py:246
  206.1 1.0 collective-permute-start.16
  207.0 8.2 %product.5 = (bf16[512,256]{1,0:T(8,128)(2,1)}, bf16[512,256]{1,0:T(8,128)(2,1)}) custom-call(s32[1]{0:T(128)} %bitcast.slab_ref, bf16[1024,4096]{1,0:T(8,128)(2,1)} %far.1.x_ref, bf16[256,4096]{1,0:T(8,128)(2,1)} %copy-done, bf16[256,4096]{1,0:T(8,128)(2,1)} %collective-permute-done.4.refs_1_), custom_call_target="tpu_custom_call" | custom-call | tf_op jit(solution)/shard_map/product/pallas_call | solution.py:246
  215.2 0.8 collective-permute-start.12
  216.3 2.0 collective-permute-start.13
  218.3 3.2 %collective-permute-done.12 = bf16[512,256]{1,0:T(8,128)(2,1)S(1)} collective-permute-done((bf16[512,256]{1,0:T(8,128)(2,1)}, bf16[512,256]{1,0:T(8,128)(2,1)S(1)}, u32[]{:S(2)}, u32[]{:S(2)}) %collective-permute-start.12) | collective-permute-done | bytes 262176 | tf_op jit(solution)/shard_map/ppermute | solution.py:358
  221.9 3.9 %collective-permute-done.13 = bf16[512,256]{1,0:T(8,128)(2,1)S(1)} collective-permute-done((bf16[512,256]{1,0:T(8,128)(2,1)S(1)}, bf16[512,256]{1,0:T(8,128)(2,1)S(1)}, u32[]{:S(2)}, u32[]{:S(2)}) %collective-permute-start.13) | collective-permute-done | bytes 262176 | tf_op jit(solution)/shard_map/ppermute | solution.py:358
  225.8 8.2 %product.7 = (bf16[512,256]{1,0:T(8,128)(2,1)}, bf16[512,256]{1,0:T(8,128)(2,1)}) custom-call(s32[1]{0:T(128)} %bitcast.slab_ref, bf16[1024,4096]{1,0:T(8,128)(2,1)} %far.1.x_ref, bf16[256,4096]{1,0:T(8,128)(2,1)} %collective-permute-done.18.refs_0_, bf16[256,4096]{1,0:T(8,128)(2,1)} %collective-permute-done.14.refs_0_.refs_1_, ...), custom_call_target="tpu_custom_call" | custom-call | tf_op jit(solution)/shard_map/product/pallas_call | solution.py:246
  234.1 1.2 collective-permute-start.21
  235.3 5.0 %collective-permute-done.20 = bf16[512,256]{1,0:T(8,128)(2,1)S(1)} collective-permute-done((bf16[512,256]{1,0:T(8,128)(2,1)}, bf16[512,256]{1,0:T(8,128)(2,1)S(1)}, u32[]{:S(2)}, u32[]{:S(2)}) %collective-permute-start.20) | collective-permute-done | bytes 262176 | tf_op jit(solution)/shard_map/ppermute | solution.py:358
  240.4 2.5 %collective-permute-done.21 = bf16[512,256]{1,0:T(8,128)(2,1)S(1)} collective-permute-done((bf16[512,256]{1,0:T(8,128)(2,1)}, bf16[512,256]{1,0:T(8,128)(2,1)S(1)}, u32[]{:S(2)}, u32[]{:S(2)}) %collective-permute-start.21) | collective-permute-done | bytes 262176 | tf_op jit(solution)/shard_map/ppermute | solution.py:358
  242.9 0.7 bitcast_dynamic-update-slice_fusion
  (62 shorter events, 3.5 us)
Async XLA Ops:
  0.0 51.9 %collective-permute-start.5 = (bf16[256,4096]{1,0:T(8,128)(2,1)}, bf16[256,4096]{1,0:T(8,128)(2,1)S(1)}, u32[]{:S(2)}, u32[]{:S(2)}) collective-permute-start(bf16[256,4096]{1,0:T(8,128)(2,1)} %bitcast.37), channel_id=1, source_target_pairs={{8,0},{12,4},{16,8},{20,12},{24,16},{28,20},{9,1},{13,5},{17,9},{2... | collective-permute-start | bytes 6291464 | tf_op jit(solution)/shard_map/ppermute | solution.py:302
  1.9 50.0 %collective-permute-start.4 = (bf16[256,4096]{1,0:T(8,128)(2,1)}, bf16[256,4096]{1,0:T(8,128)(2,1)}, u32[]{:S(2)}, u32[]{:S(2)}) collective-permute-start(bf16[256,4096]{1,0:T(8,128)(2,1)} %bitcast.38), channel_id=1, source_target_pairs={{0,8},{4,12},{8,16},{12,20},{16,24},{20,28},{1,9},{5,13},{9,17},{1... | collective-permute-start | bytes 6291464 | tf_op jit(solution)/shard_map/ppermute | solution.py:298
  7.1 3.1 %copy-start.2 = (bf16[2,512,128]{2,1,0:T(8,128)(2,1)}, bf16[2,512,128]{2,1,0:T(8,128)(2,1)S(1)}, u32[]{:S(2)}) copy-start(bf16[2,512,128]{2,1,0:T(8,128)(2,1)S(1)} %constant_dynamic-update-slice_fusion.maps_ref.refs_2_) | copy-start | bytes 786436
  7.1 12.7 %collective-permute-start.1 = (bf16[2,512,128]{2,1,0:T(8,128)(2,1)S(1)}, bf16[2,512,128]{2,1,0:T(8,128)(2,1)S(1)}, u32[]{:S(2)}, u32[]{:S(2)}) collective-permute-start(bf16[2,512,128]{2,1,0:T(8,128)(2,1)S(1)} %constant_dynamic-update-slice_fusion.maps_ref.refs_2_), channel_id=1, source_target_pairs={{0,4},{4,0},{8,12},{12,8},{16,20},{20,16},{24,28},{28,24},{1,5},{5... | collective-permute-start | bytes 786440 | tf_op jit(solution)/shard_map/ppermute | solution.py:290
  10.0 0.6 copy-start.5
  10.0 9.8 %collective-permute-start = (f32[40,512]{1,0:T(8,128)S(1)}, f32[40,512]{1,0:T(8,128)S(1)}, u32[]{:S(2)}, u32[]{:S(2)}) collective-permute-start(f32[40,512]{1,0:T(8,128)S(1)} %pad_maximum_fusion.ext_ref), channel_id=1, source_target_pairs={{0,4},{4,0},{8,12},{12,8},{16,20},{20,16},{24,28},{28,24},{1,5},{5... | collective-permute-start | bytes 245768 | tf_op jit(solution)/shard_map/ppermute | solution.py:290
  19.8 16.1 %copy-start.6 = (f32[40,512]{1,0:T(8,128)}, f32[40,512]{1,0:T(8,128)S(1)}, u32[]{:S(2)}) copy-start(f32[40,512]{1,0:T(8,128)S(1)} %collective-permute-done.ext_ref) | copy-start | bytes 245764
  19.8 16.0 %copy-start.3 = (bf16[2,512,128]{2,1,0:T(8,128)(2,1)}, bf16[2,512,128]{2,1,0:T(8,128)(2,1)S(1)}, u32[]{:S(2)}) copy-start(bf16[2,512,128]{2,1,0:T(8,128)(2,1)S(1)} %collective-permute-done.1.maps_ref.refs_3_) | copy-start | bytes 786436
  37.0 13.5 %collective-permute-start.3 = (bf16[16,144,128]{2,1,0:T(8,128)(2,1)S(1)}, bf16[16,144,128]{2,1,0:T(8,128)(2,1)S(1)}, u32[]{:S(2)}, u32[]{:S(2)}) collective-permute-start(bf16[16,144,128]{2,1,0:T(8,128)(2,1)S(1)} %constant_dynamic-slice_fusion), channel_id=1, source_target_pairs={{0,4},{4,0},{8,12},{12,8},{16,20},{20,16},{24,28},{28,24},{1,5},{5... | collective-permute-start | bytes 1769480 | tf_op jit(solution)/shard_map/ppermute | solution.py:290
  37.9 113.8 %collective-permute-start.2 = (bf16[512,4096]{1,0:T(8,128)(2,1)}, bf16[512,4096]{1,0:T(8,128)(2,1)}, u32[]{:S(2)}, u32[]{:S(2)}) collective-permute-start(bf16[512,4096]{1,0:T(8,128)(2,1)} %bitcast.35), channel_id=1, source_target_pairs={{0,4},{4,0},{8,12},{12,8},{16,20},{20,16},{24,28},{28,24},{1,5},{5... | collective-permute-start | bytes 12582920 | tf_op jit(solution)/shard_map/ppermute | solution.py:290
  51.9 57.1 %copy-start = (bf16[256,4096]{1,0:T(8,128)(2,1)}, bf16[256,4096]{1,0:T(8,128)(2,1)S(1)}, u32[]{:S(2)}) copy-start(bf16[256,4096]{1,0:T(8,128)(2,1)S(1)} %collective-permute-done.5.refs_0_.refs_1_) | copy-start | bytes 6291460
  51.9 8.7 %collective-permute-start.6 = (bf16[16,128,128]{2,1,0:T(8,128)(2,1)S(1)}, bf16[16,128,128]{2,1,0:T(8,128)(2,1)S(1)}, u32[]{:S(2)}, u32[]{:S(2)}) collective-permute-start(bf16[16,128,128]{2,1,0:T(8,128)(2,1)S(1)} %add_convert_fusion.3), channel_id=1, source_target_pairs={{24,16},{28,20},{25,17},{29,21},{26,18},{30,22},{27,19},{31,23}} | collective-permute-start | bytes 1572872 | tf_op jit(solution)/shard_map/ppermute | solution.py:319
  52.6 71.4 %collective-permute-start.14 = (bf16[256,4096]{1,0:T(8,128)(2,1)S(1)}, bf16[256,4096]{1,0:T(8,128)(2,1)}, u32[]{:S(2)}, u32[]{:S(2)}) collective-permute-start(bf16[256,4096]{1,0:T(8,128)(2,1)S(1)} %collective-permute-done.5.refs_0_.refs_1_), channel_id=1, source_target_pairs={{8,0},{12,4},{16,8},{20,12},{9,1},{13,5},{17,9},{21,13},{10,2},{14... | collective-permute-start | bytes 6291464 | tf_op jit(solution)/shard_map/ppermute | solution.py:302
  56.0 73.8 %collective-permute-start.15 = (bf16[256,4096]{1,0:T(8,128)(2,1)}, bf16[256,4096]{1,0:T(8,128)(2,1)}, u32[]{:S(2)}, u32[]{:S(2)}) collective-permute-start(bf16[256,4096]{1,0:T(8,128)(2,1)} %collective-permute-done.4.refs_1_), channel_id=1, source_target_pairs={{8,16},{12,20},{16,24},{20,28},{9,17},{13,21},{17,25},{21,29},{10,... | collective-permute-start | bytes 6291464 | tf_op jit(solution)/shard_map/ppermute | solution.py:298
  60.9 47.7 %collective-permute-start.7 = (bf16[16,128,128]{2,1,0:T(8,128)(2,1)S(1)}, bf16[16,128,128]{2,1,0:T(8,128)(2,1)S(1)}, u32[]{:S(2)}, u32[]{:S(2)}) collective-permute-start(bf16[16,128,128]{2,1,0:T(8,128)(2,1)S(1)} %add_convert_fusion.2), channel_id=1, source_target_pairs={{16,8},{20,12},{17,9},{21,13},{18,10},{22,14},{19,11},{23,15}} | collective-permute-start | bytes 1572872 | tf_op jit(solution)/shard_map/ppermute | solution.py:319
  109.0 7.4 %collective-permute-start.8 = (bf16[16,128,128]{2,1,0:T(8,128)(2,1)S(1)}, bf16[16,128,128]{2,1,0:T(8,128)(2,1)S(1)}, u32[]{:S(2)}, u32[]{:S(2)}) collective-permute-start(bf16[16,128,128]{2,1,0:T(8,128)(2,1)S(1)} %get-tuple-element.73), channel_id=1, source_target_pairs={{8,0},{12,4},{9,1},{13,5},{10,2},{14,6},{11,3},{15,7}} | collective-permute-start | bytes 1572872 | tf_op jit(solution)/shard_map/ppermute | solution.py:319
  116.6 34.9 %collective-permute-start.9 = (bf16[16,128,128]{2,1,0:T(8,128)(2,1)S(1)}, bf16[16,128,128]{2,1,0:T(8,128)(2,1)S(1)}, u32[]{:S(2)}, u32[]{:S(2)}) collective-permute-start(bf16[16,128,128]{2,1,0:T(8,128)(2,1)S(1)} %add.106), channel_id=1, source_target_pairs={{0,4},{4,0},{8,12},{12,8},{16,20},{20,16},{24,28},{28,24},{1,5},{5... | collective-permute-start | bytes 1572872 | tf_op jit(solution)/shard_map/ppermute | solution.py:290
  124.0 101.8 %collective-permute-start.18 = (bf16[256,4096]{1,0:T(8,128)(2,1)}, bf16[256,4096]{1,0:T(8,128)(2,1)}, u32[]{:S(2)}, u32[]{:S(2)}) collective-permute-start(bf16[256,4096]{1,0:T(8,128)(2,1)} %collective-permute-done.14.refs_0_.refs_1_), channel_id=1, source_target_pairs={{8,0},{12,4},{9,1},{13,5},{10,2},{14,6},{11,3},{15,7}} | collective-permute-start | bytes 6291464 | tf_op jit(solution)/shard_map/ppermute | solution.py:302
  129.8 96.1 %collective-permute-start.19 = (bf16[256,4096]{1,0:T(8,128)(2,1)}, bf16[256,4096]{1,0:T(8,128)(2,1)}, u32[]{:S(2)}, u32[]{:S(2)}) collective-permute-start(bf16[256,4096]{1,0:T(8,128)(2,1)} %collective-permute-done.15.refs_2_), channel_id=1, source_target_pairs={{16,24},{20,28},{17,25},{21,29},{18,26},{22,30},{19,27},{23,31}} | collective-permute-start | bytes 6291464 | tf_op jit(solution)/shard_map/ppermute | solution.py:298
  151.7 15.4 %copy-start.1 = (bf16[32,144,128]{2,1,0:T(8,128)(2,1)S(1)}, bf16[32,144,128]{2,1,0:T(8,128)(2,1)}, u32[]{:S(2)}) copy-start(bf16[32,144,128]{2,1,0:T(8,128)(2,1)} %get-tuple-element.63) | copy-start | bytes 3538948
  183.6 10.7 %copy-start.11 = (s32[4]{0:T(128)S(1)}, s32[4]{0:T(128)}, u32[]{:S(2)}) copy-start(s32[4]{0:T(128)} %constant.68.clone) | copy-start | bytes 52
  183.6 11.9 %copy-start.10 = (s32[4]{0:T(128)S(1)}, s32[4]{0:T(128)}, u32[]{:S(2)}) copy-start(s32[4]{0:T(128)} %constant.69.clone) | copy-start | bytes 52
  183.6 13.0 %copy-start.9 = (s32[4]{0:T(128)S(1)}, s32[4]{0:T(128)}, u32[]{:S(2)}) copy-start(s32[4]{0:T(128)} %constant.70.clone) | copy-start | bytes 52
  191.8 23.4 %collective-permute-start.10 = (bf16[512,256]{1,0:T(8,128)(2,1)}, bf16[512,256]{1,0:T(8,128)(2,1)S(1)}, u32[]{:S(2)}, u32[]{:S(2)}) collective-permute-start(bf16[512,256]{1,0:T(8,128)(2,1)} %get-tuple-element.65), channel_id=1, source_target_pairs={{0,3},{1,0},{2,1},{3,2},{4,7},{5,4},{6,5},{7,6},{8,11},{9,8},{10,9... | collective-permute-start | bytes 786440 | tf_op jit(solution)/shard_map/ppermute | solution.py:358
  194.2 22.0 %collective-permute-start.11 = (bf16[512,256]{1,0:T(8,128)(2,1)}, bf16[512,256]{1,0:T(8,128)(2,1)S(1)}, u32[]{:S(2)}, u32[]{:S(2)}) collective-permute-start(bf16[512,256]{1,0:T(8,128)(2,1)} %get-tuple-element.66), channel_id=1, source_target_pairs={{0,7},{1,4},{2,5},{3,6},{4,3},{5,0},{6,1},{7,2},{8,15},{9,12},{10,... | collective-permute-start | bytes 786440 | tf_op jit(solution)/shard_map/ppermute | solution.py:358
  206.1 28.0 %collective-permute-start.16 = (bf16[512,256]{1,0:T(8,128)(2,1)}, bf16[512,256]{1,0:T(8,128)(2,1)S(1)}, u32[]{:S(2)}, u32[]{:S(2)}) collective-permute-start(bf16[512,256]{1,0:T(8,128)(2,1)} %get-tuple-element.69), channel_id=1, source_target_pairs={{0,3},{1,0},{2,1},{3,2},{4,7},{5,4},{6,5},{7,6},{8,11},{9,8},{10,9... | collective-permute-start | bytes 786440 | tf_op jit(solution)/shard_map/ppermute | solution.py:358
  215.2 1.1 copy-start.8
  215.2 6.4 %copy-start.7 = (bf16[512,256]{1,0:T(8,128)(2,1)S(1)}, bf16[512,256]{1,0:T(8,128)(2,1)}, u32[]{:S(2)}) copy-start(bf16[512,256]{1,0:T(8,128)(2,1)} %get-tuple-element.70) | copy-start | bytes 786436
  215.2 6.4 %collective-permute-start.12 = (bf16[512,256]{1,0:T(8,128)(2,1)}, bf16[512,256]{1,0:T(8,128)(2,1)S(1)}, u32[]{:S(2)}, u32[]{:S(2)}) collective-permute-start(bf16[512,256]{1,0:T(8,128)(2,1)} %get-tuple-element.67), channel_id=1, source_target_pairs={{0,3},{1,0},{2,1},{3,2},{4,7},{5,4},{6,5},{7,6},{8,11},{9,8},{10,9... | collective-permute-start | bytes 786440 | tf_op jit(solution)/shard_map/ppermute | solution.py:358
  216.3 9.5 %collective-permute-start.13 = (bf16[512,256]{1,0:T(8,128)(2,1)S(1)}, bf16[512,256]{1,0:T(8,128)(2,1)S(1)}, u32[]{:S(2)}, u32[]{:S(2)}) collective-permute-start(bf16[512,256]{1,0:T(8,128)(2,1)S(1)} %copy-done.8), channel_id=1, source_target_pairs={{0,7},{1,4},{2,5},{3,6},{4,3},{5,0},{6,1},{7,2},{8,15},{9,12},{10,... | collective-permute-start | bytes 786440 | tf_op jit(solution)/shard_map/ppermute | solution.py:358
  221.6 13.8 %collective-permute-start.17 = (bf16[512,256]{1,0:T(8,128)(2,1)S(1)}, bf16[512,256]{1,0:T(8,128)(2,1)S(1)}, u32[]{:S(2)}, u32[]{:S(2)}) collective-permute-start(bf16[512,256]{1,0:T(8,128)(2,1)S(1)} %copy-done.7), channel_id=1, source_target_pairs={{0,7},{1,4},{2,5},{3,6},{4,3},{5,0},{6,1},{7,2},{8,15},{9,12},{10,... | collective-permute-start | bytes 786440 | tf_op jit(solution)/shard_map/ppermute | solution.py:358
  234.0 6.4 %collective-permute-start.20 = (bf16[512,256]{1,0:T(8,128)(2,1)}, bf16[512,256]{1,0:T(8,128)(2,1)S(1)}, u32[]{:S(2)}, u32[]{:S(2)}) collective-permute-start(bf16[512,256]{1,0:T(8,128)(2,1)} %get-tuple-element.71), channel_id=1, source_target_pairs={{0,3},{1,0},{2,1},{3,2},{4,7},{5,4},{6,5},{7,6},{8,11},{9,8},{10,9... | collective-permute-start | bytes 786440 | tf_op jit(solution)/shard_map/ppermute | solution.py:358
  234.1 8.8 %collective-permute-start.21 = (bf16[512,256]{1,0:T(8,128)(2,1)}, bf16[512,256]{1,0:T(8,128)(2,1)S(1)}, u32[]{:S(2)}, u32[]{:S(2)}) collective-permute-start(bf16[512,256]{1,0:T(8,128)(2,1)} %get-tuple-element.72), channel_id=1, source_target_pairs={{0,7},{1,4},{2,5},{3,6},{4,3},{5,0},{6,1},{7,2},{8,15},{9,12},{10,... | collective-permute-start | bytes 786440 | tf_op jit(solution)/shard_map/ppermute | solution.py:358
  240.4 2.5 %copy-start.4 = (bf16[1,512,2048]{2,1,0:T(8,128)(2,1)}, bf16[1,512,2048]{2,1,0:T(8,128)(2,1)S(1)}, u32[]{:S(2)}) copy-start(bf16[1,512,2048]{2,1,0:T(8,128)(2,1)S(1)} %bitcast_dynamic-update-slice_fusion.1) | copy-start | bytes 6291460

commit v3 on v2

v3 whole, which is shorter than its diff:
```python
import functools

import jax
import jax.numpy as jnp
from jax import lax
from jax.experimental import pallas as pl
from jax.experimental.pallas import tpu as pltpu
from jax.sharding import PartitionSpec as P

CHUNK = 128
GROUP = 4
EXTRA = 16
SLOTS = 3
TILE = 256
BF16 = jnp.bfloat16
F32 = jnp.float32
COST = pl.CostEstimate(flops=0, bytes_accessed=0, transcendentals=0)


def turned(cols_ref, first):
    lanes = cols_ref.shape[1]
    return pltpu.roll(
        cols_ref[...], lax.rem(2 * lanes - first - GROUP * pl.program_id(0), lanes), axis=1
    )


def prep_kernel(
    chunks, heads, decay_ref, starts_ref, reads_ref,
    cols_ref, cumr_ref, openr_ref, keep_ref, whole_ref, cntr_ref, readst_ref,
):
    groups = heads // GROUP
    rows = heads + 8
    col = lax.broadcasted_iota(jnp.int32, (rows, CHUNK), 1)
    after = jnp.zeros((rows, 1), F32)
    for c in reversed(range(chunks)):
        at = slice(c * CHUNK, (c + 1) * CHUNK)
        decay = jnp.concatenate(
            [decay_ref[at, :], jnp.zeros((CHUNK, CHUNK - heads), F32)], axis=1
        ).T[:heads]
        starts = jnp.broadcast_to(starts_ref[:, at].astype(F32), (8, CHUNK))
        cum = jnp.concatenate([decay, starts], axis=0)
        shift = 1
        while shift < CHUNK:
            cum = cum + jnp.where(col >= shift, pltpu.roll(cum, shift, axis=1), 0.0)
            shift *= 2
        last = cum[:, CHUNK - 1 :]
        cnt, end = cum[heads : heads + 1], last[heads : heads + 1]
        linked = jnp.where(cnt == end, 1.0, 0.0)
        tail = jnp.exp(jnp.minimum(last - cum, 0.0)) * linked
        later = jnp.where(after[heads : heads + 1] == 0.0, jnp.exp(after), 0.0)
        reach = tail * later
        opened = jnp.exp(cum) * jnp.where(cnt == 0.0, 1.0, 0.0)
        keep = jnp.where(end == 0.0, jnp.exp(last), 0.0)
        after = after + last
        cntr_ref[:, at] = cnt
        stack = [cum, tail[:heads], reach[:heads]]
        stack.append(jnp.zeros((CHUNK - 3 * heads - 8, CHUNK), F32))
        cols_ref[at, :] = jnp.concatenate(stack, axis=0).T
        for g in range(groups):
            lane = slice(g * GROUP, (g + 1) * GROUP)
            cumr_ref[g, :, at] = cum[lane]
            openr_ref[g, :, at] = opened[lane]
            keep_ref[g, c * GROUP : (c + 1) * GROUP, :] = jnp.broadcast_to(
                keep[lane], (GROUP, 128)
            )
    whole = jnp.where(after[heads : heads + 1] == 0.0, jnp.exp(after), 0.0)
    for g in range(groups):
        whole_ref[g] = jnp.broadcast_to(whole[g * GROUP : (g + 1) * GROUP], (GROUP, 128))
    readst_ref[...] = reads_ref[...].astype(F32).T.astype(BF16)


def near_kernel(
    chunks, heads, pieces, gain_ref, writes_ref, reads_ref, readst_ref, cntr_ref, cols_ref,
    cumr_ref, openr_ref, keep_ref, whole_ref, *refs,
):
    cot_refs, (out_ref, state_ref, score_ref) = refs[: len(pieces)], refs[len(pieces) :]
    group = pl.program_id(0)

    @pl.when(group == 0)
    def _():
        row = lax.broadcasted_iota(jnp.int32, (CHUNK, CHUNK), 0)
        col = lax.broadcasted_iota(jnp.int32, (CHUNK, CHUNK), 1)
        for c in range(chunks):
            at = slice(c * CHUNK, (c + 1) * CHUNK)
            scores = lax.dot_general(
                writes_ref[at, :], reads_ref[at, :], (((1,), (1,)), ((), ())),
                preferred_element_type=F32,
            )
            linked = (row <= col) & (cols_ref[at, heads : heads + 1] == cntr_ref[:, at])
            score_ref[at, :] = jnp.where(linked, scores, 0.0)

    cols = turned(cols_ref, 0)
    where = []
    for p, length in enumerate(pieces):
        where += [(p, i) for i in range(length // CHUNK)]
    width = readst_ref.shape[0]
    for j in range(GROUP):
        lane = slice(j * 128, (j + 1) * 128)
        gain = gain_ref[0, group * GROUP + j]
        later = None
        for c in reversed(range(chunks)):
            at = slice(c * CHUNK, (c + 1) * CHUNK)
            piece, inner = where[c]
            cot = cot_refs[piece][inner * CHUNK : (inner + 1) * CHUNK, lane]
            spread = cumr_ref[0, j : j + 1, at] - cols[at, j : j + 1]
            weight = (jnp.exp(jnp.minimum(spread, 0.0)) * score_ref[at, :]).astype(BF16)
            if later is None:
                total = jnp.dot(weight, cot, preferred_element_type=F32)
            else:
                tail = cols[at, heads + 8 + j : heads + 9 + j]
                reach = (tail * writes_ref[at, :].astype(F32)).astype(BF16)
                total = jnp.dot(
                    jnp.concatenate([weight, reach], axis=1),
                    jnp.concatenate([cot, later.astype(BF16)], axis=0),
                    preferred_element_type=F32,
                )
            out_ref[at, lane] = (total + gain * cot.astype(F32)).astype(BF16)
            scaled = (readst_ref[:, at].astype(F32) * openr_ref[0, j : j + 1, at]).astype(BF16)
            state = jnp.dot(scaled, cot, preferred_element_type=F32)
            if later is not None:
                state = state + keep_ref[0, c * GROUP + j : c * GROUP + j + 1, :] * later
            later = state
        state_ref[j, :width, :] = later.astype(BF16)
        keep = jnp.broadcast_to(whole_ref[0, j : j + 1, :], (EXTRA, 128))
        high = keep.astype(BF16)
        low = (keep - high.astype(F32)).astype(BF16)
        top = lax.broadcasted_iota(jnp.int32, (EXTRA, 128), 0) < EXTRA // 2
        state_ref[j, width:, :] = jnp.where(top, high.astype(F32), low.astype(F32)).astype(BF16)


def fetch(slab_ref, which, blocks, held, sem):
    for b, block in enumerate(blocks):
        chosen = [slab_ref[0] == q for q, w in enumerate(which) if w == b]
        if chosen:

            @pl.when(functools.reduce(jnp.logical_or, chosen))
            def _():
                pltpu.make_async_copy(block, held, sem).start()


def main_kernel(whiches, heads, slab_ref, *refs):
    near, writes, cols, later, refs = refs[0:2], refs[2:4], refs[4:6], refs[6:8], refs[8:]
    weight_ref, refs = refs[0], refs[1:]
    blocks, (x_ref, own_ref, other_ref, acc_ref, held, sems) = refs[:-6], refs[-6:]
    tokens, step_width = near[0].shape
    rows = weight_ref.shape[0]
    step, steps = pl.program_id(0), pl.num_programs(0)

    @pl.when(step == 0)
    def _():
        acc_ref[...] = jnp.zeros_like(acc_ref)
        for i, which in enumerate(whiches):
            fetch(slab_ref, which, blocks, held.at[i], sems.at[i])

    for side in range(2):
        reach = turned(cols[side], 2 * heads + 8)
        for j in range(GROUP):
            lane = slice(j * 128, (j + 1) * 128)
            far = jnp.dot(writes[side][...], later[side][j], preferred_element_type=F32)
            total = near[side][:, lane].astype(F32) + reach[:, j : j + 1] * far
            x_ref[side * tokens : (side + 1) * tokens, lane] = total.astype(BF16)

    @pl.when(step == 0)
    def _():
        for i in range(len(whiches)):
            pltpu.make_async_copy(blocks[0], held.at[i], sems.at[i]).wait()

    depth = pl.ds(pl.multiple_of(step * step_width, step_width), step_width)
    for i in range(len(whiches) + 1):
        block = weight_ref[...] if i == 0 else held[i - 1, :, depth]
        acc_ref[:, i * rows : (i + 1) * rows] += lax.dot_general(
            x_ref[...], block, (((1,), (1,)), ((), ())), preferred_element_type=F32
        )

    @pl.when(step == steps - 1)
    def _():
        own_ref[...] = acc_ref[:tokens].astype(BF16)
        other_ref[...] = acc_ref[tokens:].astype(BF16)


def product_kernel(which, slab_ref, x_ref, *refs):
    blocks, (own_ref, other_ref, held, x_held, sem, x_sems) = refs[:-6], refs[-6:]
    fetch(slab_ref, which, blocks, held, sem)
    tokens = own_ref.shape[0]
    tiles = [
        pltpu.make_async_copy(
            x_ref.at[i * TILE : (i + 1) * TILE], x_held.at[i * TILE : (i + 1) * TILE], x_sems.at[i]
        )
        for i in range(2 * tokens // TILE)
    ]
    for tile in tiles:
        tile.start()
    pltpu.make_async_copy(blocks[0], held, sem).wait()
    for i, tile in enumerate(tiles):
        tile.wait()
        out_ref = own_ref if i * TILE < tokens else other_ref
        at = (i * TILE) % tokens
        out_ref[at : at + TILE, :] = lax.dot_general(
            x_held[i * TILE : (i + 1) * TILE, :], held[...],
            (((1,), (1,)), ((), ())), preferred_element_type=F32,
        ).astype(BF16)


def gate(x, *after):
    return lax.optimization_barrier((x,) + after)[0]


def step3(g, *_):
    return (g, 0, 0)


def whole2(g, *_):
    return (0, 0)


def columns2(g, *_):
    return (0, g)


def prepared(reads, decay, starts):
    tokens, heads = decay.shape
    width = reads.shape[1]
    chunks = tokens // CHUNK
    groups = heads // GROUP

    def like(*shape):
        return jax.ShapeDtypeStruct(shape, F32)

    return pl.pallas_call(
        functools.partial(prep_kernel, chunks, heads),
        out_shape=[like(tokens, CHUNK)]
        + [like(groups, GROUP, tokens)] * 2
        + [like(groups, chunks * GROUP, 128), like(groups, GROUP, 128), like(1, tokens)]
        + [jax.ShapeDtypeStruct((width, tokens), BF16)],
        cost_estimate=COST,
        name="prep",
    )(decay, starts, reads)


def near_part(cots, writes, reads, gains, ready):
    cols, cumr, openr, keep, whole, cntr, reads_t = ready
    heads = gains.shape[1]
    tokens, width = writes.shape
    size = cots[0].shape[1] // heads
    chunks = tokens // CHUNK
    groups = heads // GROUP
    pieces = [c.shape[0] for c in cots]
    return pl.pallas_call(
        functools.partial(near_kernel, chunks, heads, pieces),
        grid=(groups,),
        in_specs=[
            pl.BlockSpec(memory_space=pltpu.SMEM),
            pl.BlockSpec((tokens, width), whole2),
            pl.BlockSpec((tokens, width), whole2),
            pl.BlockSpec((width, tokens), whole2),
            pl.BlockSpec((1, tokens), whole2),
            pl.BlockSpec((tokens, CHUNK), whole2),
            pl.BlockSpec((1, GROUP, tokens), step3),
            pl.BlockSpec((1, GROUP, tokens), step3),
            pl.BlockSpec((1, chunks * GROUP, 128), step3),
            pl.BlockSpec((1, GROUP, 128), step3),
        ]
        + [pl.BlockSpec((length, GROUP * size), columns2) for length in pieces],
        out_specs=[
            pl.BlockSpec((tokens, GROUP * size), columns2),
            pl.BlockSpec((GROUP, width + EXTRA, size), step3),
        ],
        out_shape=[
            jax.ShapeDtypeStruct((tokens, heads * size), BF16),
            jax.ShapeDtypeStruct((heads, width + EXTRA, size), BF16),
        ],
        scratch_shapes=[pltpu.VMEM((tokens, CHUNK), F32)],
        cost_estimate=COST,
        name="near",
    )(gains, writes, reads, reads_t, cntr, cols, cumr, openr, keep, whole, *cots)


def arrivals(m):
    plan = []
    for q in range(m):
        order = [(0, 0)]
        for k in range(1, m):
            order += [(1, k)] * (q >= k) + [(-1, k)] * (q + k < m)
        plan.append(order)
    return plan


def indexed(slots):
    distinct = []
    for picks in slots:
        distinct += [p for p in picks if p not in distinct]
    return distinct, [[distinct.index(p) for p in picks] for picks in slots]


def main_part(near, writes, cols, later, weight, blocks, slots, slab, heads):
    tokens, width = writes[0].shape
    rows, depth = weight.shape
    size = depth // heads
    count = len(slots) + 1
    distinct, whiches = indexed(slots)
    block2 = pl.BlockSpec((tokens, GROUP * size), columns2)
    return pl.pallas_call(
        functools.partial(main_kernel, whiches, heads),
        grid_spec=pltpu.PrefetchScalarGridSpec(
            num_scalar_prefetch=1,
            grid=(heads // GROUP,),
            in_specs=[block2] * 2
            + [pl.BlockSpec((tokens, width), whole2)] * 2
            + [pl.BlockSpec((tokens, CHUNK), whole2)] * 2
            + [pl.BlockSpec((GROUP, width, size), step3)] * 2
            + [pl.BlockSpec((rows, GROUP * size), columns2)]
            + [pl.BlockSpec(memory_space=pl.ANY)] * len(distinct),
            out_specs=[pl.BlockSpec((2 * tokens, GROUP * size), columns2)]
            + [pl.BlockSpec((tokens, count * rows), whole2)] * 2,
            scratch_shapes=[
                pltpu.VMEM((2 * tokens, count * rows), F32),
                pltpu.VMEM((count - 1, rows, depth), BF16),
                pltpu.SemaphoreType.DMA((count - 1,)),
            ],
        ),
        out_shape=[jax.ShapeDtypeStruct((2 * tokens, depth), BF16)]
        + [jax.ShapeDtypeStruct((tokens, count * rows), BF16)] * 2,
        cost_estimate=COST,
        name="main",
    )(slab.reshape(1), *near, *writes, *cols, *later, weight, *[blocks[p] for p in distinct])


def product(x, blocks, picks, slab, tokens):
    distinct, (which,) = indexed([picks])
    rows, depth = blocks[picks[0]].shape
    vmem = pl.BlockSpec(memory_space=pltpu.VMEM)
    return pl.pallas_call(
        functools.partial(product_kernel, which),
        in_specs=[pl.BlockSpec(memory_space=pltpu.SMEM)]
        + [pl.BlockSpec(memory_space=pl.ANY)] * (1 + len(distinct)),
        out_specs=[vmem] * 2,
        scratch_shapes=[
            pltpu.VMEM((rows, depth), BF16),
            pltpu.VMEM(x.shape, BF16),
            pltpu.SemaphoreType.DMA,
            pltpu.SemaphoreType.DMA((x.shape[0] // TILE,)),
        ],
        out_shape=[jax.ShapeDtypeStruct((tokens, rows), BF16)] * 2,
        cost_estimate=COST,
        name="product",
    )(slab.reshape(1), x, *[blocks[p] for p in distinct])


def assemble_kernel(counts, columns_ref, *refs):
    pieces, out_ref = refs[:-1], refs[-1]
    rows = pieces[0].shape[1] // counts[0]
    at = 0
    for piece, count in zip(pieces, counts):
        for i in range(count):
            column = pl.multiple_of(columns_ref[at] * rows, rows)
            out_ref[0, :, pl.ds(column, rows)] = piece[:, i * rows : (i + 1) * rows]
            at += 1


def assembled(pieces, columns, rows):
    counts = [piece.shape[1] // rows for piece in pieces]
    if rows % 128:
        result = jnp.zeros((1, pieces[0].shape[0], sum(counts) * rows), BF16)
        at = 0
        for piece, count in zip(pieces, counts):
            for i in range(count):
                result = lax.dynamic_update_slice(
                    result, piece[None, :, i * rows : (i + 1) * rows], (0, 0, columns[at] * rows)
                )
                at += 1
        return result
    vmem = pl.BlockSpec(memory_space=pltpu.VMEM)
    return pl.pallas_call(
        functools.partial(assemble_kernel, counts),
        in_specs=[pl.BlockSpec(memory_space=pltpu.SMEM)] + [vmem] * len(pieces),
        out_specs=vmem,
        out_shape=jax.ShapeDtypeStruct((1, pieces[0].shape[0], sum(counts) * rows), BF16),
        compiler_params=pltpu.CompilerParams(vmem_limit_bytes=32 << 20),
        cost_estimate=COST,
        name="assemble",
    )(columns, *pieces)


def parts_of(packed, width):
    state = packed[:, :width, :].astype(F32)
    high = packed[:, width : width + 1, :].astype(F32)
    low = packed[:, width + EXTRA // 2 : width + EXTRA // 2 + 1, :].astype(F32)
    return state, high + low


def body(n, pipes, cotangent, input_map, output_map, log_decay, flight_starts, skip_gain, in_weight):
    cot, weight = cotangent[0], in_weight[0]
    writes, reads, decay = input_map[0], output_map[0], log_decay[0]
    tokens, heads = decay.shape
    width = writes.shape[1]
    size = cot.shape[1] // heads
    rows = weight.shape[0]
    m = n // 2
    mine = lax.axis_index("seq")
    slab, side = mine // 2, mine % 2
    first = side == 0

    pair = [(s, s ^ 1) for s in range(n)]

    def swap(x):
        return lax.ppermute(x, "seq", pair)

    def down(k):
        return [(s, s - 2) for s in range(2, n - 2 * (k - 1))]

    blocks = {(0, 0): weight}
    for k in range(1, m):
        blocks[1, k] = lax.ppermute(
            blocks.get((1, k - 1), weight), "seq",
            [(s, s + 2) for s in range(2 * (k - 1), n - 2)],
        )
        if k < m - 1:
            blocks[-1, k] = lax.ppermute(blocks.get((-1, k - 1), weight), "seq", down(k))

    writes_b, reads_b, decay_b, starts_b = [
        swap(x) for x in (writes, reads, decay, flight_starts)
    ]
    small = (writes_b, reads_b, decay_b, starts_b)
    cots_b = [swap(gate(cot[:CHUNK], *small)), swap(cot[CHUNK:])]

    ready_a = prepared(reads, decay, flight_starts)
    near_a, state_a = near_part(
        [gate(cot, *small)], writes, reads, skip_gain, ready_a
    )
    ready_b = prepared(reads_b, decay_b, starts_b)
    half = heads // 2
    leaving = lax.dynamic_slice_in_dim(state_a, (1 - side) * half, half, 0)
    got = swap(gate(leaving, cots_b[0]))
    kept = lax.dynamic_slice_in_dim(state_a, side * half, half, 0)
    state_0, keep_0 = parts_of(jnp.where(first, kept, got), width)
    state_1, keep_1 = parts_of(jnp.where(first, got, kept), width)
    slab_state, slab_keep = state_0 + keep_0 * state_1, keep_0 * keep_1
    later = jnp.zeros((half, width, size), BF16)
    for at in reversed(range(1, m)):
        leaving = (slab_state + slab_keep * later.astype(F32)).astype(BF16)
        if at == m - 1:
            leaving = gate(leaving, blocks[1, 1], blocks[-1, 1], ready_b[0])
        later = later + lax.ppermute(
            leaving, "seq", [(2 * at + y, 2 * at - 2 + y) for y in range(2)]
        )
    blocks[-1, m - 1] = lax.ppermute(gate(blocks[-1, m - 2], later), "seq", down(m - 1))
    other = swap(later)
    cots_b[0] = gate(cots_b[0], later)
    near_b, state_b = near_part(cots_b, writes_b, reads_b, skip_gain, ready_b)
    last = jnp.where(first, jnp.stack([later, other]), jnp.stack([other, later]))
    last = last.reshape(heads, width, size)
    state_1, keep_1 = parts_of(jnp.where(first, state_b, state_a), width)
    early = (state_1 + keep_1 * last.astype(F32)).astype(BF16)
    later_a = jnp.where(first, early, last)
    later_b = jnp.where(first, last, early)

    plan = arrivals(m)
    slots = [[plan[q][slot] for q in range(m)] for slot in range(m)]
    count = min(m - 1, SLOTS)
    x, own, swapped = main_part(
        (near_a, near_b), (writes, writes_b), (ready_a[0], ready_b[0]), (later_a, later_b),
        weight, blocks, slots[1:count], slab, heads,
    )
    todo = [(slots[:count], (own, swapped))]
    for slot in range(count, m):
        todo.append(([slots[slot]], product(x, blocks, slots[slot], slab, tokens)))
    pieces, columns = [], []
    for picked, got in todo:
        table = jnp.array(
            [[2 * (q - way * k) for q, (way, k) in enumerate(picks)] for picks in picked],
            jnp.int32,
        )[:, slab]
        for flip in range(2):
            route = [
                (s * pipes + p, (s ^ flip) * pipes + (p - 1) % pipes)
                for s in range(n) for p in range(pipes)
            ]
            pieces.append(lax.ppermute(got[flip], ("seq", "pipe"), route))
            columns.append(table + (side ^ flip))
    return assembled(pieces, jnp.concatenate(columns), rows)


def solution(mesh):
    n, pipes = mesh.shape["seq"], mesh.shape["pipe"]
    placed = (
        P("pipe", "seq", None),
        P("pipe", "seq", None),
        P("pipe", "seq", None),
        P("pipe", "seq", None),
        P("pipe", "seq"),
        P("pipe", None),
        P("pipe", "seq", None),
    )
    return jax.shard_map(
        functools.partial(body, n, pipes),
        mesh=mesh,
        in_specs=placed,
        out_specs=P("pipe", "seq", None),
        check_vma=False,
    )
```

time: 247 us -> 215 us (0.87); the launches traced: 244 us -> 214 us
  Pallas kernels: 90.9 us -> 67.8 us
  waiting for transfers between devices: 98.8 us -> 89 us
  starting transfers between devices: 35.3 us -> 38.4 us
    pallas_call x9 -> x7, Pallas kernels: 90.9 us -> 67.8 us  [the longest x2 30.5 us: near_part(): pl.pallas_call(functools.partial(near_kernel, chunks, heads, pieces), gri...]
    ppermute x5 -> x8, waiting for transfers between devices: 31.6 us -> 11.2 us  [swap(): return lax.ppermute(x, 'seq', pair)]
    ppermute x3, waiting for transfers between devices: 0.01 us -> 7.79 us  [body(): lax.ppermute(blocks.get((1, k - 1), weight), 'seq', [(s, s + 2) for s in...]
    slice x0 -> x2, local copies, waits for them, and re-layouts: none -> 6.45 us  [body(): cots_b = [swap(gate(cot[:CHUNK], *small)), swap(cot[CHUNK:])]]
    ppermute x3, waiting for transfers between devices: 52.5 us -> 55.5 us  [body(): lax.ppermute(leaving, 'seq', [(2 * at + y, 2 * at - 2 + y) for y in range...]
    ppermute x5 -> x8, starting transfers between devices: 3.13 us -> 5.89 us  [swap(): return lax.ppermute(x, 'seq', pair)]
    ppermute x11 -> x7, starting transfers between devices: 18.8 us -> 18.2 us  [the longest x4 8.26 us: body(): pieces.append(lax.ppermute(got[flip], ('seq', 'pipe'), route))]
    ppermute x11 -> x7, waiting for transfers between devices: 14.6 us -> 14.5 us  [the longest x4 11.6 us: body(): pieces.append(lax.ppermute(got[flip], ('seq', 'pipe'), route))]
  transfers between devices with their start and end apart: 22 -> 21, of which waited for: 8 -> 9; matrix products, arithmetic and copies ran while one was open for 6% -> 8% of each run, Pallas kernels for 37% -> 31%
where the time goes in v3:
time: 215 us; the launch traced here: 214 us
  waiting for transfers between devices  89 us (41%)
  Pallas kernels  67.8 us (32%)
  starting transfers between devices  38.4 us (18%)
  local copies, waits for them, and re-layouts  10.1 us (5%)
  other arithmetic  7.67 us (4%)
    ppermute x3, waiting for transfers between devices, body(): lax.ppermute(leaving, 'seq', [(2 * at + y, 2 * at - 2 + y) for y in range...  55.5 us
    pallas_call x2, Pallas kernels, near_part(): pl.pallas_call(functools.partial(near_kernel, chunks, heads, pieces), gri...  30.5 us
    pallas_call x1, Pallas kernels, main_part(): pl.pallas_call(functools.partial(main_kernel, whiches, heads), grid_spec=...  21.4 us
    ppermute x4, waiting for transfers between devices, body(): pieces.append(lax.ppermute(got[flip], ('seq', 'pipe'), route))  11.6 us
    ppermute x8, waiting for transfers between devices, swap(): return lax.ppermute(x, 'seq', pair)  11.2 us
    ppermute x3, starting transfers between devices, body(): lax.ppermute(blocks.get((1, k - 1), weight), 'seq', [(s, s + 2) for s in...  11 us
    ppermute x4, starting transfers between devices, body(): pieces.append(lax.ppermute(got[flip], ('seq', 'pipe'), route))  8.26 us
    pallas_call x1, Pallas kernels, product(): pl.pallas_call(functools.partial(product_kernel, which), in_specs=[pl.Blo...  8.03 us
  transfers between devices with their start and end apart: 21, of which 9 were waited for; matrix products, arithmetic and copies ran while one was open for 8% of the time, Pallas kernels for 31%

profile of v3, /device:TPU:9, one launch (start us, length us, event | category | flops | bytes accessed | tf_op | source)
XLA Modules:
  0.0 214.5 jit_solution(15055227059985322228)
XLA Ops:
  0.0 1.2 collective-permute-start
  1.2 0.2 collective-permute-start.1
  1.5 1.0 copy.10
  2.4 1.3 collective-permute-start.2
  4.0 2.4 %slice_bitcast_fusion.1 = bf16[128,4096]{1,0:T(8,128)(2,1)} fusion(bf16[1,512,4096]{2,1,0:T(8,128)(2,1)} %param.9), kind=kLoop, calls=%fused_computation.10 | loop fusion | bytes 2097152 | tf_op jit(solution)/shard_map/slice | solution.py:424
  6.4 6.7 %collective-permute-done.3.starts_ref = s32[1,512]{1,0:T(1,128)S(1)} collective-permute-done((s32[1,512]{1,0:T(1,128)}, s32[1,512]{1,0:T(1,128)S(1)}, u32[]{:S(2)}, u32[]{:S(2)}) %collective-permute-start.3) | collective-permute-done | bytes 2080 | tf_op jit(solution)/shard_map/ppermute | solution.py:406
  13.1 1.3 collective-permute-start.4
  14.4 3.2 %collective-permute-start.6 = (bf16[256,4096]{1,0:T(8,128)(2,1)}, bf16[256,4096]{1,0:T(8,128)(2,1)S(1)}, u32[]{:S(2)}, u32[]{:S(2)}) collective-permute-start(bf16[256,4096]{1,0:T(8,128)(2,1)} %bitcast.13.refs_8_), channel_id=1, source_target_pairs={{0,8},{4,12},{8,16},{12,20},{16,24},{20,28},{1,9},{5,13},{9,17},{1... | collective-permute-start | bytes 6291464 | tf_op jit(solution)/shard_map/ppermute | solution.py:413
  17.6 2.2 %collective-permute-start.7 = (bf16[256,4096]{1,0:T(8,128)(2,1)}, bf16[256,4096]{1,0:T(8,128)(2,1)}, u32[]{:S(2)}, u32[]{:S(2)}) collective-permute-start(bf16[256,4096]{1,0:T(8,128)(2,1)} %bitcast.13.refs_8_), channel_id=1, source_target_pairs={{8,0},{12,4},{16,8},{20,12},{24,16},{28,20},{9,1},{13,5},{17,9},{2... | collective-permute-start | bytes 6291464 | tf_op jit(solution)/shard_map/ppermute | solution.py:418
  19.8 2.9 %prep.2 = (f32[512,128]{1,0:T(8,128)}, f32[8,4,512]{2,1,0:T(4,128)}, f32[8,4,512]{2,1,0:T(4,128)}, f32[8,16,128]{2,1,0:T(8,128)}, f32[8,4,128]{2,1,0:T(4,128)}, ...) custom-call(f32[512,32]{1,0:T(8,128)} %bitcast.28, s32[1,512]{1,0:T(1,128)} %starts_ref.1, bf16[512,128]{1,0:T(8,128)(2,1)} %bitcast.34), custom_call_target="tpu_custom_call" | custom-call | tf_op jit(solution)/shard_map/prep/pallas_call | solution.py:229
  22.7 15.3 %near.2 = (bf16[512,4096]{1,0:T(8,128)(2,1)}, bf16[32,144,128]{2,1,0:T(8,128)(2,1)}) custom-call(f32[1,32]{1,0:T(1,128)} %gain_ref.3, bf16[512,128]{1,0:T(8,128)(2,1)} %bitcast.30, bf16[512,128]{1,0:T(8,128)(2,1)} %bitcast.35, bf16[128,512]{1,0:T(8,128)(2,1)} %get-tuple-element.34.readst_ref, f32[1,512]{1,0:T(1,128)} %get-tuple-element.35.cntr_ref, ...), custom_call_target="tpu_custom_call" | custom-call | tf_op jit(solution)/shard_map/near/pallas_call | solution.py:248
  38.0 2.0 constant_dynamic-slice_fusion
  40.0 0.2 collective-permute-start.5
  40.2 4.1 %slice_bitcast_fusion = bf16[384,4096]{1,0:T(8,128)(2,1)} fusion(bf16[1,512,4096]{2,1,0:T(8,128)(2,1)} %param.9), kind=kLoop, calls=%fused_computation | loop fusion | bytes 6291456 | tf_op jit(solution)/shard_map/slice | solution.py:424
  44.2 1.1 collective-permute-start.11
  45.4 2.8 %prep.3 = (f32[512,128]{1,0:T(8,128)}, f32[8,4,512]{2,1,0:T(4,128)}, f32[8,4,512]{2,1,0:T(4,128)}, f32[8,16,128]{2,1,0:T(8,128)}, f32[8,4,128]{2,1,0:T(4,128)}, ...) custom-call(f32[512,32]{1,0:T(8,128)} %copy-done.6, s32[1,512]{1,0:T(1,128)} %copy-done.7, bf16[512,128]{1,0:T(8,128)(2,1)} %copy-done.5), custom_call_target="tpu_custom_call" | custom-call | tf_op jit(solution)/shard_map/prep/pallas_call | solution.py:229
  48.2 4.5 %collective-permute-done.5 = bf16[16,144,128]{2,1,0:T(8,128)(2,1)} collective-permute-done((bf16[16,144,128]{2,1,0:T(8,128)(2,1)}, bf16[16,144,128]{2,1,0:T(8,128)(2,1)}, u32[]{:S(2)}, u32[]{:S(2)}) %collective-permute-start.5) | collective-permute-done | bytes 589856 | tf_op jit(solution)/shard_map/ppermute | solution.py:406
  52.7 1.1 broadcast_select_fusion.2
  54.1 7.8 %collective-permute-done.6.refs_10_.refs_11_.refs_12_ = bf16[256,4096]{1,0:T(8,128)(2,1)S(1)} collective-permute-done((bf16[256,4096]{1,0:T(8,128)(2,1)}, bf16[256,4096]{1,0:T(8,128)(2,1)S(1)}, u32[]{:S(2)}, u32[]{:S(2)}) %collective-permute-start.6) | collective-permute-done | bytes 2097184 | tf_op jit(solution)/shard_map/ppermute | solution.py:413
  61.9 2.9 %collective-permute-done.7.refs_9_ = bf16[256,4096]{1,0:T(8,128)(2,1)} collective-permute-done((bf16[256,4096]{1,0:T(8,128)(2,1)}, bf16[256,4096]{1,0:T(8,128)(2,1)}, u32[]{:S(2)}, u32[]{:S(2)}) %collective-permute-start.7) | collective-permute-done | bytes 2097184 | tf_op jit(solution)/shard_map/ppermute | solution.py:418
  64.8 0.7 collective-permute-start.8
  65.5 2.2 %collective-permute-start.13 = (bf16[256,4096]{1,0:T(8,128)(2,1)}, bf16[256,4096]{1,0:T(8,128)(2,1)}, u32[]{:S(2)}, u32[]{:S(2)}) collective-permute-start(bf16[256,4096]{1,0:T(8,128)(2,1)} %collective-permute-done.7.refs_9_), channel_id=1, source_target_pairs={{8,0},{12,4},{16,8},{20,12},{9,1},{13,5},{17,9},{21,13},{10,2},{14... | collective-permute-start | bytes 6291464 | tf_op jit(solution)/shard_map/ppermute | solution.py:418
  67.7 5.8 %collective-permute-start.14 = (bf16[256,4096]{1,0:T(8,128)(2,1)S(1)}, bf16[256,4096]{1,0:T(8,128)(2,1)}, u32[]{:S(2)}, u32[]{:S(2)}) collective-permute-start(bf16[256,4096]{1,0:T(8,128)(2,1)S(1)} %collective-permute-done.6.refs_10_.refs_11_.refs_12_), channel_id=1, source_target_pairs={{8,16},{12,20},{16,24},{20,28},{9,17},{13,21},{17,25},{21,29},{10,... | collective-permute-start | bytes 6291464 | tf_op jit(solution)/shard_map/ppermute | solution.py:413
  73.5 0.3 add_convert_fusion.2
  73.8 1.3 collective-permute-start.9
  75.1 47.9 %collective-permute-done.9 = bf16[16,128,128]{2,1,0:T(8,128)(2,1)S(1)} collective-permute-done((bf16[16,128,128]{2,1,0:T(8,128)(2,1)S(1)}, bf16[16,128,128]{2,1,0:T(8,128)(2,1)S(1)}, u32[]{:S(2)}, u32[]{:S(2)}) %collective-permute-start.9) | collective-permute-done | bytes 524320 | tf_op jit(solution)/shard_map/ppermute | solution.py:443
  123.0 0.4 add_convert_fusion.1
  123.5 1.3 collective-permute-start.10
  124.8 7.6 %collective-permute-done.10 = bf16[16,128,128]{2,1,0:T(8,128)(2,1)S(1)} collective-permute-done((bf16[16,128,128]{2,1,0:T(8,128)(2,1)S(1)}, bf16[16,128,128]{2,1,0:T(8,128)(2,1)S(1)}, u32[]{:S(2)}, u32[]{:S(2)}) %collective-permute-start.10) | collective-permute-done | bytes 524320 | tf_op jit(solution)/shard_map/ppermute | solution.py:443
  132.4 1.0 add.96
  133.4 5.5 %collective-permute-start.17 = (bf16[256,4096]{1,0:T(8,128)(2,1)}, bf16[256,4096]{1,0:T(8,128)(2,1)}, u32[]{:S(2)}, u32[]{:S(2)}) collective-permute-start(bf16[256,4096]{1,0:T(8,128)(2,1)} %collective-permute-done.13.refs_13_.refs_1_), channel_id=1, source_target_pairs={{8,0},{12,4},{9,1},{13,5},{10,2},{14,6},{11,3},{15,7}} | collective-permute-start | bytes 6291464 | tf_op jit(solution)/shard_map/ppermute | solution.py:446
  138.9 2.0 collective-permute-start.18
  140.9 0.2 collective-permute-start.12
  141.1 15.3 %near.3 = (bf16[512,4096]{1,0:T(8,128)(2,1)}, bf16[32,144,128]{2,1,0:T(8,128)(2,1)}) custom-call(f32[1,32]{1,0:T(1,128)} %gain_ref.3, bf16[512,128]{1,0:T(8,128)(2,1)} %copy-done.4, bf16[512,128]{1,0:T(8,128)(2,1)} %copy-done.5, bf16[128,512]{1,0:T(8,128)(2,1)} %get-tuple-element.43.readst_ref, f32[1,512]{1,0:T(1,128)} %get-tuple-element.44.cntr_ref, ...), custom_call_target="tpu_custom_call" | custom-call | tf_op jit(solution)/shard_map/near/pallas_call | solution.py:248
  156.4 1.5 broadcast_select_fusion
  158.1 2.2 %fusion = (bf16[32,128,128]{2,1,0:T(8,128)(2,1)}, bf16[32,128,128]{2,1,0:T(8,128)(2,1)}) fusion(bf16[2,16,128,128]{3,2,1,0:T(8,128)(2,1)S(1)} %maximum_select_fusion, f32[32,128]{1,0:T(8,128)S(1)} %bitcast.42, pred[]{:T(512)S(6)} %eq.5, bf16[32,144,128]{2,1,0:T(8,128)(2,1)S(1)} %broadcast_select_fusion), kind=kLoop, calls=%fused_computation.2 | loop fusion | flops 3670016 | bytes 4210689 | tf_op jit(solution)/shard_map/jit(_where)/select_n | solution.py:455
  160.3 21.4 %main.1 = (bf16[1024,4096]{1,0:T(8,128)(2,1)}, bf16[512,768]{1,0:T(8,128)(2,1)}, bf16[512,768]{1,0:T(8,128)(2,1)}) custom-call(s32[1]{0:T(128)} %bitcast.5.slab_ref, bf16[512,4096]{1,0:T(8,128)(2,1)} %get-tuple-element.42.refs_0_, bf16[512,4096]{1,0:T(8,128)(2,1)} %get-tuple-element.55.refs_1_, bf16[512,128]{1,0:T(8,128)(2,1)} %bitcast.31, ...), custom_call_target="tpu_custom_call" | custom-call | tf_op jit(solution)/shard_map/main/pallas_call | solution.py:302
  181.7 5.1 %collective-permute-start.15 = (bf16[512,768]{1,0:T(8,128)(2,1)}, bf16[512,768]{1,0:T(8,128)(2,1)S(1)}, u32[]{:S(2)}, u32[]{:S(2)}) collective-permute-start(bf16[512,768]{1,0:T(8,128)(2,1)} %get-tuple-element.57), channel_id=1, source_target_pairs={{0,3},{1,0},{2,1},{3,2},{4,7},{5,4},{6,5},{7,6},{8,11},{9,8},{10,9... | collective-permute-start | bytes 2359304 | tf_op jit(solution)/shard_map/ppermute | solution.py:478
  186.8 0.9 collective-permute-start.16
  187.7 8.0 %product.1 = (bf16[512,256]{1,0:T(8,128)(2,1)}, bf16[512,256]{1,0:T(8,128)(2,1)}) custom-call(s32[1]{0:T(128)} %bitcast.5.slab_ref, bf16[1024,4096]{1,0:T(8,128)(2,1)} %get-tuple-element.59.x_ref, bf16[256,4096]{1,0:T(8,128)(2,1)} %collective-permute-done.17.refs_0_, bf16[256,4096]{1,0:T(8,128)(2,1)} %collective-permute-done.13.refs_13_.refs_1_, ...), custom_call_target="tpu_custom_call" | custom-call | tf_op jit(solution)/shard_map/product/pallas_call | solution.py:332
  195.7 1.2 collective-permute-start.19
  197.0 1.0 collective-permute-start.20
  198.0 0.6 constant_dynamic-slice_fusion.1
  200.0 0.7 add_bitcast_fusion.1
  200.8 6.0 %collective-permute-done.16.refs_1_ = bf16[512,768]{1,0:T(8,128)(2,1)S(1)} collective-permute-done((bf16[512,768]{1,0:T(8,128)(2,1)}, bf16[512,768]{1,0:T(8,128)(2,1)S(1)}, u32[]{:S(2)}, u32[]{:S(2)}) %collective-permute-start.16) | collective-permute-done | bytes 786464 | tf_op jit(solution)/shard_map/ppermute | solution.py:478
  206.8 2.6 %collective-permute-done.19.refs_2_ = bf16[512,256]{1,0:T(8,128)(2,1)S(1)} collective-permute-done((bf16[512,256]{1,0:T(8,128)(2,1)}, bf16[512,256]{1,0:T(8,128)(2,1)S(1)}, u32[]{:S(2)}, u32[]{:S(2)}) %collective-permute-start.19) | collective-permute-done | bytes 262176 | tf_op jit(solution)/shard_map/ppermute | solution.py:478
  209.3 3.0 %collective-permute-done.20.refs_3_ = bf16[512,256]{1,0:T(8,128)(2,1)S(1)} collective-permute-done((bf16[512,256]{1,0:T(8,128)(2,1)}, bf16[512,256]{1,0:T(8,128)(2,1)S(1)}, u32[]{:S(2)}, u32[]{:S(2)}) %collective-permute-start.20) | collective-permute-done | bytes 262176 | tf_op jit(solution)/shard_map/ppermute | solution.py:478
  212.3 2.1 %assemble.1 = bf16[1,512,2048]{2,1,0:T(8,128)(2,1)} custom-call(s32[8]{0:T(128)S(1)} %pad_add_fusion.columns_ref, bf16[512,768]{1,0:T(8,128)(2,1)S(1)} %collective-permute-done.15.refs_0_, bf16[512,768]{1,0:T(8,128)(2,1)S(1)} %collective-permute-done.16.refs_1_, bf16[512,256]{1,0:T(8,128)(2,1)S(1)} %collective-permute-done.19.refs_2_, ...), custom_call_target="tpu_custom_call" | custom-call | tf_op jit(solution)/shard_map/assemble/pallas_call | solution.py:373
  (37 shorter events, 0.8 us)
Async XLA Ops:
  0.0 13.1 %collective-permute-start = (bf16[512,128]{1,0:T(8,128)(2,1)}, bf16[512,128]{1,0:T(8,128)(2,1)S(1)}, u32[]{:S(2)}, u32[]{:S(2)}) collective-permute-start(bf16[512,128]{1,0:T(8,128)(2,1)} %bitcast.29), channel_id=1, source_target_pairs={{0,4},{4,0},{8,12},{12,8},{16,20},{20,16},{24,28},{28,24},{1,5},{5... | collective-permute-start | bytes 393224 | tf_op jit(solution)/shard_map/ppermute | solution.py:406
  1.2 11.8 %collective-permute-start.1 = (bf16[512,128]{1,0:T(8,128)(2,1)}, bf16[512,128]{1,0:T(8,128)(2,1)S(1)}, u32[]{:S(2)}, u32[]{:S(2)}) collective-permute-start(bf16[512,128]{1,0:T(8,128)(2,1)} %bitcast.33), channel_id=1, source_target_pairs={{0,4},{4,0},{8,12},{12,8},{16,20},{20,16},{24,28},{28,24},{1,5},{5... | collective-permute-start | bytes 393224 | tf_op jit(solution)/shard_map/ppermute | solution.py:406
  2.4 17.4 %copy-start.3 = (f32[1,512,32]{2,1,0:T(8,128)}, f32[1,512,32]{2,1,0:T(8,128)S(1)}, u32[]{:S(2)}) copy-start(f32[1,512,32]{2,1,0:T(8,128)S(1)} %copy.10) | copy-start | bytes 196612
  2.4 10.6 %collective-permute-start.2 = (f32[512,32]{1,0:T(8,128)S(1)}, f32[512,32]{1,0:T(8,128)S(1)}, u32[]{:S(2)}, u32[]{:S(2)}) collective-permute-start(f32[512,32]{1,0:T(8,128)S(1)} %bitcast.27), channel_id=1, source_target_pairs={{0,4},{4,0},{8,12},{12,8},{16,20},{20,16},{24,28},{28,24},{1,5},{5... | collective-permute-start | bytes 196616 | tf_op jit(solution)/shard_map/ppermute | solution.py:406
  3.8 9.3 %collective-permute-start.3 = (s32[1,512]{1,0:T(1,128)}, s32[1,512]{1,0:T(1,128)S(1)}, u32[]{:S(2)}, u32[]{:S(2)}) collective-permute-start(s32[1,512]{1,0:T(1,128)} %starts_ref.1), channel_id=1, source_target_pairs={{0,4},{4,0},{8,12},{12,8},{16,20},{20,16},{24,28},{28,24},{1,5},{5... | collective-permute-start | bytes 6152 | tf_op jit(solution)/shard_map/ppermute | solution.py:406
  13.0 24.9 %copy-start.7 = (s32[1,512]{1,0:T(1,128)}, s32[1,512]{1,0:T(1,128)S(1)}, u32[]{:S(2)}) copy-start(s32[1,512]{1,0:T(1,128)S(1)} %collective-permute-done.3.starts_ref) | copy-start | bytes 6148
  13.1 24.9 %copy-start.6 = (f32[512,32]{1,0:T(8,128)}, f32[512,32]{1,0:T(8,128)S(1)}, u32[]{:S(2)}) copy-start(f32[512,32]{1,0:T(8,128)S(1)} %collective-permute-done.2.decay_ref) | copy-start | bytes 196612
  13.1 24.9 %copy-start.4 = (bf16[512,128]{1,0:T(8,128)(2,1)}, bf16[512,128]{1,0:T(8,128)(2,1)S(1)}, u32[]{:S(2)}) copy-start(bf16[512,128]{1,0:T(8,128)(2,1)S(1)} %collective-permute-done.writes_ref.refs_3_) | copy-start | bytes 393220
  13.1 24.9 %copy-start.5 = (bf16[512,128]{1,0:T(8,128)(2,1)}, bf16[512,128]{1,0:T(8,128)(2,1)S(1)}, u32[]{:S(2)}) copy-start(bf16[512,128]{1,0:T(8,128)(2,1)S(1)} %collective-permute-done.1.reads_ref) | copy-start | bytes 393220
  13.1 26.9 %collective-permute-start.4 = (bf16[128,4096]{1,0:T(8,128)(2,1)}, bf16[128,4096]{1,0:T(8,128)(2,1)}, u32[]{:S(2)}, u32[]{:S(2)}) collective-permute-start(bf16[128,4096]{1,0:T(8,128)(2,1)} %slice_bitcast_fusion.1), channel_id=1, source_target_pairs={{0,4},{4,0},{8,12},{12,8},{16,20},{20,16},{24,28},{28,24},{1,5},{5... | collective-permute-start | bytes 3145736 | tf_op jit(solution)/shard_map/ppermute | solution.py:406
  14.4 47.5 %collective-permute-start.6 = (bf16[256,4096]{1,0:T(8,128)(2,1)}, bf16[256,4096]{1,0:T(8,128)(2,1)S(1)}, u32[]{:S(2)}, u32[]{:S(2)}) collective-permute-start(bf16[256,4096]{1,0:T(8,128)(2,1)} %bitcast.13.refs_8_), channel_id=1, source_target_pairs={{0,8},{4,12},{8,16},{12,20},{16,24},{20,28},{1,9},{5,13},{9,17},{1... | collective-permute-start | bytes 6291464 | tf_op jit(solution)/shard_map/ppermute | solution.py:413
  17.6 47.2 %collective-permute-start.7 = (bf16[256,4096]{1,0:T(8,128)(2,1)}, bf16[256,4096]{1,0:T(8,128)(2,1)}, u32[]{:S(2)}, u32[]{:S(2)}) collective-permute-start(bf16[256,4096]{1,0:T(8,128)(2,1)} %bitcast.13.refs_8_), channel_id=1, source_target_pairs={{8,0},{12,4},{16,8},{20,12},{24,16},{28,20},{9,1},{13,5},{17,9},{2... | collective-permute-start | bytes 6291464 | tf_op jit(solution)/shard_map/ppermute | solution.py:418
  39.9 12.8 %copy-start.1 = (bf16[32,144,128]{2,1,0:T(8,128)(2,1)S(1)}, bf16[32,144,128]{2,1,0:T(8,128)(2,1)}, u32[]{:S(2)}) copy-start(bf16[32,144,128]{2,1,0:T(8,128)(2,1)} %get-tuple-element.51) | copy-start | bytes 3538948
  40.0 12.7 %collective-permute-start.5 = (bf16[16,144,128]{2,1,0:T(8,128)(2,1)}, bf16[16,144,128]{2,1,0:T(8,128)(2,1)}, u32[]{:S(2)}, u32[]{:S(2)}) collective-permute-start(bf16[16,144,128]{2,1,0:T(8,128)(2,1)} %constant_dynamic-slice_fusion), channel_id=1, source_target_pairs={{0,4},{4,0},{8,12},{12,8},{16,20},{20,16},{24,28},{28,24},{1,5},{5... | collective-permute-start | bytes 1769480 | tf_op jit(solution)/shard_map/ppermute | solution.py:406
  44.2 96.9 %collective-permute-start.11 = (bf16[384,4096]{1,0:T(8,128)(2,1)}, bf16[384,4096]{1,0:T(8,128)(2,1)}, u32[]{:S(2)}, u32[]{:S(2)}) collective-permute-start(bf16[384,4096]{1,0:T(8,128)(2,1)} %slice_bitcast_fusion), channel_id=1, source_target_pairs={{0,4},{4,0},{8,12},{12,8},{16,20},{20,16},{24,28},{28,24},{1,5},{5... | collective-permute-start | bytes 9437192 | tf_op jit(solution)/shard_map/ppermute | solution.py:406
  61.9 61.6 %copy-start = (bf16[256,4096]{1,0:T(8,128)(2,1)}, bf16[256,4096]{1,0:T(8,128)(2,1)S(1)}, u32[]{:S(2)}) copy-start(bf16[256,4096]{1,0:T(8,128)(2,1)S(1)} %collective-permute-done.6.refs_10_.refs_11_.refs_12_) | copy-start | bytes 6291460
  64.8 8.7 %collective-permute-start.8 = (bf16[16,128,128]{2,1,0:T(8,128)(2,1)S(1)}, bf16[16,128,128]{2,1,0:T(8,128)(2,1)S(1)}, u32[]{:S(2)}, u32[]{:S(2)}) collective-permute-start(bf16[16,128,128]{2,1,0:T(8,128)(2,1)S(1)} %add_convert_fusion.3), channel_id=1, source_target_pairs={{24,16},{28,20},{25,17},{29,21},{26,18},{30,22},{27,19},{31,23}} | collective-permute-start | bytes 1572872 | tf_op jit(solution)/shard_map/ppermute | solution.py:443
  65.5 67.8 %collective-permute-start.13 = (bf16[256,4096]{1,0:T(8,128)(2,1)}, bf16[256,4096]{1,0:T(8,128)(2,1)}, u32[]{:S(2)}, u32[]{:S(2)}) collective-permute-start(bf16[256,4096]{1,0:T(8,128)(2,1)} %collective-permute-done.7.refs_9_), channel_id=1, source_target_pairs={{8,0},{12,4},{16,8},{20,12},{9,1},{13,5},{17,9},{21,13},{10,2},{14... | collective-permute-start | bytes 6291464 | tf_op jit(solution)/shard_map/ppermute | solution.py:418
  67.7 71.1 %collective-permute-start.14 = (bf16[256,4096]{1,0:T(8,128)(2,1)S(1)}, bf16[256,4096]{1,0:T(8,128)(2,1)}, u32[]{:S(2)}, u32[]{:S(2)}) collective-permute-start(bf16[256,4096]{1,0:T(8,128)(2,1)S(1)} %collective-permute-done.6.refs_10_.refs_11_.refs_12_), channel_id=1, source_target_pairs={{8,16},{12,20},{16,24},{20,28},{9,17},{13,21},{17,25},{21,29},{10,... | collective-permute-start | bytes 6291464 | tf_op jit(solution)/shard_map/ppermute | solution.py:413
  73.8 49.2 %collective-permute-start.9 = (bf16[16,128,128]{2,1,0:T(8,128)(2,1)S(1)}, bf16[16,128,128]{2,1,0:T(8,128)(2,1)S(1)}, u32[]{:S(2)}, u32[]{:S(2)}) collective-permute-start(bf16[16,128,128]{2,1,0:T(8,128)(2,1)S(1)} %add_convert_fusion.2), channel_id=1, source_target_pairs={{16,8},{20,12},{17,9},{21,13},{18,10},{22,14},{19,11},{23,15}} | collective-permute-start | bytes 1572872 | tf_op jit(solution)/shard_map/ppermute | solution.py:443
  123.5 8.9 %collective-permute-start.10 = (bf16[16,128,128]{2,1,0:T(8,128)(2,1)S(1)}, bf16[16,128,128]{2,1,0:T(8,128)(2,1)S(1)}, u32[]{:S(2)}, u32[]{:S(2)}) collective-permute-start(bf16[16,128,128]{2,1,0:T(8,128)(2,1)S(1)} %get-tuple-element.63), channel_id=1, source_target_pairs={{8,0},{12,4},{9,1},{13,5},{10,2},{14,6},{11,3},{15,7}} | collective-permute-start | bytes 1572872 | tf_op jit(solution)/shard_map/ppermute | solution.py:443
  133.4 54.3 %collective-permute-start.17 = (bf16[256,4096]{1,0:T(8,128)(2,1)}, bf16[256,4096]{1,0:T(8,128)(2,1)}, u32[]{:S(2)}, u32[]{:S(2)}) collective-permute-start(bf16[256,4096]{1,0:T(8,128)(2,1)} %collective-permute-done.13.refs_13_.refs_1_), channel_id=1, source_target_pairs={{8,0},{12,4},{9,1},{13,5},{10,2},{14,6},{11,3},{15,7}} | collective-permute-start | bytes 6291464 | tf_op jit(solution)/shard_map/ppermute | solution.py:446
  138.9 48.8 %collective-permute-start.18 = (bf16[256,4096]{1,0:T(8,128)(2,1)}, bf16[256,4096]{1,0:T(8,128)(2,1)}, u32[]{:S(2)}, u32[]{:S(2)}) collective-permute-start(bf16[256,4096]{1,0:T(8,128)(2,1)} %collective-permute-done.14.refs_14_.refs_2_), channel_id=1, source_target_pairs={{16,24},{20,28},{17,25},{21,29},{18,26},{22,30},{19,27},{23,31}} | collective-permute-start | bytes 6291464 | tf_op jit(solution)/shard_map/ppermute | solution.py:413
  140.9 17.0 %collective-permute-start.12 = (bf16[16,128,128]{2,1,0:T(8,128)(2,1)}, bf16[16,128,128]{2,1,0:T(8,128)(2,1)S(1)}, u32[]{:S(2)}, u32[]{:S(2)}) collective-permute-start(bf16[16,128,128]{2,1,0:T(8,128)(2,1)} %add.96), channel_id=1, source_target_pairs={{0,4},{4,0},{8,12},{12,8},{16,20},{20,16},{24,28},{28,24},{1,5},{5... | collective-permute-start | bytes 1572872 | tf_op jit(solution)/shard_map/ppermute | solution.py:406
  156.4 1.5 copy-start.2
  181.7 19.1 %collective-permute-start.15 = (bf16[512,768]{1,0:T(8,128)(2,1)}, bf16[512,768]{1,0:T(8,128)(2,1)S(1)}, u32[]{:S(2)}, u32[]{:S(2)}) collective-permute-start(bf16[512,768]{1,0:T(8,128)(2,1)} %get-tuple-element.57), channel_id=1, source_target_pairs={{0,3},{1,0},{2,1},{3,2},{4,7},{5,4},{6,5},{7,6},{8,11},{9,8},{10,9... | collective-permute-start | bytes 2359304 | tf_op jit(solution)/shard_map/ppermute | solution.py:478
  186.8 20.0 %collective-permute-start.16 = (bf16[512,768]{1,0:T(8,128)(2,1)}, bf16[512,768]{1,0:T(8,128)(2,1)S(1)}, u32[]{:S(2)}, u32[]{:S(2)}) collective-permute-start(bf16[512,768]{1,0:T(8,128)(2,1)} %get-tuple-element.58), channel_id=1, source_target_pairs={{0,7},{1,4},{2,5},{3,6},{4,3},{5,0},{6,1},{7,2},{8,15},{9,12},{10,... | collective-permute-start | bytes 2359304 | tf_op jit(solution)/shard_map/ppermute | solution.py:478
  187.7 10.3 %copy-start.8 = (s32[1,4]{1,0:T(1,128)S(1)}, s32[1,4]{1,0:T(1,128)}, u32[]{:S(2)}) copy-start(s32[1,4]{1,0:T(1,128)} %constant.46.clone) | copy-start | bytes 52
  195.7 13.6 %collective-permute-start.19 = (bf16[512,256]{1,0:T(8,128)(2,1)}, bf16[512,256]{1,0:T(8,128)(2,1)S(1)}, u32[]{:S(2)}, u32[]{:S(2)}) collective-permute-start(bf16[512,256]{1,0:T(8,128)(2,1)} %get-tuple-element.61), channel_id=1, source_target_pairs={{0,3},{1,0},{2,1},{3,2},{4,7},{5,4},{6,5},{7,6},{8,11},{9,8},{10,9... | collective-permute-start | bytes 786440 | tf_op jit(solution)/shard_map/ppermute | solution.py:478
  197.0 15.4 %collective-permute-start.20 = (bf16[512,256]{1,0:T(8,128)(2,1)}, bf16[512,256]{1,0:T(8,128)(2,1)S(1)}, u32[]{:S(2)}, u32[]{:S(2)}) collective-permute-start(bf16[512,256]{1,0:T(8,128)(2,1)} %get-tuple-element.62), channel_id=1, source_target_pairs={{0,7},{1,4},{2,5},{3,6},{4,3},{5,0},{6,1},{7,2},{8,15},{9,12},{10,... | collective-permute-start | bytes 786440 | tf_op jit(solution)/shard_map/ppermute | solution.py:478

commit v4 on v3

--- a/solution.py
+++ b/solution.py
@@ -11,7 +11,6 @@
 GROUP = 4
 EXTRA = 16
 SLOTS = 3
-TILE = 256
 BF16 = jnp.bfloat16
 F32 = jnp.float32
 COST = pl.CostEstimate(flops=0, bytes_accessed=0, transcendentals=0)
@@ -26,12 +25,13 @@
 
 def prep_kernel(
     chunks, heads, decay_ref, starts_ref, reads_ref,
-    cols_ref, cumr_ref, openr_ref, keep_ref, whole_ref, cntr_ref, readst_ref,
+    cols_ref, cumr_ref, openr_ref, keep_ref, whole_ref, cntr_ref, readst_ref, allr_ref,
 ):
     groups = heads // GROUP
     rows = heads + 8
     col = lax.broadcasted_iota(jnp.int32, (rows, CHUNK), 1)
     after = jnp.zeros((rows, 1), F32)
+    kept = []
     for c in reversed(range(chunks)):
         at = slice(c * CHUNK, (c + 1) * CHUNK)
         decay = jnp.concatenate(
@@ -52,6 +52,7 @@
         opened = jnp.exp(cum) * jnp.where(cnt == 0.0, 1.0, 0.0)
         keep = jnp.where(end == 0.0, jnp.exp(last), 0.0)
         after = after + last
+        kept.append((cum, last))
         cntr_ref[:, at] = cnt
         stack = [cum, tail[:heads], reach[:heads]]
         stack.append(jnp.zeros((CHUNK - 3 * heads - 8, CHUNK), F32))
@@ -66,6 +67,13 @@
     whole = jnp.where(after[heads : heads + 1] == 0.0, jnp.exp(after), 0.0)
     for g in range(groups):
         whole_ref[g] = jnp.broadcast_to(whole[g * GROUP : (g + 1) * GROUP], (GROUP, 128))
+    before = jnp.zeros((rows, 1), F32)
+    for c, (cum, last) in enumerate(reversed(kept)):
+        total = cum + before
+        opened = jnp.exp(total) * jnp.where(total[heads : heads + 1] == 0.0, 1.0, 0.0)
+        before = before + last
+        for g in range(groups):
+            allr_ref[g, :, c * CHUNK : (c + 1) * CHUNK] = opened[g * GROUP : (g + 1) * GROUP]
     readst_ref[...] = reads_ref[...].astype(F32).T.astype(BF16)
 
 
@@ -73,7 +81,8 @@
     chunks, heads, pieces, gain_ref, writes_ref, reads_ref, readst_ref, cntr_ref, cols_ref,
     cumr_ref, openr_ref, keep_ref, whole_ref, *refs,
 ):
-    cot_refs, (out_ref, state_ref, score_ref) = refs[: len(pieces)], refs[len(pieces) :]
+    cot_refs, out_ref, score_ref = refs[: len(pieces)], refs[len(pieces)], refs[-1]
+    state_ref = refs[-2] if len(refs) > len(pieces) + 2 else None
     group = pl.program_id(0)
 
     @pl.when(group == 0)
@@ -115,17 +124,32 @@
                     preferred_element_type=F32,
                 )
             out_ref[at, lane] = (total + gain * cot.astype(F32)).astype(BF16)
+            if c == 0 and state_ref is None:
+                continue
             scaled = (readst_ref[:, at].astype(F32) * openr_ref[0, j : j + 1, at]).astype(BF16)
             state = jnp.dot(scaled, cot, preferred_element_type=F32)
             if later is not None:
                 state = state + keep_ref[0, c * GROUP + j : c * GROUP + j + 1, :] * later
             later = state
-        state_ref[j, :width, :] = later.astype(BF16)
-        keep = jnp.broadcast_to(whole_ref[0, j : j + 1, :], (EXTRA, 128))
-        high = keep.astype(BF16)
-        low = (keep - high.astype(F32)).astype(BF16)
-        top = lax.broadcasted_iota(jnp.int32, (EXTRA, 128), 0) < EXTRA // 2
-        state_ref[j, width:, :] = jnp.where(top, high.astype(F32), low.astype(F32)).astype(BF16)
+        if state_ref is not None:
+            pack(state_ref, j, later, whole_ref[0, j : j + 1, :])
+
+
+def pack(state_ref, j, state, keep):
+    width = state.shape[0]
+    state_ref[j, :width, :] = state.astype(BF16)
+    keep = jnp.broadcast_to(keep, (EXTRA, 128))
+    high = keep.astype(BF16)
+    low = (keep - high.astype(F32)).astype(BF16)
+    top = lax.broadcasted_iota(jnp.int32, (EXTRA, 128), 0) < EXTRA // 2
+    state_ref[j, width:, :] = jnp.where(top, high.astype(F32), low.astype(F32)).astype(BF16)
+
+
+def states_kernel(readst_ref, allr_ref, whole_ref, cot_ref, state_ref):
+    for j in range(GROUP):
+        scaled = (readst_ref[...].astype(F32) * allr_ref[0, j : j + 1, :]).astype(BF16)
+        state = jnp.dot(scaled, cot_ref[:, j * 128 : (j + 1) * 128], preferred_element_type=F32)
+        pack(state_ref, j, state, whole_ref[0, j : j + 1, :])
 
 
 def fetch(slab_ref, which, blocks, held, sem):
@@ -152,24 +176,25 @@
         for i, which in enumerate(whiches):
             fetch(slab_ref, which, blocks, held.at[i], sems.at[i])
 
+    depth = pl.ds(pl.multiple_of(step * step_width, step_width), step_width)
     for side in range(2):
         reach = turned(cols[side], 2 * heads + 8)
         for j in range(GROUP):
             lane = slice(j * 128, (j + 1) * 128)
+            at = pl.ds(pl.multiple_of(step * step_width + j * 128, 128), 128)
             far = jnp.dot(writes[side][...], later[side][j], preferred_element_type=F32)
             total = near[side][:, lane].astype(F32) + reach[:, j : j + 1] * far
-            x_ref[side * tokens : (side + 1) * tokens, lane] = total.astype(BF16)
+            x_ref[side * tokens : (side + 1) * tokens, at] = total.astype(BF16)
 
     @pl.when(step == 0)
     def _():
         for i in range(len(whiches)):
             pltpu.make_async_copy(blocks[0], held.at[i], sems.at[i]).wait()
 
-    depth = pl.ds(pl.multiple_of(step * step_width, step_width), step_width)
     for i in range(len(whiches) + 1):
         block = weight_ref[...] if i == 0 else held[i - 1, :, depth]
         acc_ref[:, i * rows : (i + 1) * rows] += lax.dot_general(
-            x_ref[...], block, (((1,), (1,)), ((), ())), preferred_element_type=F32
+            x_ref[:, depth], block, (((1,), (1,)), ((), ())), preferred_element_type=F32
         )
 
     @pl.when(step == steps - 1)
@@ -179,24 +204,13 @@
 
 
 def product_kernel(which, slab_ref, x_ref, *refs):
-    blocks, (own_ref, other_ref, held, x_held, sem, x_sems) = refs[:-6], refs[-6:]
+    blocks, (own_ref, other_ref, held, sem) = refs[:-4], refs[-4:]
     fetch(slab_ref, which, blocks, held, sem)
+    pltpu.make_async_copy(blocks[0], held, sem).wait()
     tokens = own_ref.shape[0]
-    tiles = [
-        pltpu.make_async_copy(
-            x_ref.at[i * TILE : (i + 1) * TILE], x_held.at[i * TILE : (i + 1) * TILE], x_sems.at[i]
-        )
-        for i in range(2 * tokens // TILE)
-    ]
-    for tile in tiles:
-        tile.start()
-    pltpu.make_async_copy(blocks[0], held, sem).wait()
-    for i, tile in enumerate(tiles):
-        tile.wait()
-        out_ref = own_ref if i * TILE < tokens else other_ref
-        at = (i * TILE) % tokens
-        out_ref[at : at + TILE, :] = lax.dot_general(
-            x_held[i * TILE : (i + 1) * TILE, :], held[...],
+    for side, out_ref in enumerate((own_ref, other_ref)):
+        out_ref[...] = lax.dot_general(
+            x_ref[side * tokens : (side + 1) * tokens, :], held[...],
             (((1,), (1,)), ((), ())), preferred_element_type=F32,
         ).astype(BF16)
 
@@ -231,14 +245,14 @@
         out_shape=[like(tokens, CHUNK)]
         + [like(groups, GROUP, tokens)] * 2
         + [like(groups, chunks * GROUP, 128), like(groups, GROUP, 128), like(1, tokens)]
-        + [jax.ShapeDtypeStruct((width, tokens), BF16)],
+        + [jax.ShapeDtypeStruct((width, tokens), BF16), like(groups, GROUP, tokens)],
         cost_estimate=COST,
         name="prep",
     )(decay, starts, reads)
 
 
-def near_part(cots, writes, reads, gains, ready):
-    cols, cumr, openr, keep, whole, cntr, reads_t = ready
+def near_part(cots, writes, reads, gains, ready, states):
+    cols, cumr, openr, keep, whole, cntr, reads_t = ready[:7]
     heads = gains.shape[1]
     tokens, width = writes.shape
     size = cots[0].shape[1] // heads
@@ -264,15 +278,37 @@
         out_specs=[
             pl.BlockSpec((tokens, GROUP * size), columns2),
             pl.BlockSpec((GROUP, width + EXTRA, size), step3),
-        ],
+        ][: 1 + states],
         out_shape=[
             jax.ShapeDtypeStruct((tokens, heads * size), BF16),
             jax.ShapeDtypeStruct((heads, width + EXTRA, size), BF16),
-        ],
+        ][: 1 + states],
         scratch_shapes=[pltpu.VMEM((tokens, CHUNK), F32)],
         cost_estimate=COST,
         name="near",
     )(gains, writes, reads, reads_t, cntr, cols, cumr, openr, keep, whole, *cots)
+
+
+def states_part(cot, ready):
+    whole, reads_t, allr = ready[4], ready[6], ready[7]
+    groups, _, tokens = allr.shape
+    width = reads_t.shape[0]
+    heads = groups * GROUP
+    size = cot.shape[1] // heads
+    return pl.pallas_call(
+        states_kernel,
+        grid=(groups,),
+        in_specs=[
+            pl.BlockSpec((width, tokens), whole2),
+            pl.BlockSpec((1, GROUP, tokens), step3),
+            pl.BlockSpec((1, GROUP, 128), step3),
+            pl.BlockSpec((tokens, GROUP * size), columns2),
+        ],
+        out_specs=pl.BlockSpec((GROUP, width + EXTRA, size), step3),
+        out_shape=jax.ShapeDtypeStruct((heads, width + EXTRA, size), BF16),
+        cost_estimate=COST,
+        name="states",
+    )(reads_t, allr, whole, cot)
 
 
 def arrivals(m):
@@ -310,7 +346,7 @@
             + [pl.BlockSpec((GROUP, width, size), step3)] * 2
             + [pl.BlockSpec((rows, GROUP * size), columns2)]
             + [pl.BlockSpec(memory_space=pl.ANY)] * len(distinct),
-            out_specs=[pl.BlockSpec((2 * tokens, GROUP * size), columns2)]
+            out_specs=[pl.BlockSpec(memory_space=pltpu.VMEM)]
             + [pl.BlockSpec((tokens, count * rows), whole2)] * 2,
             scratch_shapes=[
                 pltpu.VMEM((2 * tokens, count * rows), F32),
@@ -318,8 +354,9 @@
                 pltpu.SemaphoreType.DMA((count - 1,)),
             ],
         ),
-        out_shape=[jax.ShapeDtypeStruct((2 * tokens, depth), BF16)]
+        out_shape=[pltpu.VMEM((2 * tokens, depth), BF16)]
         + [jax.ShapeDtypeStruct((tokens, count * rows), BF16)] * 2,
+        compiler_params=pltpu.CompilerParams(vmem_limit_bytes=36 << 20),
         cost_estimate=COST,
         name="main",
     )(slab.reshape(1), *near, *writes, *cols, *later, weight, *[blocks[p] for p in distinct])
@@ -331,16 +368,15 @@
     vmem = pl.BlockSpec(memory_space=pltpu.VMEM)
     return pl.pallas_call(
         functools.partial(product_kernel, which),
-        in_specs=[pl.BlockSpec(memory_space=pltpu.SMEM)]
-        + [pl.BlockSpec(memory_space=pl.ANY)] * (1 + len(distinct)),
+        in_specs=[pl.BlockSpec(memory_space=pltpu.SMEM), vmem]
+        + [pl.BlockSpec(memory_space=pl.ANY)] * len(distinct),
         out_specs=[vmem] * 2,
         scratch_shapes=[
             pltpu.VMEM((rows, depth), BF16),
-            pltpu.VMEM(x.shape, BF16),
             pltpu.SemaphoreType.DMA,
-            pltpu.SemaphoreType.DMA((x.shape[0] // TILE,)),
         ],
         out_shape=[jax.ShapeDtypeStruct((tokens, rows), BF16)] * 2,
+        compiler_params=pltpu.CompilerParams(vmem_limit_bytes=24 << 20),
         cost_estimate=COST,
         name="product",
     )(slab.reshape(1), x, *[blocks[p] for p in distinct])
@@ -421,16 +457,14 @@
         swap(x) for x in (writes, reads, decay, flight_starts)
     ]
     small = (writes_b, reads_b, decay_b, starts_b)
-    cots_b = [swap(gate(cot[:CHUNK], *small)), swap(cot[CHUNK:])]
-
     ready_a = prepared(reads, decay, flight_starts)
-    near_a, state_a = near_part(
-        [gate(cot, *small)], writes, reads, skip_gain, ready_a
-    )
+    state_a = states_part(cot, ready_a)
+    cot_b = swap(gate(cot, state_a))
+    (near_a,) = near_part([gate(cot, state_a)], writes, reads, skip_gain, ready_a, False)
     ready_b = prepared(reads_b, decay_b, starts_b)
     half = heads // 2
     leaving = lax.dynamic_slice_in_dim(state_a, (1 - side) * half, half, 0)
-    got = swap(gate(leaving, cots_b[0]))
+    got = swap(gate(leaving, *small))
     kept = lax.dynamic_slice_in_dim(state_a, side * half, half, 0)
     state_0, keep_0 = parts_of(jnp.where(first, kept, got), width)
     state_1, keep_1 = parts_of(jnp.where(first, got, kept), width)
@@ -439,14 +473,14 @@
     for at in reversed(range(1, m)):
         leaving = (slab_state + slab_keep * later.astype(F32)).astype(BF16)
         if at == m - 1:
-            leaving = gate(leaving, blocks[1, 1], blocks[-1, 1], ready_b[0])
+            leaving = gate(leaving, blocks[1, 1], blocks[-1, 1], ready_b[0], near_a)
         later = later + lax.ppermute(
             leaving, "seq", [(2 * at + y, 2 * at - 2 + y) for y in range(2)]
         )
     blocks[-1, m - 1] = lax.ppermute(gate(blocks[-1, m - 2], later), "seq", down(m - 1))
     other = swap(later)
-    cots_b[0] = gate(cots_b[0], later)
-    near_b, state_b = near_part(cots_b, writes_b, reads_b, skip_gain, ready_b)
+    cot_b = gate(cot_b, later)
+    near_b, state_b = near_part([cot_b], writes_b, reads_b, skip_gain, ready_b, True)
     last = jnp.where(first, jnp.stack([later, other]), jnp.stack([other, later]))
     last = last.reshape(heads, width, size)
     state_1, keep_1 = parts_of(jnp.where(first, state_b, state_a), width)

time: 215 us -> 206 us (0.958)
  waiting for transfers between devices: 89 us -> 85.3 us
  local copies, waits for them, and re-layouts: 10.1 us -> 7.2 us
    ppermute x8 -> x7, waiting for transfers between devices: 11.2 us -> 3.68 us  [swap(): return lax.ppermute(x, 'seq', pair)]
    pallas_call x0 -> x1, Pallas kernels: none -> 7.17 us  [states_part(): pl.pallas_call(states_kernel, grid=(groups,), in_specs=[pl.BlockSpec((wid...]
    slice x2 -> x0, local copies, waits for them, and re-layouts: 6.45 us -> none  [body(): cots_b = [swap(gate(cot[:CHUNK], *small)), swap(cot[CHUNK:])]]
    pallas_call x1, Pallas kernels: 8.03 us -> 2.52 us  [product(): pl.pallas_call(functools.partial(product_kernel, which), in_specs=[pl.Blo...]
    ppermute x3, waiting for transfers between devices: 7.79 us -> 2.42 us  [body(): lax.ppermute(blocks.get((1, k - 1), weight), 'seq', [(s, s + 2) for s in...]
    ppermute x4, waiting for transfers between devices: 11.6 us -> 16.9 us  [body(): pieces.append(lax.ppermute(got[flip], ('seq', 'pipe'), route))]
    ppermute x3, waiting for transfers between devices: 55.5 us -> 59.4 us  [body(): lax.ppermute(leaving, 'seq', [(2 * at + y, 2 * at - 2 + y) for y in range...]
    unnamed x19 -> x35, local copies, waits for them, and re-layouts: 1 us -> 4.66 us
  transfers between devices with their start and end apart: 21 -> 20, of which waited for: 9 -> 9; matrix products, arithmetic and copies ran while one was open for 8% -> 5% of each run, Pallas kernels for 31% -> 32%
where the time goes in v4:
time: 206 us; the launch traced here: 205 us
  waiting for transfers between devices  85.3 us (41%)
  Pallas kernels  67.8 us (33%)
  starting transfers between devices  36.6 us (18%)
  local copies, waits for them, and re-layouts  7.2 us (3%)
  other arithmetic  6.57 us (3%)
    ppermute x3, waiting for transfers between devices, body(): lax.ppermute(leaving, 'seq', [(2 * at + y, 2 * at - 2 + y) for y in range...  59.4 us
    pallas_call x2, Pallas kernels, near_part(): pl.pallas_call(functools.partial(near_kernel, chunks, heads, pieces), gri...  28.6 us
    pallas_call x1, Pallas kernels, main_part(): pl.pallas_call(functools.partial(main_kernel, whiches, heads), grid_spec=...  21 us
    ppermute x4, waiting for transfers between devices, body(): pieces.append(lax.ppermute(got[flip], ('seq', 'pipe'), route))  16.9 us
    ppermute x3, starting transfers between devices, body(): lax.ppermute(blocks.get((1, k - 1), weight), 'seq', [(s, s + 2) for s in...  8.55 us
    pallas_call x1, Pallas kernels, states_part(): pl.pallas_call(states_kernel, grid=(groups,), in_specs=[pl.BlockSpec((wid...  7.17 us
    ppermute x2, starting transfers between devices, body(): lax.ppermute(blocks.get((-1, k - 1), weight), 'seq', down(k))  6.7 us
    ppermute x4, starting transfers between devices, body(): pieces.append(lax.ppermute(got[flip], ('seq', 'pipe'), route))  6.68 us
  transfers between devices with their start and end apart: 20, of which 9 were waited for; matrix products, arithmetic and copies ran while one was open for 5% of the time, Pallas kernels for 32%

profile of v4, /device:TPU:9, one launch (start us, length us, event | category | flops | bytes accessed | tf_op | source)
XLA Modules:
  0.0 205.0 jit_solution(18270187763630592921)
XLA Ops:
  0.0 3.2 %collective-permute-start.6 = (bf16[256,4096]{1,0:T(8,128)(2,1)}, bf16[256,4096]{1,0:T(8,128)(2,1)}, u32[]{:S(2)}, u32[]{:S(2)}) collective-permute-start(bf16[256,4096]{1,0:T(8,128)(2,1)} %bitcast.21), channel_id=1, source_target_pairs={{0,8},{4,12},{8,16},{12,20},{16,24},{20,28},{1,9},{5,13},{9,17},{1... | collective-permute-start | bytes 6291464 | tf_op jit(solution)/shard_map/ppermute | solution.py:449
  3.2 3.4 %collective-permute-start.7 = (bf16[256,4096]{1,0:T(8,128)(2,1)}, bf16[256,4096]{1,0:T(8,128)(2,1)S(1)}, u32[]{:S(2)}, u32[]{:S(2)}) collective-permute-start(bf16[256,4096]{1,0:T(8,128)(2,1)} %bitcast.22), channel_id=1, source_target_pairs={{8,0},{12,4},{16,8},{20,12},{24,16},{28,20},{9,1},{13,5},{17,9},{2... | collective-permute-start | bytes 6291464 | tf_op jit(solution)/shard_map/ppermute | solution.py:454
  6.6 1.3 collective-permute-start
  8.1 1.2 collective-permute-start.3
  9.3 1.7 copy.10
  11.0 2.9 %prep.2 = (f32[512,128]{1,0:T(8,128)}, f32[8,4,512]{2,1,0:T(4,128)}, f32[8,4,512]{2,1,0:T(4,128)}, f32[8,16,128]{2,1,0:T(8,128)}, f32[8,4,128]{2,1,0:T(4,128)}, ...) custom-call(f32[512,32]{1,0:T(8,128)} %bitcast.30, s32[1,512]{1,0:T(1,128)} %starts_ref.1, ...), custom_call_target="tpu_custom_call" | custom-call | tf_op jit(solution)/shard_map/prep/pallas_call | solution.py:243
  14.0 7.2 %states.1 = bf16[32,144,128]{2,1,0:T(8,128)(2,1)} custom-call(bf16[128,512]{1,0:T(8,128)(2,1)} %get-tuple-element.32.readst_ref, f32[8,4,512]{2,1,0:T(4,128)} %get-tuple-element.39.allr_ref, f32[8,4,128]{2,1,0:T(4,128)} %get-tuple-element.38.whole_ref, bf16[512,4096]{1,0:T(8,128)(2,1)} %bitcast.27), custom_call_target="tpu_custom_call" | custom-call | tf_op jit(solution)/shard_map/states/pallas_call | solution.py:298
  21.1 0.3 collective-permute-start.2
  21.4 1.9 constant_dynamic-slice_fusion
  23.4 3.7 %collective-permute-done.2.decay_ref = f32[512,32]{1,0:T(8,128)S(1)} collective-permute-done((f32[512,32]{1,0:T(8,128)S(1)}, f32[512,32]{1,0:T(8,128)S(1)}, u32[]{:S(2)}, u32[]{:S(2)}) %collective-permute-start.2) | collective-permute-done | bytes 65568 | tf_op jit(solution)/shard_map/ppermute | solution.py:442
  27.1 0.3 collective-permute-start.5
  27.4 1.2 collective-permute-start.4
  28.6 13.3 %near.2.refs_0_ = bf16[512,4096]{1,0:T(8,128)(2,1)} custom-call(f32[1,32]{1,0:T(1,128)} %gain_ref.3, bf16[512,128]{1,0:T(8,128)(2,1)} %bitcast.25, bf16[512,128]{1,0:T(8,128)(2,1)} %bitcast.34, bf16[128,512]{1,0:T(8,128)(2,1)} %get-tuple-element.32.readst_ref, f32[1,512]{1,0:T(1,128)} %get-tuple-element.33.cntr_ref, ...), custom_call_target="tpu_custom_call" | custom-call | tf_op jit(solution)/shard_map/near/pallas_call | solution.py:262
  41.9 2.9 %prep.3 = (f32[512,128]{1,0:T(8,128)}, f32[8,4,512]{2,1,0:T(4,128)}, f32[8,4,512]{2,1,0:T(4,128)}, f32[8,16,128]{2,1,0:T(8,128)}, f32[8,4,128]{2,1,0:T(4,128)}, ...) custom-call(f32[512,32]{1,0:T(8,128)} %copy-done.14, s32[1,512]{1,0:T(1,128)} %copy-done.15, ...), custom_call_target="tpu_custom_call" | custom-call | tf_op jit(solution)/shard_map/prep/pallas_call | solution.py:243
  44.9 1.2 broadcast_select_fusion.2
  46.3 2.4 %collective-permute-done.6.refs_10_.refs_11_.refs_12_ = bf16[256,4096]{1,0:T(8,128)(2,1)} collective-permute-done((bf16[256,4096]{1,0:T(8,128)(2,1)}, bf16[256,4096]{1,0:T(8,128)(2,1)}, u32[]{:S(2)}, u32[]{:S(2)}) %collective-permute-start.6) | collective-permute-done | bytes 2097184 | tf_op jit(solution)/shard_map/ppermute | solution.py:449
  48.7 2.9 %collective-permute-done.7.refs_9_ = bf16[256,4096]{1,0:T(8,128)(2,1)S(1)} collective-permute-done((bf16[256,4096]{1,0:T(8,128)(2,1)}, bf16[256,4096]{1,0:T(8,128)(2,1)S(1)}, u32[]{:S(2)}, u32[]{:S(2)}) %collective-permute-start.7) | collective-permute-done | bytes 2097184 | tf_op jit(solution)/shard_map/ppermute | solution.py:454
  51.6 1.3 copy-done.3
  52.9 0.7 collective-permute-start.8
  53.6 3.3 %collective-permute-start.12 = (bf16[256,4096]{1,0:T(8,128)(2,1)}, bf16[256,4096]{1,0:T(8,128)(2,1)S(1)}, u32[]{:S(2)}, u32[]{:S(2)}) collective-permute-start(bf16[256,4096]{1,0:T(8,128)(2,1)} %copy-done.3), channel_id=1, source_target_pairs={{8,0},{12,4},{16,8},{20,12},{9,1},{13,5},{17,9},{21,13},{10,2},{14... | collective-permute-start | bytes 6291464 | tf_op jit(solution)/shard_map/ppermute | solution.py:454
  57.0 3.4 %collective-permute-start.13 = (bf16[256,4096]{1,0:T(8,128)(2,1)}, bf16[256,4096]{1,0:T(8,128)(2,1)}, u32[]{:S(2)}, u32[]{:S(2)}) collective-permute-start(bf16[256,4096]{1,0:T(8,128)(2,1)} %collective-permute-done.6.refs_10_.refs_11_.refs_12_), channel_id=1, source_target_pairs={{8,16},{12,20},{16,24},{20,28},{9,17},{13,21},{17,25},{21,29},{10,... | collective-permute-start | bytes 6291464 | tf_op jit(solution)/shard_map/ppermute | solution.py:449
  60.3 0.3 add_convert_fusion.2
  60.6 1.3 collective-permute-start.9
  61.9 50.5 %collective-permute-done.9 = bf16[16,128,128]{2,1,0:T(8,128)(2,1)S(1)} collective-permute-done((bf16[16,128,128]{2,1,0:T(8,128)(2,1)S(1)}, bf16[16,128,128]{2,1,0:T(8,128)(2,1)S(1)}, u32[]{:S(2)}, u32[]{:S(2)}) %collective-permute-start.9) | collective-permute-done | bytes 524320 | tf_op jit(solution)/shard_map/ppermute | solution.py:477
  112.4 0.4 add_convert_fusion.1
  112.8 1.3 collective-permute-start.10
  114.2 8.9 %collective-permute-done.10 = bf16[16,128,128]{2,1,0:T(8,128)(2,1)S(1)} collective-permute-done((bf16[16,128,128]{2,1,0:T(8,128)(2,1)S(1)}, bf16[16,128,128]{2,1,0:T(8,128)(2,1)S(1)}, u32[]{:S(2)}, u32[]{:S(2)}) %collective-permute-start.10) | collective-permute-done | bytes 524320 | tf_op jit(solution)/shard_map/ppermute | solution.py:477
  123.0 1.0 add.96
  124.0 5.6 %collective-permute-start.16 = (bf16[256,4096]{1,0:T(8,128)(2,1)S(1)}, bf16[256,4096]{1,0:T(8,128)(2,1)}, u32[]{:S(2)}, u32[]{:S(2)}) collective-permute-start(bf16[256,4096]{1,0:T(8,128)(2,1)S(1)} %collective-permute-done.12.refs_13_.refs_1_), channel_id=1, source_target_pairs={{8,0},{12,4},{9,1},{13,5},{10,2},{14,6},{11,3},{15,7}} | collective-permute-start | bytes 6291464 | tf_op jit(solution)/shard_map/ppermute | solution.py:480
  129.6 2.0 collective-permute-start.17
  131.6 1.2 collective-permute-start.11
  132.8 15.2 %near.3 = (bf16[512,4096]{1,0:T(8,128)(2,1)}, bf16[32,144,128]{2,1,0:T(8,128)(2,1)}) custom-call(f32[1,32]{1,0:T(1,128)} %gain_ref.3, bf16[512,128]{1,0:T(8,128)(2,1)} %copy-done.7, bf16[512,128]{1,0:T(8,128)(2,1)} %copy-done.13, bf16[128,512]{1,0:T(8,128)(2,1)} %get-tuple-element.41.readst_ref, f32[1,512]{1,0:T(1,128)} %get-tuple-element.42.cntr_ref, ...), custom_call_target="tpu_custom_call" | custom-call | tf_op jit(solution)/shard_map/near/pallas_call | solution.py:262
  148.1 1.8 maximum_select_fusion
  150.1 0.8 fusion
  151.0 0.8 copy-done.2
  151.8 0.6 copy-done.4
  152.5 21.0 %main.1 = (bf16[1024,4096]{1,0:T(8,128)(2,1)S(1)}, bf16[512,768]{1,0:T(8,128)(2,1)}, bf16[512,768]{1,0:T(8,128)(2,1)}) custom-call(s32[1]{0:T(128)} %bitcast.5.slab_ref, bf16[512,4096]{1,0:T(8,128)(2,1)} %near.2.refs_0_, bf16[512,4096]{1,0:T(8,128)(2,1)} %get-tuple-element.51.refs_1_, bf16[512,128]{1,0:T(8,128)(2,1)S(1)} %bitcast.26, ...), custom_call_target="tpu_custom_call" | custom-call | tf_op jit(solution)/shard_map/main/pallas_call | solution.py:338
  173.4 3.7 %collective-permute-start.14 = (bf16[512,768]{1,0:T(8,128)(2,1)}, bf16[512,768]{1,0:T(8,128)(2,1)S(1)}, u32[]{:S(2)}, u32[]{:S(2)}) collective-permute-start(bf16[512,768]{1,0:T(8,128)(2,1)} %get-tuple-element.53), channel_id=1, source_target_pairs={{0,3},{1,0},{2,1},{3,2},{4,7},{5,4},{6,5},{7,6},{8,11},{9,8},{10,9... | collective-permute-start | bytes 2359304 | tf_op jit(solution)/shard_map/ppermute | solution.py:512
  177.4 2.5 %product.1 = (bf16[512,256]{1,0:T(8,128)(2,1)S(1)}, bf16[512,256]{1,0:T(8,128)(2,1)S(1)}) custom-call(s32[1]{0:T(128)} %bitcast.5.slab_ref, bf16[1024,4096]{1,0:T(8,128)(2,1)S(1)} %get-tuple-element.55.x_ref, bf16[256,4096]{1,0:T(8,128)(2,1)} %collective-permute-done.16.refs_0_, bf16[256,4096]{1,0:T(8,128)(2,1)S(1)} %copy-done.1, ...), custom_call_target="tpu_custom_call" | custom-call | tf_op jit(solution)/shard_map/product/pallas_call | solution.py:369
  179.9 1.4 collective-permute-start.18
  181.3 1.4 collective-permute-start.19
  182.7 0.6 constant_dynamic-slice_fusion.1
  184.5 0.7 add_bitcast_fusion.1
  185.3 3.3 %collective-permute-done.14.refs_0_ = bf16[512,768]{1,0:T(8,128)(2,1)S(1)} collective-permute-done((bf16[512,768]{1,0:T(8,128)(2,1)}, bf16[512,768]{1,0:T(8,128)(2,1)S(1)}, u32[]{:S(2)}, u32[]{:S(2)}) %collective-permute-start.14) | collective-permute-done | bytes 786464 | tf_op jit(solution)/shard_map/ppermute | solution.py:512
  188.5 8.2 %collective-permute-done.15.refs_1_ = bf16[512,768]{1,0:T(8,128)(2,1)} collective-permute-done((bf16[512,768]{1,0:T(8,128)(2,1)}, bf16[512,768]{1,0:T(8,128)(2,1)}, u32[]{:S(2)}, u32[]{:S(2)}) %collective-permute-start.15) | collective-permute-done | bytes 786464 | tf_op jit(solution)/shard_map/ppermute | solution.py:512
  196.7 3.0 %collective-permute-done.18.refs_2_ = bf16[512,256]{1,0:T(8,128)(2,1)S(1)} collective-permute-done((bf16[512,256]{1,0:T(8,128)(2,1)S(1)}, bf16[512,256]{1,0:T(8,128)(2,1)S(1)}, u32[]{:S(2)}, u32[]{:S(2)}) %collective-permute-start.18) | collective-permute-done | bytes 262176 | tf_op jit(solution)/shard_map/ppermute | solution.py:512
  199.7 2.5 %collective-permute-done.19.refs_3_ = bf16[512,256]{1,0:T(8,128)(2,1)S(1)} collective-permute-done((bf16[512,256]{1,0:T(8,128)(2,1)S(1)}, bf16[512,256]{1,0:T(8,128)(2,1)S(1)}, u32[]{:S(2)}, u32[]{:S(2)}) %collective-permute-start.19) | collective-permute-done | bytes 262176 | tf_op jit(solution)/shard_map/ppermute | solution.py:512
  202.2 2.7 %assemble.1 = bf16[1,512,2048]{2,1,0:T(8,128)(2,1)} custom-call(s32[8]{0:T(128)S(1)} %pad_add_fusion.columns_ref, bf16[512,768]{1,0:T(8,128)(2,1)S(1)} %collective-permute-done.14.refs_0_, bf16[512,768]{1,0:T(8,128)(2,1)} %collective-permute-done.15.refs_1_, bf16[512,256]{1,0:T(8,128)(2,1)S(1)} %collective-permute-done.18.refs_2_, ...), custom_call_target="tpu_custom_call" | custom-call | tf_op jit(solution)/shard_map/assemble/pallas_call | solution.py:409
  (50 shorter events, 1.2 us)
Async XLA Ops:
  0.0 48.7 %collective-permute-start.6 = (bf16[256,4096]{1,0:T(8,128)(2,1)}, bf16[256,4096]{1,0:T(8,128)(2,1)}, u32[]{:S(2)}, u32[]{:S(2)}) collective-permute-start(bf16[256,4096]{1,0:T(8,128)(2,1)} %bitcast.21), channel_id=1, source_target_pairs={{0,8},{4,12},{8,16},{12,20},{16,24},{20,28},{1,9},{5,13},{9,17},{1... | collective-permute-start | bytes 6291464 | tf_op jit(solution)/shard_map/ppermute | solution.py:449
  3.2 48.4 %collective-permute-start.7 = (bf16[256,4096]{1,0:T(8,128)(2,1)}, bf16[256,4096]{1,0:T(8,128)(2,1)S(1)}, u32[]{:S(2)}, u32[]{:S(2)}) collective-permute-start(bf16[256,4096]{1,0:T(8,128)(2,1)} %bitcast.22), channel_id=1, source_target_pairs={{8,0},{12,4},{16,8},{20,12},{24,16},{28,20},{9,1},{13,5},{17,9},{2... | collective-permute-start | bytes 6291464 | tf_op jit(solution)/shard_map/ppermute | solution.py:454
  6.6 20.5 %collective-permute-start = (bf16[512,128]{1,0:T(8,128)(2,1)}, bf16[512,128]{1,0:T(8,128)(2,1)S(1)}, u32[]{:S(2)}, u32[]{:S(2)}) collective-permute-start(bf16[512,128]{1,0:T(8,128)(2,1)} %bitcast.24), channel_id=1, source_target_pairs={{0,4},{4,0},{8,12},{12,8},{16,20},{20,16},{24,28},{28,24},{1,5},{5... | collective-permute-start | bytes 393224 | tf_op jit(solution)/shard_map/ppermute | solution.py:442
  7.9 19.2 %collective-permute-start.1 = (bf16[512,128]{1,0:T(8,128)(2,1)}, bf16[512,128]{1,0:T(8,128)(2,1)S(1)}, u32[]{:S(2)}, u32[]{:S(2)}) collective-permute-start(bf16[512,128]{1,0:T(8,128)(2,1)} %bitcast.32), channel_id=1, source_target_pairs={{0,4},{4,0},{8,12},{12,8},{16,20},{20,16},{24,28},{28,24},{1,5},{5... | collective-permute-start | bytes 393224 | tf_op jit(solution)/shard_map/ppermute | solution.py:442
  8.1 13.0 %collective-permute-start.3 = (s32[1,512]{1,0:T(1,128)}, s32[1,512]{1,0:T(1,128)S(1)}, u32[]{:S(2)}, u32[]{:S(2)}) collective-permute-start(s32[1,512]{1,0:T(1,128)} %starts_ref.1), channel_id=1, source_target_pairs={{0,4},{4,0},{8,12},{12,8},{16,20},{20,16},{24,28},{28,24},{1,5},{5... | collective-permute-start | bytes 6152 | tf_op jit(solution)/shard_map/ppermute | solution.py:442
  14.0 7.2 %copy-start.12 = (f32[1,512,32]{2,1,0:T(8,128)S(1)}, f32[1,512,32]{2,1,0:T(8,128)}, u32[]{:S(2)}) copy-start(f32[1,512,32]{2,1,0:T(8,128)} %copy.10) | copy-start | bytes 196612
  21.1 20.8 %copy-start.15 = (s32[1,512]{1,0:T(1,128)}, s32[1,512]{1,0:T(1,128)S(1)}, u32[]{:S(2)}) copy-start(s32[1,512]{1,0:T(1,128)S(1)} %collective-permute-done.3.starts_ref) | copy-start | bytes 6148
  21.1 5.9 %collective-permute-start.2 = (f32[512,32]{1,0:T(8,128)S(1)}, f32[512,32]{1,0:T(8,128)S(1)}, u32[]{:S(2)}, u32[]{:S(2)}) collective-permute-start(f32[512,32]{1,0:T(8,128)S(1)} %bitcast.31), channel_id=1, source_target_pairs={{0,4},{4,0},{8,12},{12,8},{16,20},{20,16},{24,28},{28,24},{1,5},{5... | collective-permute-start | bytes 196616 | tf_op jit(solution)/shard_map/ppermute | solution.py:442
  27.0 1.6 copy-start.14
  27.0 14.9 %copy-start.7 = (bf16[512,128]{1,0:T(8,128)(2,1)}, bf16[512,128]{1,0:T(8,128)(2,1)S(1)}, u32[]{:S(2)}) copy-start(bf16[512,128]{1,0:T(8,128)(2,1)S(1)} %collective-permute-done.writes_ref.refs_3_) | copy-start | bytes 393220
  27.0 14.9 %copy-start.13 = (bf16[512,128]{1,0:T(8,128)(2,1)}, bf16[512,128]{1,0:T(8,128)(2,1)S(1)}, u32[]{:S(2)}) copy-start(bf16[512,128]{1,0:T(8,128)(2,1)S(1)} %collective-permute-done.1.reads_ref) | copy-start | bytes 393220
  27.1 17.8 %collective-permute-start.5 = (bf16[16,144,128]{2,1,0:T(8,128)(2,1)}, bf16[16,144,128]{2,1,0:T(8,128)(2,1)}, u32[]{:S(2)}, u32[]{:S(2)}) collective-permute-start(bf16[16,144,128]{2,1,0:T(8,128)(2,1)} %constant_dynamic-slice_fusion), channel_id=1, source_target_pairs={{0,4},{4,0},{8,12},{12,8},{16,20},{20,16},{24,28},{28,24},{1,5},{5... | collective-permute-start | bytes 1769480 | tf_op jit(solution)/shard_map/ppermute | solution.py:442
  27.4 105.5 %collective-permute-start.4 = (bf16[512,4096]{1,0:T(8,128)(2,1)}, bf16[512,4096]{1,0:T(8,128)(2,1)}, u32[]{:S(2)}, u32[]{:S(2)}) collective-permute-start(bf16[512,4096]{1,0:T(8,128)(2,1)} %bitcast.28), channel_id=1, source_target_pairs={{0,4},{4,0},{8,12},{12,8},{16,20},{20,16},{24,28},{28,24},{1,5},{5... | collective-permute-start | bytes 12582920 | tf_op jit(solution)/shard_map/ppermute | solution.py:442
  28.6 16.3 %copy-start.10 = (bf16[32,144,128]{2,1,0:T(8,128)(2,1)S(1)}, bf16[32,144,128]{2,1,0:T(8,128)(2,1)}, u32[]{:S(2)}) copy-start(bf16[32,144,128]{2,1,0:T(8,128)(2,1)} %states.1) | copy-start | bytes 3538948
  51.6 1.3 copy-start.3
  52.9 7.4 %collective-permute-start.8 = (bf16[16,128,128]{2,1,0:T(8,128)(2,1)S(1)}, bf16[16,128,128]{2,1,0:T(8,128)(2,1)S(1)}, u32[]{:S(2)}, u32[]{:S(2)}) collective-permute-start(bf16[16,128,128]{2,1,0:T(8,128)(2,1)S(1)} %add_convert_fusion.3), channel_id=1, source_target_pairs={{24,16},{28,20},{25,17},{29,21},{26,18},{30,22},{27,19},{31,23}} | collective-permute-start | bytes 1572872 | tf_op jit(solution)/shard_map/ppermute | solution.py:477
  53.6 70.4 %collective-permute-start.12 = (bf16[256,4096]{1,0:T(8,128)(2,1)}, bf16[256,4096]{1,0:T(8,128)(2,1)S(1)}, u32[]{:S(2)}, u32[]{:S(2)}) collective-permute-start(bf16[256,4096]{1,0:T(8,128)(2,1)} %copy-done.3), channel_id=1, source_target_pairs={{8,0},{12,4},{16,8},{20,12},{9,1},{13,5},{17,9},{21,13},{10,2},{14... | collective-permute-start | bytes 6291464 | tf_op jit(solution)/shard_map/ppermute | solution.py:454
  57.0 72.6 %collective-permute-start.13 = (bf16[256,4096]{1,0:T(8,128)(2,1)}, bf16[256,4096]{1,0:T(8,128)(2,1)}, u32[]{:S(2)}, u32[]{:S(2)}) collective-permute-start(bf16[256,4096]{1,0:T(8,128)(2,1)} %collective-permute-done.6.refs_10_.refs_11_.refs_12_), channel_id=1, source_target_pairs={{8,16},{12,20},{16,24},{20,28},{9,17},{13,21},{17,25},{21,29},{10,... | collective-permute-start | bytes 6291464 | tf_op jit(solution)/shard_map/ppermute | solution.py:449
  60.6 51.8 %collective-permute-start.9 = (bf16[16,128,128]{2,1,0:T(8,128)(2,1)S(1)}, bf16[16,128,128]{2,1,0:T(8,128)(2,1)S(1)}, u32[]{:S(2)}, u32[]{:S(2)}) collective-permute-start(bf16[16,128,128]{2,1,0:T(8,128)(2,1)S(1)} %add_convert_fusion.2), channel_id=1, source_target_pairs={{16,8},{20,12},{17,9},{21,13},{18,10},{22,14},{19,11},{23,15}} | collective-permute-start | bytes 1572872 | tf_op jit(solution)/shard_map/ppermute | solution.py:477
  112.8 10.2 %collective-permute-start.10 = (bf16[16,128,128]{2,1,0:T(8,128)(2,1)S(1)}, bf16[16,128,128]{2,1,0:T(8,128)(2,1)S(1)}, u32[]{:S(2)}, u32[]{:S(2)}) collective-permute-start(bf16[16,128,128]{2,1,0:T(8,128)(2,1)S(1)} %get-tuple-element.59), channel_id=1, source_target_pairs={{8,0},{12,4},{9,1},{13,5},{10,2},{14,6},{11,3},{15,7}} | collective-permute-start | bytes 1572872 | tf_op jit(solution)/shard_map/ppermute | solution.py:477
  124.0 24.0 %copy-start = (bf16[256,4096]{1,0:T(8,128)(2,1)}, bf16[256,4096]{1,0:T(8,128)(2,1)S(1)}, u32[]{:S(2)}) copy-start(bf16[256,4096]{1,0:T(8,128)(2,1)S(1)} %collective-permute-done.12.refs_13_.refs_1_) | copy-start | bytes 6291460
  124.0 53.3 %collective-permute-start.16 = (bf16[256,4096]{1,0:T(8,128)(2,1)S(1)}, bf16[256,4096]{1,0:T(8,128)(2,1)}, u32[]{:S(2)}, u32[]{:S(2)}) collective-permute-start(bf16[256,4096]{1,0:T(8,128)(2,1)S(1)} %collective-permute-done.12.refs_13_.refs_1_), channel_id=1, source_target_pairs={{8,0},{12,4},{9,1},{13,5},{10,2},{14,6},{11,3},{15,7}} | collective-permute-start | bytes 6291464 | tf_op jit(solution)/shard_map/ppermute | solution.py:480
  129.6 47.8 %collective-permute-start.17 = (bf16[256,4096]{1,0:T(8,128)(2,1)}, bf16[256,4096]{1,0:T(8,128)(2,1)}, u32[]{:S(2)}, u32[]{:S(2)}) collective-permute-start(bf16[256,4096]{1,0:T(8,128)(2,1)} %collective-permute-done.13.refs_14_.refs_2_), channel_id=1, source_target_pairs={{16,24},{20,28},{17,25},{21,29},{18,26},{22,30},{19,27},{23,31}} | collective-permute-start | bytes 6291464 | tf_op jit(solution)/shard_map/ppermute | solution.py:449
  131.6 16.5 %collective-permute-start.11 = (bf16[16,128,128]{2,1,0:T(8,128)(2,1)}, bf16[16,128,128]{2,1,0:T(8,128)(2,1)}, u32[]{:S(2)}, u32[]{:S(2)}) collective-permute-start(bf16[16,128,128]{2,1,0:T(8,128)(2,1)} %add.96), channel_id=1, source_target_pairs={{0,4},{4,0},{8,12},{12,8},{16,20},{20,16},{24,28},{28,24},{1,5},{5... | collective-permute-start | bytes 1572872 | tf_op jit(solution)/shard_map/ppermute | solution.py:442
  148.0 1.9 copy-start.11
  149.9 1.0 copy-start.5
  150.0 1.0 copy-start.6
  150.0 1.1 copy-start.8
  150.0 1.1 copy-start.9
  150.1 1.7 copy-start.2
  150.1 2.3 %copy-start.4 = (bf16[256,4096]{1,0:T(8,128)(2,1)S(1)}, bf16[256,4096]{1,0:T(8,128)(2,1)}, u32[]{:S(2)}) copy-start(bf16[256,4096]{1,0:T(8,128)(2,1)} %copy-done.3) | copy-start | bytes 6291460
  152.5 24.9 %copy-start.1 = (bf16[256,4096]{1,0:T(8,128)(2,1)S(1)}, bf16[256,4096]{1,0:T(8,128)(2,1)}, u32[]{:S(2)}) copy-start(bf16[256,4096]{1,0:T(8,128)(2,1)} %copy-done) | copy-start | bytes 6291460
  173.4 15.1 %collective-permute-start.14 = (bf16[512,768]{1,0:T(8,128)(2,1)}, bf16[512,768]{1,0:T(8,128)(2,1)S(1)}, u32[]{:S(2)}, u32[]{:S(2)}) collective-permute-start(bf16[512,768]{1,0:T(8,128)(2,1)} %get-tuple-element.53), channel_id=1, source_target_pairs={{0,3},{1,0},{2,1},{3,2},{4,7},{5,4},{6,5},{7,6},{8,11},{9,8},{10,9... | collective-permute-start | bytes 2359304 | tf_op jit(solution)/shard_map/ppermute | solution.py:512
  177.2 19.6 %collective-permute-start.15 = (bf16[512,768]{1,0:T(8,128)(2,1)}, bf16[512,768]{1,0:T(8,128)(2,1)}, u32[]{:S(2)}, u32[]{:S(2)}) collective-permute-start(bf16[512,768]{1,0:T(8,128)(2,1)} %get-tuple-element.54), channel_id=1, source_target_pairs={{0,7},{1,4},{2,5},{3,6},{4,3},{5,0},{6,1},{7,2},{8,15},{9,12},{10,... | collective-permute-start | bytes 2359304 | tf_op jit(solution)/shard_map/ppermute | solution.py:512
  177.4 5.3 %copy-start.16 = (s32[1,4]{1,0:T(1,128)S(1)}, s32[1,4]{1,0:T(1,128)}, u32[]{:S(2)}) copy-start(s32[1,4]{1,0:T(1,128)} %constant.46.clone) | copy-start | bytes 52
  179.9 19.8 %collective-permute-start.18 = (bf16[512,256]{1,0:T(8,128)(2,1)S(1)}, bf16[512,256]{1,0:T(8,128)(2,1)S(1)}, u32[]{:S(2)}, u32[]{:S(2)}) collective-permute-start(bf16[512,256]{1,0:T(8,128)(2,1)S(1)} %get-tuple-element.57), channel_id=1, source_target_pairs={{0,3},{1,0},{2,1},{3,2},{4,7},{5,4},{6,5},{7,6},{8,11},{9,8},{10,9... | collective-permute-start | bytes 786440 | tf_op jit(solution)/shard_map/ppermute | solution.py:512
  181.3 20.9 %collective-permute-start.19 = (bf16[512,256]{1,0:T(8,128)(2,1)S(1)}, bf16[512,256]{1,0:T(8,128)(2,1)S(1)}, u32[]{:S(2)}, u32[]{:S(2)}) collective-permute-start(bf16[512,256]{1,0:T(8,128)(2,1)S(1)} %get-tuple-element.58), channel_id=1, source_target_pairs={{0,7},{1,4},{2,5},{3,6},{4,3},{5,0},{6,1},{7,2},{8,15},{9,12},{10,... | collective-permute-start | bytes 786440 | tf_op jit(solution)/shard_map/ppermute | solution.py:512

commit v5 on v4

--- a/solution.py
+++ b/solution.py
@@ -10,7 +10,6 @@
 CHUNK = 128
 GROUP = 4
 EXTRA = 16
-SLOTS = 3
 BF16 = jnp.bfloat16
 F32 = jnp.float32
 COST = pl.CostEstimate(flops=0, bytes_accessed=0, transcendentals=0)
@@ -24,7 +23,7 @@
 
 
 def prep_kernel(
-    chunks, heads, decay_ref, starts_ref, reads_ref,
+    chunks, heads, ext_ref, reads_ref,
     cols_ref, cumr_ref, openr_ref, keep_ref, whole_ref, cntr_ref, readst_ref, allr_ref,
 ):
     groups = heads // GROUP
@@ -34,11 +33,7 @@
     kept = []
     for c in reversed(range(chunks)):
         at = slice(c * CHUNK, (c + 1) * CHUNK)
-        decay = jnp.concatenate(
-            [decay_ref[at, :], jnp.zeros((CHUNK, CHUNK - heads), F32)], axis=1
-        ).T[:heads]
-        starts = jnp.broadcast_to(starts_ref[:, at].astype(F32), (8, CHUNK))
-        cum = jnp.concatenate([decay, starts], axis=0)
+        cum = ext_ref[:, at]
         shift = 1
         while shift < CHUNK:
             cum = cum + jnp.where(col >= shift, pltpu.roll(cum, shift, axis=1), 0.0)
@@ -162,21 +157,10 @@
                 pltpu.make_async_copy(block, held, sem).start()
 
 
-def main_kernel(whiches, heads, slab_ref, *refs):
-    near, writes, cols, later, refs = refs[0:2], refs[2:4], refs[4:6], refs[6:8], refs[8:]
-    weight_ref, refs = refs[0], refs[1:]
-    blocks, (x_ref, own_ref, other_ref, acc_ref, held, sems) = refs[:-6], refs[-6:]
+def far_kernel(heads, *refs):
+    near, writes, cols, later, x_ref = refs[0:2], refs[2:4], refs[4:6], refs[6:8], refs[8]
     tokens, step_width = near[0].shape
-    rows = weight_ref.shape[0]
-    step, steps = pl.program_id(0), pl.num_programs(0)
-
-    @pl.when(step == 0)
-    def _():
-        acc_ref[...] = jnp.zeros_like(acc_ref)
-        for i, which in enumerate(whiches):
-            fetch(slab_ref, which, blocks, held.at[i], sems.at[i])
-
-    depth = pl.ds(pl.multiple_of(step * step_width, step_width), step_width)
+    step = pl.program_id(0)
     for side in range(2):
         reach = turned(cols[side], 2 * heads + 8)
         for j in range(GROUP):
@@ -185,22 +169,6 @@
             far = jnp.dot(writes[side][...], later[side][j], preferred_element_type=F32)
             total = near[side][:, lane].astype(F32) + reach[:, j : j + 1] * far
             x_ref[side * tokens : (side + 1) * tokens, at] = total.astype(BF16)
-
-    @pl.when(step == 0)
-    def _():
-        for i in range(len(whiches)):
-            pltpu.make_async_copy(blocks[0], held.at[i], sems.at[i]).wait()
-
-    for i in range(len(whiches) + 1):
-        block = weight_ref[...] if i == 0 else held[i - 1, :, depth]
-        acc_ref[:, i * rows : (i + 1) * rows] += lax.dot_general(
-            x_ref[:, depth], block, (((1,), (1,)), ((), ())), preferred_element_type=F32
-        )
-
-    @pl.when(step == steps - 1)
-    def _():
-        own_ref[...] = acc_ref[:tokens].astype(BF16)
-        other_ref[...] = acc_ref[tokens:].astype(BF16)
 
 
 def product_kernel(which, slab_ref, x_ref, *refs):
@@ -231,9 +199,9 @@
     return (0, g)
 
 
-def prepared(reads, decay, starts):
-    tokens, heads = decay.shape
-    width = reads.shape[1]
+def prepared(reads, ext):
+    heads = ext.shape[0] - 8
+    tokens, width = reads.shape
     chunks = tokens // CHUNK
     groups = heads // GROUP
 
@@ -248,7 +216,7 @@
         + [jax.ShapeDtypeStruct((width, tokens), BF16), like(groups, GROUP, tokens)],
         cost_estimate=COST,
         name="prep",
-    )(decay, starts, reads)
+    )(ext, reads)
 
 
 def near_part(cots, writes, reads, gains, ready, states):
@@ -328,38 +296,23 @@
     return distinct, [[distinct.index(p) for p in picks] for picks in slots]
 
 
-def main_part(near, writes, cols, later, weight, blocks, slots, slab, heads):
+def far_part(near, writes, cols, later, heads):
     tokens, width = writes[0].shape
-    rows, depth = weight.shape
+    depth = near[0].shape[1]
     size = depth // heads
-    count = len(slots) + 1
-    distinct, whiches = indexed(slots)
-    block2 = pl.BlockSpec((tokens, GROUP * size), columns2)
-    return pl.pallas_call(
-        functools.partial(main_kernel, whiches, heads),
-        grid_spec=pltpu.PrefetchScalarGridSpec(
-            num_scalar_prefetch=1,
-            grid=(heads // GROUP,),
-            in_specs=[block2] * 2
-            + [pl.BlockSpec((tokens, width), whole2)] * 2
-            + [pl.BlockSpec((tokens, CHUNK), whole2)] * 2
-            + [pl.BlockSpec((GROUP, width, size), step3)] * 2
-            + [pl.BlockSpec((rows, GROUP * size), columns2)]
-            + [pl.BlockSpec(memory_space=pl.ANY)] * len(distinct),
-            out_specs=[pl.BlockSpec(memory_space=pltpu.VMEM)]
-            + [pl.BlockSpec((tokens, count * rows), whole2)] * 2,
-            scratch_shapes=[
-                pltpu.VMEM((2 * tokens, count * rows), F32),
-                pltpu.VMEM((count - 1, rows, depth), BF16),
-                pltpu.SemaphoreType.DMA((count - 1,)),
-            ],
-        ),
-        out_shape=[pltpu.VMEM((2 * tokens, depth), BF16)]
-        + [jax.ShapeDtypeStruct((tokens, count * rows), BF16)] * 2,
+    return pl.pallas_call(
+        functools.partial(far_kernel, heads),
+        grid=(heads // GROUP,),
+        in_specs=[pl.BlockSpec((tokens, GROUP * size), columns2)] * 2
+        + [pl.BlockSpec((tokens, width), whole2)] * 2
+        + [pl.BlockSpec((tokens, CHUNK), whole2)] * 2
+        + [pl.BlockSpec((GROUP, width, size), step3)] * 2,
+        out_specs=pl.BlockSpec(memory_space=pltpu.VMEM),
+        out_shape=pltpu.VMEM((2 * tokens, depth), BF16),
         compiler_params=pltpu.CompilerParams(vmem_limit_bytes=36 << 20),
         cost_estimate=COST,
-        name="main",
-    )(slab.reshape(1), *near, *writes, *cols, *later, weight, *[blocks[p] for p in distinct])
+        name="far",
+    )(*near, *writes, *cols, *later)
 
 
 def product(x, blocks, picks, slab, tokens):
@@ -382,18 +335,18 @@
     )(slab.reshape(1), x, *[blocks[p] for p in distinct])
 
 
-def assemble_kernel(counts, columns_ref, *refs):
+def assemble_kernel(counts, mine_ref, columns_ref, *refs):
     pieces, out_ref = refs[:-1], refs[-1]
     rows = pieces[0].shape[1] // counts[0]
     at = 0
     for piece, count in zip(pieces, counts):
         for i in range(count):
-            column = pl.multiple_of(columns_ref[at] * rows, rows)
+            column = pl.multiple_of(columns_ref[mine_ref[0], at] * rows, rows)
             out_ref[0, :, pl.ds(column, rows)] = piece[:, i * rows : (i + 1) * rows]
             at += 1
 
 
-def assembled(pieces, columns, rows):
+def assembled(pieces, columns, mine, rows):
     counts = [piece.shape[1] // rows for piece in pieces]
     if rows % 128:
         result = jnp.zeros((1, pieces[0].shape[0], sum(counts) * rows), BF16)
@@ -401,20 +354,20 @@
         for piece, count in zip(pieces, counts):
             for i in range(count):
                 result = lax.dynamic_update_slice(
-                    result, piece[None, :, i * rows : (i + 1) * rows], (0, 0, columns[at] * rows)
+                    result, piece[None, :, i * rows : (i + 1) * rows], (0, 0, columns[mine, at] * rows)
                 )
                 at += 1
         return result
     vmem = pl.BlockSpec(memory_space=pltpu.VMEM)
     return pl.pallas_call(
         functools.partial(assemble_kernel, counts),
-        in_specs=[pl.BlockSpec(memory_space=pltpu.SMEM)] + [vmem] * len(pieces),
+        in_specs=[pl.BlockSpec(memory_space=pltpu.SMEM)] * 2 + [vmem] * len(pieces),
         out_specs=vmem,
         out_shape=jax.ShapeDtypeStruct((1, pieces[0].shape[0], sum(counts) * rows), BF16),
         compiler_params=pltpu.CompilerParams(vmem_limit_bytes=32 << 20),
         cost_estimate=COST,
         name="assemble",
-    )(columns, *pieces)
+    )(mine.reshape(1), columns, *pieces)
 
 
 def parts_of(packed, width):
@@ -453,15 +406,14 @@
         if k < m - 1:
             blocks[-1, k] = lax.ppermute(blocks.get((-1, k - 1), weight), "seq", down(k))
 
-    writes_b, reads_b, decay_b, starts_b = [
-        swap(x) for x in (writes, reads, decay, flight_starts)
-    ]
-    small = (writes_b, reads_b, decay_b, starts_b)
-    ready_a = prepared(reads, decay, flight_starts)
+    starts = jnp.broadcast_to(flight_starts.astype(F32), (8, tokens))
+    ext = jnp.concatenate([decay.T, starts], axis=0)
+    small = writes_b, reads_b, ext_b = [swap(x) for x in (writes, reads, ext)]
+    ready_a = prepared(reads, ext)
     state_a = states_part(cot, ready_a)
     cot_b = swap(gate(cot, state_a))
     (near_a,) = near_part([gate(cot, state_a)], writes, reads, skip_gain, ready_a, False)
-    ready_b = prepared(reads_b, decay_b, starts_b)
+    ready_b = prepared(reads_b, ext_b)
     half = heads // 2
     leaving = lax.dynamic_slice_in_dim(state_a, (1 - side) * half, half, 0)
     got = swap(gate(leaving, *small))
@@ -490,28 +442,23 @@
 
     plan = arrivals(m)
     slots = [[plan[q][slot] for q in range(m)] for slot in range(m)]
-    count = min(m - 1, SLOTS)
-    x, own, swapped = main_part(
-        (near_a, near_b), (writes, writes_b), (ready_a[0], ready_b[0]), (later_a, later_b),
-        weight, blocks, slots[1:count], slab, heads,
+    x = far_part(
+        (near_a, near_b), (writes, writes_b), (ready_a[0], ready_b[0]), (later_a, later_b), heads
     )
-    todo = [(slots[:count], (own, swapped))]
-    for slot in range(count, m):
-        todo.append(([slots[slot]], product(x, blocks, slots[slot], slab, tokens)))
-    pieces, columns = [], []
+    todo = [([picks], product(x, blocks, picks, slab, tokens)) for picks in slots]
+    pieces, columns = [], [[] for _ in range(n)]
     for picked, got in todo:
-        table = jnp.array(
-            [[2 * (q - way * k) for q, (way, k) in enumerate(picks)] for picks in picked],
-            jnp.int32,
-        )[:, slab]
-        for flip in range(2):
+        for flip in (1, 0):
             route = [
                 (s * pipes + p, (s ^ flip) * pipes + (p - 1) % pipes)
                 for s in range(n) for p in range(pipes)
             ]
             pieces.append(lax.ppermute(got[flip], ("seq", "pipe"), route))
-            columns.append(table + (side ^ flip))
-    return assembled(pieces, jnp.concatenate(columns), rows)
+            for picks in picked:
+                for s in range(n):
+                    way, k = picks[s // 2]
+                    columns[s].append(2 * (s // 2 - way * k) + (s % 2 ^ flip))
+    return assembled(pieces, jnp.array(columns, jnp.int32), mine, rows)
 
 
 def solution(mesh):

time: 206 us -> 197 us (0.956)
  waiting for transfers between devices: 85.3 us -> 77.9 us
  starting transfers between devices: 36.6 us -> 41 us
  local copies, waits for them, and re-layouts: 7.2 us -> 3.57 us
    pallas_call x1 -> x4, Pallas kernels: 2.52 us -> 13 us  [product(): pl.pallas_call(functools.partial(product_kernel, which), in_specs=[pl.Blo...]
    pallas_call x1, Pallas kernels: 21 us -> 10.7 us  [far_part(): pl.pallas_call(functools.partial(far_kernel, heads), grid=(heads // GROUP...]
    ppermute x4 -> x8, waiting for transfers between devices: 16.9 us -> 9.59 us  [body(): pieces.append(lax.ppermute(got[flip], ('seq', 'pipe'), route))]
    ppermute x3, waiting for transfers between devices: 2.42 us -> 7.48 us  [body(): lax.ppermute(blocks.get((1, k - 1), weight), 'seq', [(s, s + 2) for s in...]
    ppermute x7 -> x6, waiting for transfers between devices: 3.68 us -> 0.02 us  [swap(): return lax.ppermute(x, 'seq', pair)]
    ppermute x4 -> x8, starting transfers between devices: 6.68 us -> 10.2 us  [body(): pieces.append(lax.ppermute(got[flip], ('seq', 'pipe'), route))]
    unnamed x35 -> x26, local copies, waits for them, and re-layouts: 4.66 us -> 1.63 us
    ppermute x7 -> x6, starting transfers between devices: 5.83 us -> 5.54 us  [swap(): return lax.ppermute(x, 'seq', pair)]
  transfers between devices with their start and end apart: 20 -> 23, of which waited for: 9 -> 8; matrix products, arithmetic and copies ran while one was open for 5% -> 5% of each run, Pallas kernels for 32% -> 33%
where the time goes in v5:
time: 197 us
  waiting for transfers between devices  77.9 us (40%)
  Pallas kernels  66.5 us (34%)
  starting transfers between devices  41 us (21%)
  other arithmetic  7.27 us (4%)
  local copies, waits for them, and re-layouts  3.57 us (2%)
    ppermute x3, waiting for transfers between devices, body(): lax.ppermute(leaving, 'seq', [(2 * at + y, 2 * at - 2 + y) for y in range...  58 us
    pallas_call x2, Pallas kernels, near_part(): pl.pallas_call(functools.partial(near_kernel, chunks, heads, pieces), gri...  28.6 us
    pallas_call x4, Pallas kernels, product(): pl.pallas_call(functools.partial(product_kernel, which), in_specs=[pl.Blo...  13 us
    pallas_call x1, Pallas kernels, far_part(): pl.pallas_call(functools.partial(far_kernel, heads), grid=(heads // GROUP...  10.7 us
    ppermute x8, starting transfers between devices, body(): pieces.append(lax.ppermute(got[flip], ('seq', 'pipe'), route))  10.2 us
    ppermute x3, starting transfers between devices, body(): lax.ppermute(blocks.get((1, k - 1), weight), 'seq', [(s, s + 2) for s in...  9.8 us
    ppermute x8, waiting for transfers between devices, body(): pieces.append(lax.ppermute(got[flip], ('seq', 'pipe'), route))  9.59 us
    ppermute x3, waiting for transfers between devices, body(): lax.ppermute(blocks.get((1, k - 1), weight), 'seq', [(s, s + 2) for s in...  7.48 us
  transfers between devices with their start and end apart: 23, of which 8 were waited for; matrix products, arithmetic and copies ran while one was open for 5% of the time, Pallas kernels for 33%

profile of v5, /device:TPU:9, one launch (start us, length us, event | category | flops | bytes accessed | tf_op | source)
XLA Modules:
  0.0 196.6 jit_solution(3992340580474707153)
XLA Ops:
  0.0 3.2 %collective-permute-start.5 = (bf16[256,4096]{1,0:T(8,128)(2,1)}, bf16[256,4096]{1,0:T(8,128)(2,1)}, u32[]{:S(2)}, u32[]{:S(2)}) collective-permute-start(bf16[256,4096]{1,0:T(8,128)(2,1)} %bitcast.18), channel_id=1, source_target_pairs={{0,8},{4,12},{8,16},{12,20},{16,24},{20,28},{1,9},{5,13},{9,17},{1... | collective-permute-start | bytes 6291464 | tf_op jit(solution)/shard_map/ppermute | solution.py:402
  3.2 3.4 %collective-permute-start.6 = (bf16[256,4096]{1,0:T(8,128)(2,1)}, bf16[256,4096]{1,0:T(8,128)(2,1)S(1)}, u32[]{:S(2)}, u32[]{:S(2)}) collective-permute-start(bf16[256,4096]{1,0:T(8,128)(2,1)} %bitcast.19), channel_id=1, source_target_pairs={{8,0},{12,4},{16,8},{20,12},{24,16},{28,20},{9,1},{13,5},{17,9},{2... | collective-permute-start | bytes 6291464 | tf_op jit(solution)/shard_map/ppermute | solution.py:407
  6.6 1.3 collective-permute-start
  7.9 0.2 collective-permute-start.1
  8.1 0.7 convert_element_type.53
  8.8 0.8 pad_maximum_fusion.ext_ref
  9.6 1.2 collective-permute-start.2
  10.9 2.5 %prep.2 = (f32[512,128]{1,0:T(8,128)}, f32[8,4,512]{2,1,0:T(4,128)}, f32[8,4,512]{2,1,0:T(4,128)}, f32[8,16,128]{2,1,0:T(8,128)}, f32[8,4,128]{2,1,0:T(4,128)}, ...) custom-call(f32[40,512]{1,0:T(8,128)} %copy-done.11, bf16[512,128]{1,0:T(8,128)(2,1)} %bitcast.31), custom_call_target="tpu_custom_call" | custom-call | tf_op jit(solution)/shard_map/prep/pallas_call | solution.py:211
  13.4 7.1 %states.1 = bf16[32,144,128]{2,1,0:T(8,128)(2,1)} custom-call(bf16[128,512]{1,0:T(8,128)(2,1)} %get-tuple-element.35.readst_ref, f32[8,4,512]{2,1,0:T(4,128)} %get-tuple-element.42.allr_ref, f32[8,4,128]{2,1,0:T(4,128)} %get-tuple-element.41.whole_ref, bf16[512,4096]{1,0:T(8,128)(2,1)} %bitcast.27), custom_call_target="tpu_custom_call" | custom-call | tf_op jit(solution)/shard_map/states/pallas_call | solution.py:266
  20.5 1.9 constant_dynamic-slice_fusion
  22.5 0.7 collective-permute-start.4
  23.2 0.8 collective-permute-start.3
  24.0 13.3 %near.2.refs_0_ = bf16[512,4096]{1,0:T(8,128)(2,1)} custom-call(f32[1,32]{1,0:T(1,128)} %gain_ref.3, bf16[512,128]{1,0:T(8,128)(2,1)} %bitcast.25, bf16[512,128]{1,0:T(8,128)(2,1)} %bitcast.32, bf16[128,512]{1,0:T(8,128)(2,1)} %get-tuple-element.35.readst_ref, f32[1,512]{1,0:T(1,128)} %get-tuple-element.36.cntr_ref, ...), custom_call_target="tpu_custom_call" | custom-call | tf_op jit(solution)/shard_map/near/pallas_call | solution.py:230
  37.3 2.5 %prep.3 = (f32[512,128]{1,0:T(8,128)}, f32[8,4,512]{2,1,0:T(4,128)}, f32[8,4,512]{2,1,0:T(4,128)}, f32[8,16,128]{2,1,0:T(8,128)}, f32[8,4,128]{2,1,0:T(4,128)}, ...) custom-call(f32[40,512]{1,0:T(8,128)} %copy-done.12, bf16[512,128]{1,0:T(8,128)(2,1)} %copy-done.10), custom_call_target="tpu_custom_call" | custom-call | tf_op jit(solution)/shard_map/prep/pallas_call | solution.py:211
  39.8 1.2 broadcast_select_fusion.2
  41.2 7.5 %collective-permute-done.5.refs_1_.refs_2_.refs_3_ = bf16[256,4096]{1,0:T(8,128)(2,1)} collective-permute-done((bf16[256,4096]{1,0:T(8,128)(2,1)}, bf16[256,4096]{1,0:T(8,128)(2,1)}, u32[]{:S(2)}, u32[]{:S(2)}) %collective-permute-start.5) | collective-permute-done | bytes 2097184 | tf_op jit(solution)/shard_map/ppermute | solution.py:402
  48.7 2.9 %collective-permute-done.6.refs_0_.refs_1_.refs_2_ = bf16[256,4096]{1,0:T(8,128)(2,1)S(1)} collective-permute-done((bf16[256,4096]{1,0:T(8,128)(2,1)}, bf16[256,4096]{1,0:T(8,128)(2,1)S(1)}, u32[]{:S(2)}, u32[]{:S(2)}) %collective-permute-start.6) | collective-permute-done | bytes 2097184 | tf_op jit(solution)/shard_map/ppermute | solution.py:407
  51.6 0.7 collective-permute-start.7
  52.3 3.4 %collective-permute-start.15 = (bf16[256,4096]{1,0:T(8,128)(2,1)S(1)}, bf16[256,4096]{1,0:T(8,128)(2,1)}, u32[]{:S(2)}, u32[]{:S(2)}) collective-permute-start(bf16[256,4096]{1,0:T(8,128)(2,1)S(1)} %collective-permute-done.6.refs_0_.refs_1_.refs_2_), channel_id=1, source_target_pairs={{8,0},{12,4},{16,8},{20,12},{9,1},{13,5},{17,9},{21,13},{10,2},{14... | collective-permute-start | bytes 6291464 | tf_op jit(solution)/shard_map/ppermute | solution.py:407
  55.6 4.6 %collective-permute-start.16 = (bf16[256,4096]{1,0:T(8,128)(2,1)}, bf16[256,4096]{1,0:T(8,128)(2,1)}, u32[]{:S(2)}, u32[]{:S(2)}) collective-permute-start(bf16[256,4096]{1,0:T(8,128)(2,1)} %collective-permute-done.5.refs_1_.refs_2_.refs_3_), channel_id=1, source_target_pairs={{8,16},{12,20},{16,24},{20,28},{9,17},{13,21},{17,25},{21,29},{10,... | collective-permute-start | bytes 6291464 | tf_op jit(solution)/shard_map/ppermute | solution.py:402
  60.2 0.3 add_convert_fusion.2
  60.5 1.3 collective-permute-start.8
  61.8 49.1 %collective-permute-done.8 = bf16[16,128,128]{2,1,0:T(8,128)(2,1)S(1)} collective-permute-done((bf16[16,128,128]{2,1,0:T(8,128)(2,1)S(1)}, bf16[16,128,128]{2,1,0:T(8,128)(2,1)S(1)}, u32[]{:S(2)}, u32[]{:S(2)}) %collective-permute-start.8) | collective-permute-done | bytes 524320 | tf_op jit(solution)/shard_map/ppermute | solution.py:429
  110.9 0.4 add_convert_fusion.1
  111.3 1.3 collective-permute-start.9
  112.6 8.9 %collective-permute-done.9 = bf16[16,128,128]{2,1,0:T(8,128)(2,1)S(1)} collective-permute-done((bf16[16,128,128]{2,1,0:T(8,128)(2,1)S(1)}, bf16[16,128,128]{2,1,0:T(8,128)(2,1)S(1)}, u32[]{:S(2)}, u32[]{:S(2)}) %collective-permute-start.9) | collective-permute-done | bytes 524320 | tf_op jit(solution)/shard_map/ppermute | solution.py:429
  121.5 0.9 add.51
  122.5 5.5 %collective-permute-start.19 = (bf16[256,4096]{1,0:T(8,128)(2,1)}, bf16[256,4096]{1,0:T(8,128)(2,1)}, u32[]{:S(2)}, u32[]{:S(2)}) collective-permute-start(bf16[256,4096]{1,0:T(8,128)(2,1)} %collective-permute-done.15.refs_0_.refs_1_), channel_id=1, source_target_pairs={{8,0},{12,4},{9,1},{13,5},{10,2},{14,6},{11,3},{15,7}} | collective-permute-start | bytes 6291464 | tf_op jit(solution)/shard_map/ppermute | solution.py:432
  128.0 2.0 %collective-permute-start.20 = (bf16[256,4096]{1,0:T(8,128)(2,1)}, bf16[256,4096]{1,0:T(8,128)(2,1)}, u32[]{:S(2)}, u32[]{:S(2)}) collective-permute-start(bf16[256,4096]{1,0:T(8,128)(2,1)} %collective-permute-done.16.refs_3_.refs_2_), channel_id=1, source_target_pairs={{16,24},{20,28},{17,25},{21,29},{18,26},{22,30},{19,27},{23,31}} | collective-permute-start | bytes 6291464 | tf_op jit(solution)/shard_map/ppermute | solution.py:402
  130.0 1.2 collective-permute-start.10
  131.3 15.2 %near.3 = (bf16[512,4096]{1,0:T(8,128)(2,1)}, bf16[32,144,128]{2,1,0:T(8,128)(2,1)}) custom-call(f32[1,32]{1,0:T(1,128)} %gain_ref.3, bf16[512,128]{1,0:T(8,128)(2,1)} %copy-done.4, bf16[512,128]{1,0:T(8,128)(2,1)} %copy-done.10, bf16[128,512]{1,0:T(8,128)(2,1)} %get-tuple-element.44.readst_ref, f32[1,512]{1,0:T(1,128)} %get-tuple-element.45.cntr_ref, ...), custom_call_target="tpu_custom_call" | custom-call | tf_op jit(solution)/shard_map/near/pallas_call | solution.py:230
  146.5 1.8 maximum_select_fusion
  148.6 0.8 fusion
  149.5 1.4 copy-done.1
  150.9 10.7 %far.1.x_ref = bf16[1024,4096]{1,0:T(8,128)(2,1)S(1)} custom-call(bf16[512,4096]{1,0:T(8,128)(2,1)S(1)} %copy-done.1, bf16[512,4096]{1,0:T(8,128)(2,1)} %get-tuple-element.54.refs_1_, bf16[512,128]{1,0:T(8,128)(2,1)S(1)} %bitcast.26, bf16[512,128]{1,0:T(8,128)(2,1)S(1)} %copy-done.5, f32[512,128]{1,0:T(8,128)S(1)} %copy-done.3, f32[512,128]{1,0:T(8,128)S(1)} %copy-done.2, ...), custom_call_target="tpu_custom_call" | custom-call | tf_op jit(solution)/shard_map/far/pallas_call | solution.py:303
  161.6 2.5 %product.4 = (bf16[512,256]{1,0:T(8,128)(2,1)S(1)}, bf16[512,256]{1,0:T(8,128)(2,1)S(1)}) custom-call(s32[1]{0:T(128)} %bitcast.1.slab_ref, bf16[1024,4096]{1,0:T(8,128)(2,1)S(1)} %far.1.x_ref, bf16[256,4096]{1,0:T(8,128)(2,1)S(1)} %bitcast.20, bf16[256,4096]{1,0:T(8,128)(2,1)S(1)} %bitcast.21, bf16[256,4096]{1,0:T(8,128)(2,1)S(1)} %bitcast.22, ...), custom_call_target="tpu_custom_call" | custom-call | tf_op jit(solution)/shard_map/product/pallas_call | solution.py:322
  164.1 3.8 %collective-permute-start.11 = (bf16[512,256]{1,0:T(8,128)(2,1)S(1)}, bf16[512,256]{1,0:T(8,128)(2,1)S(1)}, u32[]{:S(2)}, u32[]{:S(2)}) collective-permute-start(bf16[512,256]{1,0:T(8,128)(2,1)S(1)} %get-tuple-element.56), channel_id=1, source_target_pairs={{0,7},{1,4},{2,5},{3,6},{4,3},{5,0},{6,1},{7,2},{8,15},{9,12},{10,... | collective-permute-start | bytes 786440 | tf_op jit(solution)/shard_map/ppermute | solution.py:456
  167.9 4.0 %product.5 = (bf16[512,256]{1,0:T(8,128)(2,1)S(1)}, bf16[512,256]{1,0:T(8,128)(2,1)S(1)}) custom-call(s32[1]{0:T(128)} %bitcast.1.slab_ref, bf16[1024,4096]{1,0:T(8,128)(2,1)S(1)} %far.1.x_ref, bf16[256,4096]{1,0:T(8,128)(2,1)S(1)} %collective-permute-done.6.refs_0_.refs_1_.refs_2_, bf16[256,4096]{1,0:T(8,128)(2,1)} %collective-permute-done.5.refs_1_.refs_2_.refs_3_, ...), custom_call_target="tpu_custom_call" | custom-call | tf_op jit(solution)/shard_map/product/pallas_call | solution.py:322
  171.9 2.8 %collective-permute-start.13 = (bf16[512,256]{1,0:T(8,128)(2,1)S(1)}, bf16[512,256]{1,0:T(8,128)(2,1)S(1)}, u32[]{:S(2)}, u32[]{:S(2)}) collective-permute-start(bf16[512,256]{1,0:T(8,128)(2,1)S(1)} %get-tuple-element.58), channel_id=1, source_target_pairs={{0,7},{1,4},{2,5},{3,6},{4,3},{5,0},{6,1},{7,2},{8,15},{9,12},{10,... | collective-permute-start | bytes 786440 | tf_op jit(solution)/shard_map/ppermute | solution.py:456
  174.7 2.5 %product.6 = (bf16[512,256]{1,0:T(8,128)(2,1)S(1)}, bf16[512,256]{1,0:T(8,128)(2,1)S(1)}) custom-call(s32[1]{0:T(128)} %bitcast.1.slab_ref, bf16[1024,4096]{1,0:T(8,128)(2,1)S(1)} %far.1.x_ref, bf16[256,4096]{1,0:T(8,128)(2,1)} %collective-permute-done.15.refs_0_.refs_1_, bf16[256,4096]{1,0:T(8,128)(2,1)S(1)} %collective-permute-done.6.refs_0_.refs_1_.refs_2_, ...), custom_call_target="tpu_custom_call" | custom-call | tf_op jit(solution)/shard_map/product/pallas_call | solution.py:322
  177.3 0.7 collective-permute-start.17
  178.1 4.0 %product.7 = (bf16[512,256]{1,0:T(8,128)(2,1)S(1)}, bf16[512,256]{1,0:T(8,128)(2,1)S(1)}) custom-call(s32[1]{0:T(128)} %bitcast.1.slab_ref, bf16[1024,4096]{1,0:T(8,128)(2,1)S(1)} %far.1.x_ref, bf16[256,4096]{1,0:T(8,128)(2,1)} %collective-permute-done.19.refs_0_, bf16[256,4096]{1,0:T(8,128)(2,1)} %collective-permute-done.15.refs_0_.refs_1_, ...), custom_call_target="tpu_custom_call" | custom-call | tf_op jit(solution)/shard_map/product/pallas_call | solution.py:322
  182.1 2.7 %collective-permute-start.21 = (bf16[512,256]{1,0:T(8,128)(2,1)S(1)}, bf16[512,256]{1,0:T(8,128)(2,1)S(1)}, u32[]{:S(2)}, u32[]{:S(2)}) collective-permute-start(bf16[512,256]{1,0:T(8,128)(2,1)S(1)} %get-tuple-element.63), channel_id=1, source_target_pairs={{0,7},{1,4},{2,5},{3,6},{4,3},{5,0},{6,1},{7,2},{8,15},{9,12},{10,... | collective-permute-start | bytes 786440 | tf_op jit(solution)/shard_map/ppermute | solution.py:456
  184.8 1.6 collective-permute-done.17.refs_4_
  186.4 2.6 %collective-permute-done.18.refs_5_ = bf16[512,256]{1,0:T(8,128)(2,1)S(1)} collective-permute-done((bf16[512,256]{1,0:T(8,128)(2,1)S(1)}, bf16[512,256]{1,0:T(8,128)(2,1)S(1)}, u32[]{:S(2)}, u32[]{:S(2)}) %collective-permute-start.18) | collective-permute-done | bytes 262176 | tf_op jit(solution)/shard_map/ppermute | solution.py:456
  189.0 3.0 %collective-permute-done.21.refs_6_ = bf16[512,256]{1,0:T(8,128)(2,1)S(1)} collective-permute-done((bf16[512,256]{1,0:T(8,128)(2,1)S(1)}, bf16[512,256]{1,0:T(8,128)(2,1)S(1)}, u32[]{:S(2)}, u32[]{:S(2)}) %collective-permute-start.21) | collective-permute-done | bytes 262176 | tf_op jit(solution)/shard_map/ppermute | solution.py:456
  192.0 2.4 %collective-permute-done.22.refs_7_ = bf16[512,256]{1,0:T(8,128)(2,1)S(1)} collective-permute-done((bf16[512,256]{1,0:T(8,128)(2,1)S(1)}, bf16[512,256]{1,0:T(8,128)(2,1)S(1)}, u32[]{:S(2)}, u32[]{:S(2)}) %collective-permute-start.22) | collective-permute-done | bytes 262176 | tf_op jit(solution)/shard_map/ppermute | solution.py:456
  194.4 2.2 %assemble.1 = bf16[1,512,2048]{2,1,0:T(8,128)(2,1)} custom-call(s32[1]{0:T(128)} %bitcast.mine_ref, s32[8,8]{1,0:T(8,128)S(1)} %copy-done.7, bf16[512,256]{1,0:T(8,128)(2,1)S(1)} %collective-permute-done.11.refs_0_, bf16[512,256]{1,0:T(8,128)(2,1)S(1)} %collective-permute-done.12.refs_1_, bf16[512,256]{1,0:T(8,128)(2,1)S(1)} %collective-permute-done.13.refs_2_, ...), custom_call_target="tpu_custom_call" | custom-call | tf_op jit(solution)/shard_map/assemble/pallas_call | solution.py:362
  (50 shorter events, 0.8 us)
Async XLA Ops:
  0.0 48.7 %collective-permute-start.5 = (bf16[256,4096]{1,0:T(8,128)(2,1)}, bf16[256,4096]{1,0:T(8,128)(2,1)}, u32[]{:S(2)}, u32[]{:S(2)}) collective-permute-start(bf16[256,4096]{1,0:T(8,128)(2,1)} %bitcast.18), channel_id=1, source_target_pairs={{0,8},{4,12},{8,16},{12,20},{16,24},{20,28},{1,9},{5,13},{9,17},{1... | collective-permute-start | bytes 6291464 | tf_op jit(solution)/shard_map/ppermute | solution.py:402
  3.2 48.4 %collective-permute-start.6 = (bf16[256,4096]{1,0:T(8,128)(2,1)}, bf16[256,4096]{1,0:T(8,128)(2,1)S(1)}, u32[]{:S(2)}, u32[]{:S(2)}) collective-permute-start(bf16[256,4096]{1,0:T(8,128)(2,1)} %bitcast.19), channel_id=1, source_target_pairs={{8,0},{12,4},{16,8},{20,12},{24,16},{28,20},{9,1},{13,5},{17,9},{2... | collective-permute-start | bytes 6291464 | tf_op jit(solution)/shard_map/ppermute | solution.py:407
  6.6 15.9 %collective-permute-start = (bf16[512,128]{1,0:T(8,128)(2,1)}, bf16[512,128]{1,0:T(8,128)(2,1)S(1)}, u32[]{:S(2)}, u32[]{:S(2)}) collective-permute-start(bf16[512,128]{1,0:T(8,128)(2,1)} %bitcast.24), channel_id=1, source_target_pairs={{0,4},{4,0},{8,12},{12,8},{16,20},{20,16},{24,28},{28,24},{1,5},{5... | collective-permute-start | bytes 393224 | tf_op jit(solution)/shard_map/ppermute | solution.py:395
  7.9 14.6 %collective-permute-start.1 = (bf16[512,128]{1,0:T(8,128)(2,1)}, bf16[512,128]{1,0:T(8,128)(2,1)S(1)}, u32[]{:S(2)}, u32[]{:S(2)}) collective-permute-start(bf16[512,128]{1,0:T(8,128)(2,1)} %bitcast.30), channel_id=1, source_target_pairs={{0,4},{4,0},{8,12},{12,8},{16,20},{20,16},{24,28},{28,24},{1,5},{5... | collective-permute-start | bytes 393224 | tf_op jit(solution)/shard_map/ppermute | solution.py:395
  9.6 1.2 copy-start.11
  9.6 12.8 %collective-permute-start.2 = (f32[40,512]{1,0:T(8,128)S(1)}, f32[40,512]{1,0:T(8,128)S(1)}, u32[]{:S(2)}, u32[]{:S(2)}) collective-permute-start(f32[40,512]{1,0:T(8,128)S(1)} %pad_maximum_fusion.ext_ref), channel_id=1, source_target_pairs={{0,4},{4,0},{8,12},{12,8},{16,20},{20,16},{24,28},{28,24},{1,5},{5... | collective-permute-start | bytes 245768 | tf_op jit(solution)/shard_map/ppermute | solution.py:395
  22.4 1.6 copy-start.12
  22.4 14.9 %copy-start.4 = (bf16[512,128]{1,0:T(8,128)(2,1)}, bf16[512,128]{1,0:T(8,128)(2,1)S(1)}, u32[]{:S(2)}) copy-start(bf16[512,128]{1,0:T(8,128)(2,1)S(1)} %collective-permute-done.writes_ref.refs_3_) | copy-start | bytes 393220
  22.4 14.9 %copy-start.10 = (bf16[512,128]{1,0:T(8,128)(2,1)}, bf16[512,128]{1,0:T(8,128)(2,1)S(1)}, u32[]{:S(2)}) copy-start(bf16[512,128]{1,0:T(8,128)(2,1)S(1)} %collective-permute-done.1.reads_ref) | copy-start | bytes 393220
  22.5 17.4 %collective-permute-start.4 = (bf16[16,144,128]{2,1,0:T(8,128)(2,1)}, bf16[16,144,128]{2,1,0:T(8,128)(2,1)}, u32[]{:S(2)}, u32[]{:S(2)}) collective-permute-start(bf16[16,144,128]{2,1,0:T(8,128)(2,1)} %constant_dynamic-slice_fusion), channel_id=1, source_target_pairs={{0,4},{4,0},{8,12},{12,8},{16,20},{20,16},{24,28},{28,24},{1,5},{5... | collective-permute-start | bytes 1769480 | tf_op jit(solution)/shard_map/ppermute | solution.py:395
  23.2 108.1 %collective-permute-start.3 = (bf16[512,4096]{1,0:T(8,128)(2,1)}, bf16[512,4096]{1,0:T(8,128)(2,1)}, u32[]{:S(2)}, u32[]{:S(2)}) collective-permute-start(bf16[512,4096]{1,0:T(8,128)(2,1)} %bitcast.28), channel_id=1, source_target_pairs={{0,4},{4,0},{8,12},{12,8},{16,20},{20,16},{24,28},{28,24},{1,5},{5... | collective-permute-start | bytes 12582920 | tf_op jit(solution)/shard_map/ppermute | solution.py:395
  24.0 15.8 %copy-start.8 = (bf16[32,144,128]{2,1,0:T(8,128)(2,1)S(1)}, bf16[32,144,128]{2,1,0:T(8,128)(2,1)}, u32[]{:S(2)}) copy-start(bf16[32,144,128]{2,1,0:T(8,128)(2,1)} %states.1) | copy-start | bytes 3538948
  51.6 8.6 %collective-permute-start.7 = (bf16[16,128,128]{2,1,0:T(8,128)(2,1)S(1)}, bf16[16,128,128]{2,1,0:T(8,128)(2,1)S(1)}, u32[]{:S(2)}, u32[]{:S(2)}) collective-permute-start(bf16[16,128,128]{2,1,0:T(8,128)(2,1)S(1)} %add_convert_fusion.3), channel_id=1, source_target_pairs={{24,16},{28,20},{25,17},{29,21},{26,18},{30,22},{27,19},{31,23}} | collective-permute-start | bytes 1572872 | tf_op jit(solution)/shard_map/ppermute | solution.py:429
  52.3 70.2 %collective-permute-start.15 = (bf16[256,4096]{1,0:T(8,128)(2,1)S(1)}, bf16[256,4096]{1,0:T(8,128)(2,1)}, u32[]{:S(2)}, u32[]{:S(2)}) collective-permute-start(bf16[256,4096]{1,0:T(8,128)(2,1)S(1)} %collective-permute-done.6.refs_0_.refs_1_.refs_2_), channel_id=1, source_target_pairs={{8,0},{12,4},{16,8},{20,12},{9,1},{13,5},{17,9},{21,13},{10,2},{14... | collective-permute-start | bytes 6291464 | tf_op jit(solution)/shard_map/ppermute | solution.py:407
  55.6 72.3 %collective-permute-start.16 = (bf16[256,4096]{1,0:T(8,128)(2,1)}, bf16[256,4096]{1,0:T(8,128)(2,1)}, u32[]{:S(2)}, u32[]{:S(2)}) collective-permute-start(bf16[256,4096]{1,0:T(8,128)(2,1)} %collective-permute-done.5.refs_1_.refs_2_.refs_3_), channel_id=1, source_target_pairs={{8,16},{12,20},{16,24},{20,28},{9,17},{13,21},{17,25},{21,29},{10,... | collective-permute-start | bytes 6291464 | tf_op jit(solution)/shard_map/ppermute | solution.py:402
  60.5 50.4 %collective-permute-start.8 = (bf16[16,128,128]{2,1,0:T(8,128)(2,1)S(1)}, bf16[16,128,128]{2,1,0:T(8,128)(2,1)S(1)}, u32[]{:S(2)}, u32[]{:S(2)}) collective-permute-start(bf16[16,128,128]{2,1,0:T(8,128)(2,1)S(1)} %add_convert_fusion.2), channel_id=1, source_target_pairs={{16,8},{20,12},{17,9},{21,13},{18,10},{22,14},{19,11},{23,15}} | collective-permute-start | bytes 1572872 | tf_op jit(solution)/shard_map/ppermute | solution.py:429
  111.3 10.2 %collective-permute-start.9 = (bf16[16,128,128]{2,1,0:T(8,128)(2,1)S(1)}, bf16[16,128,128]{2,1,0:T(8,128)(2,1)S(1)}, u32[]{:S(2)}, u32[]{:S(2)}) collective-permute-start(bf16[16,128,128]{2,1,0:T(8,128)(2,1)S(1)} %get-tuple-element.65), channel_id=1, source_target_pairs={{8,0},{12,4},{9,1},{13,5},{10,2},{14,6},{11,3},{15,7}} | collective-permute-start | bytes 1572872 | tf_op jit(solution)/shard_map/ppermute | solution.py:429
  122.5 54.8 %collective-permute-start.19 = (bf16[256,4096]{1,0:T(8,128)(2,1)}, bf16[256,4096]{1,0:T(8,128)(2,1)}, u32[]{:S(2)}, u32[]{:S(2)}) collective-permute-start(bf16[256,4096]{1,0:T(8,128)(2,1)} %collective-permute-done.15.refs_0_.refs_1_), channel_id=1, source_target_pairs={{8,0},{12,4},{9,1},{13,5},{10,2},{14,6},{11,3},{15,7}} | collective-permute-start | bytes 6291464 | tf_op jit(solution)/shard_map/ppermute | solution.py:432
  128.0 49.3 %collective-permute-start.20 = (bf16[256,4096]{1,0:T(8,128)(2,1)}, bf16[256,4096]{1,0:T(8,128)(2,1)}, u32[]{:S(2)}, u32[]{:S(2)}) collective-permute-start(bf16[256,4096]{1,0:T(8,128)(2,1)} %collective-permute-done.16.refs_3_.refs_2_), channel_id=1, source_target_pairs={{16,24},{20,28},{17,25},{21,29},{18,26},{22,30},{19,27},{23,31}} | collective-permute-start | bytes 6291464 | tf_op jit(solution)/shard_map/ppermute | solution.py:402
  130.0 16.5 %collective-permute-start.10 = (bf16[16,128,128]{2,1,0:T(8,128)(2,1)}, bf16[16,128,128]{2,1,0:T(8,128)(2,1)}, u32[]{:S(2)}, u32[]{:S(2)}) collective-permute-start(bf16[16,128,128]{2,1,0:T(8,128)(2,1)} %add.51), channel_id=1, source_target_pairs={{0,4},{4,0},{8,12},{12,8},{16,20},{20,16},{24,28},{28,24},{1,5},{5... | collective-permute-start | bytes 1572872 | tf_op jit(solution)/shard_map/ppermute | solution.py:395
  146.5 1.9 copy-start.9
  148.4 1.0 copy-start.2
  148.4 1.0 copy-start.3
  148.4 1.1 copy-start.5
  148.4 1.1 copy-start.6
  148.6 2.3 %copy-start.1 = (bf16[512,4096]{1,0:T(8,128)(2,1)S(1)}, bf16[512,4096]{1,0:T(8,128)(2,1)}, u32[]{:S(2)}) copy-start(bf16[512,4096]{1,0:T(8,128)(2,1)} %near.2.refs_0_) | copy-start | bytes 12582916
  150.9 10.7 %copy-start = (bf16[1,256,4096]{2,1,0:T(8,128)(2,1)S(1)}, bf16[1,256,4096]{2,1,0:T(8,128)(2,1)}, u32[]{:S(2)}) copy-start(bf16[1,256,4096]{2,1,0:T(8,128)(2,1)} %param.14) | copy-start | bytes 6291460
  164.1 17.9 %collective-permute-start.11 = (bf16[512,256]{1,0:T(8,128)(2,1)S(1)}, bf16[512,256]{1,0:T(8,128)(2,1)S(1)}, u32[]{:S(2)}, u32[]{:S(2)}) collective-permute-start(bf16[512,256]{1,0:T(8,128)(2,1)S(1)} %get-tuple-element.56), channel_id=1, source_target_pairs={{0,7},{1,4},{2,5},{3,6},{4,3},{5,0},{6,1},{7,2},{8,15},{9,12},{10,... | collective-permute-start | bytes 786440 | tf_op jit(solution)/shard_map/ppermute | solution.py:456
  167.9 14.2 %collective-permute-start.12 = (bf16[512,256]{1,0:T(8,128)(2,1)S(1)}, bf16[512,256]{1,0:T(8,128)(2,1)S(1)}, u32[]{:S(2)}, u32[]{:S(2)}) collective-permute-start(bf16[512,256]{1,0:T(8,128)(2,1)S(1)} %get-tuple-element.57), channel_id=1, source_target_pairs={{0,3},{1,0},{2,1},{3,2},{4,7},{5,4},{6,5},{7,6},{8,11},{9,8},{10,9... | collective-permute-start | bytes 786440 | tf_op jit(solution)/shard_map/ppermute | solution.py:456
  171.9 12.9 %collective-permute-start.13 = (bf16[512,256]{1,0:T(8,128)(2,1)S(1)}, bf16[512,256]{1,0:T(8,128)(2,1)S(1)}, u32[]{:S(2)}, u32[]{:S(2)}) collective-permute-start(bf16[512,256]{1,0:T(8,128)(2,1)S(1)} %get-tuple-element.58), channel_id=1, source_target_pairs={{0,7},{1,4},{2,5},{3,6},{4,3},{5,0},{6,1},{7,2},{8,15},{9,12},{10,... | collective-permute-start | bytes 786440 | tf_op jit(solution)/shard_map/ppermute | solution.py:456
  177.2 7.6 %collective-permute-start.14 = (bf16[512,256]{1,0:T(8,128)(2,1)S(1)}, bf16[512,256]{1,0:T(8,128)(2,1)S(1)}, u32[]{:S(2)}, u32[]{:S(2)}) collective-permute-start(bf16[512,256]{1,0:T(8,128)(2,1)S(1)} %get-tuple-element.59), channel_id=1, source_target_pairs={{0,3},{1,0},{2,1},{3,2},{4,7},{5,4},{6,5},{7,6},{8,11},{9,8},{10,9... | collective-permute-start | bytes 786440 | tf_op jit(solution)/shard_map/ppermute | solution.py:456
  177.3 17.1 %copy-start.7 = (s32[8,8]{1,0:T(8,128)S(1)}, s32[8,8]{1,0:T(8,128)}, u32[]{:S(2)}) copy-start(s32[8,8]{1,0:T(8,128)} %constant.41.clone.columns_ref) | copy-start | bytes 772
  177.3 9.1 %collective-permute-start.17 = (bf16[512,256]{1,0:T(8,128)(2,1)S(1)}, bf16[512,256]{1,0:T(8,128)(2,1)S(1)}, u32[]{:S(2)}, u32[]{:S(2)}) collective-permute-start(bf16[512,256]{1,0:T(8,128)(2,1)S(1)} %get-tuple-element.60), channel_id=1, source_target_pairs={{0,7},{1,4},{2,5},{3,6},{4,3},{5,0},{6,1},{7,2},{8,15},{9,12},{10,... | collective-permute-start | bytes 786440 | tf_op jit(solution)/shard_map/ppermute | solution.py:456
  182.0 7.0 %collective-permute-start.18 = (bf16[512,256]{1,0:T(8,128)(2,1)S(1)}, bf16[512,256]{1,0:T(8,128)(2,1)S(1)}, u32[]{:S(2)}, u32[]{:S(2)}) collective-permute-start(bf16[512,256]{1,0:T(8,128)(2,1)S(1)} %get-tuple-element.61), channel_id=1, source_target_pairs={{0,3},{1,0},{2,1},{3,2},{4,7},{5,4},{6,5},{7,6},{8,11},{9,8},{10,9... | collective-permute-start | bytes 786440 | tf_op jit(solution)/shard_map/ppermute | solution.py:456
  182.1 9.9 %collective-permute-start.21 = (bf16[512,256]{1,0:T(8,128)(2,1)S(1)}, bf16[512,256]{1,0:T(8,128)(2,1)S(1)}, u32[]{:S(2)}, u32[]{:S(2)}) collective-permute-start(bf16[512,256]{1,0:T(8,128)(2,1)S(1)} %get-tuple-element.63), channel_id=1, source_target_pairs={{0,7},{1,4},{2,5},{3,6},{4,3},{5,0},{6,1},{7,2},{8,15},{9,12},{10,... | collective-permute-start | bytes 786440 | tf_op jit(solution)/shard_map/ppermute | solution.py:456
  184.8 9.6 %collective-permute-start.22 = (bf16[512,256]{1,0:T(8,128)(2,1)S(1)}, bf16[512,256]{1,0:T(8,128)(2,1)S(1)}, u32[]{:S(2)}, u32[]{:S(2)}) collective-permute-start(bf16[512,256]{1,0:T(8,128)(2,1)S(1)} %get-tuple-element.64), channel_id=1, source_target_pairs={{0,3},{1,0},{2,1},{3,2},{4,7},{5,4},{6,5},{7,6},{8,11},{9,8},{10,9... | collective-permute-start | bytes 786440 | tf_op jit(solution)/shard_map/ppermute | solution.py:456

commit v6 on v5

--- a/solution.py
+++ b/solution.py
@@ -425,7 +425,9 @@
     for at in reversed(range(1, m)):
         leaving = (slab_state + slab_keep * later.astype(F32)).astype(BF16)
         if at == m - 1:
-            leaving = gate(leaving, blocks[1, 1], blocks[-1, 1], ready_b[0], near_a)
+            leaving = gate(leaving, ready_b[0], near_a)
+        elif at == m - 2:
+            leaving = gate(leaving, blocks[1, 1], blocks[-1, 1])
         later = later + lax.ppermute(
             leaving, "seq", [(2 * at + y, 2 * at - 2 + y) for y in range(2)]
         )
@@ -433,6 +435,7 @@
     other = swap(later)
     cot_b = gate(cot_b, later)
     near_b, state_b = near_part([cot_b], writes_b, reads_b, skip_gain, ready_b, True)
+    other = gate(other, state_b)
     last = jnp.where(first, jnp.stack([later, other]), jnp.stack([other, later]))
     last = last.reshape(heads, width, size)
     state_1, keep_1 = parts_of(jnp.where(first, state_b, state_a), width)

time: 197 us -> 194 us (0.985)
    ppermute x3, waiting for transfers between devices: 7.48 us -> 0.01 us  [body(): lax.ppermute(blocks.get((1, k - 1), weight), 'seq', [(s, s + 2) for s in...]
    ppermute x2, waiting for transfers between devices: 2.9 us -> 8.04 us  [body(): lax.ppermute(blocks.get((-1, k - 1), weight), 'seq', down(k))]
    ppermute x2, starting transfers between devices: 6.7 us -> 4.14 us  [body(): lax.ppermute(blocks.get((-1, k - 1), weight), 'seq', down(k))]
  transfers between devices with their start and end apart: 23 -> 23, of which waited for: 8 -> 7; matrix products, arithmetic and copies ran while one was open for 5% -> 5% of each run, Pallas kernels for 33% -> 33%
where the time goes in v6:
time: 194 us; the launch traced here: 193 us
  waiting for transfers between devices  76.1 us (39%)
  Pallas kernels  66.5 us (34%)
  starting transfers between devices  39.5 us (20%)
  other arithmetic  7.27 us (4%)
  local copies, waits for them, and re-layouts  3.57 us (2%)
    ppermute x3, waiting for transfers between devices, body(): lax.ppermute(leaving, 'seq', [(2 * at + y, 2 * at - 2 + y) for y in range...  58.4 us
    pallas_call x2, Pallas kernels, near_part(): pl.pallas_call(functools.partial(near_kernel, chunks, heads, pieces), gri...  28.6 us
    pallas_call x4, Pallas kernels, product(): pl.pallas_call(functools.partial(product_kernel, which), in_specs=[pl.Blo...  13 us
    ppermute x3, starting transfers between devices, body(): lax.ppermute(blocks.get((1, k - 1), weight), 'seq', [(s, s + 2) for s in...  11.1 us
    pallas_call x1, Pallas kernels, far_part(): pl.pallas_call(functools.partial(far_kernel, heads), grid=(heads // GROUP...  10.7 us
    ppermute x8, starting transfers between devices, body(): pieces.append(lax.ppermute(got[flip], ('seq', 'pipe'), route))  9.92 us
    ppermute x8, waiting for transfers between devices, body(): pieces.append(lax.ppermute(got[flip], ('seq', 'pipe'), route))  9.59 us
    ppermute x2, waiting for transfers between devices, body(): lax.ppermute(blocks.get((-1, k - 1), weight), 'seq', down(k))  8.04 us
  transfers between devices with their start and end apart: 23, of which 7 were waited for; matrix products, arithmetic and copies ran while one was open for 5% of the time, Pallas kernels for 33%

profile of v6, /device:TPU:9, one launch (start us, length us, event | category | flops | bytes accessed | tf_op | source)
XLA Modules:
  0.0 193.2 jit_solution(4877385641901594012)
XLA Ops:
  0.0 1.9 collective-permute-start.7
  1.9 3.4 %collective-permute-start.6 = (bf16[256,4096]{1,0:T(8,128)(2,1)}, bf16[256,4096]{1,0:T(8,128)(2,1)}, u32[]{:S(2)}, u32[]{:S(2)}) collective-permute-start(bf16[256,4096]{1,0:T(8,128)(2,1)} %bitcast.19), channel_id=1, source_target_pairs={{0,8},{4,12},{8,16},{12,20},{16,24},{20,28},{1,9},{5,13},{9,17},{1... | collective-permute-start | bytes 6291464 | tf_op jit(solution)/shard_map/ppermute | solution.py:402
  5.3 1.3 collective-permute-start
  6.6 0.2 collective-permute-start.1
  6.8 0.7 convert_element_type.53
  7.5 0.8 pad_maximum_fusion.ext_ref
  8.4 1.2 collective-permute-start.2
  9.6 2.5 %prep.2 = (f32[512,128]{1,0:T(8,128)}, f32[8,4,512]{2,1,0:T(4,128)}, f32[8,4,512]{2,1,0:T(4,128)}, f32[8,16,128]{2,1,0:T(8,128)}, f32[8,4,128]{2,1,0:T(4,128)}, ...) custom-call(f32[40,512]{1,0:T(8,128)} %copy-done.11, bf16[512,128]{1,0:T(8,128)(2,1)} %bitcast.31), custom_call_target="tpu_custom_call" | custom-call | tf_op jit(solution)/shard_map/prep/pallas_call | solution.py:211
  12.1 7.1 %states.1 = bf16[32,144,128]{2,1,0:T(8,128)(2,1)} custom-call(bf16[128,512]{1,0:T(8,128)(2,1)} %get-tuple-element.37.readst_ref, f32[8,4,512]{2,1,0:T(4,128)} %get-tuple-element.44.allr_ref, f32[8,4,128]{2,1,0:T(4,128)} %get-tuple-element.43.whole_ref, bf16[512,4096]{1,0:T(8,128)(2,1)} %bitcast.27), custom_call_target="tpu_custom_call" | custom-call | tf_op jit(solution)/shard_map/states/pallas_call | solution.py:266
  19.2 1.9 constant_dynamic-slice_fusion
  21.2 0.7 collective-permute-start.4
  21.9 0.8 collective-permute-start.3
  22.7 13.3 %near.2.refs_0_ = bf16[512,4096]{1,0:T(8,128)(2,1)} custom-call(f32[1,32]{1,0:T(1,128)} %gain_ref.3, bf16[512,128]{1,0:T(8,128)(2,1)} %bitcast.25, bf16[512,128]{1,0:T(8,128)(2,1)} %bitcast.32, bf16[128,512]{1,0:T(8,128)(2,1)} %get-tuple-element.37.readst_ref, f32[1,512]{1,0:T(1,128)} %get-tuple-element.38.cntr_ref, ...), custom_call_target="tpu_custom_call" | custom-call | tf_op jit(solution)/shard_map/near/pallas_call | solution.py:230
  36.1 2.5 %prep.3 = (f32[512,128]{1,0:T(8,128)}, f32[8,4,512]{2,1,0:T(4,128)}, f32[8,4,512]{2,1,0:T(4,128)}, f32[8,16,128]{2,1,0:T(8,128)}, f32[8,4,128]{2,1,0:T(4,128)}, ...) custom-call(f32[40,512]{1,0:T(8,128)} %copy-done.12, bf16[512,128]{1,0:T(8,128)(2,1)} %copy-done.10), custom_call_target="tpu_custom_call" | custom-call | tf_op jit(solution)/shard_map/prep/pallas_call | solution.py:211
  38.5 1.2 broadcast_select_fusion.2
  39.7 0.2 add_convert_fusion.3
  40.0 0.7 collective-permute-start.5
  40.7 8.0 %collective-permute-done.7.refs_0_.refs_1_.refs_2_ = bf16[256,4096]{1,0:T(8,128)(2,1)S(1)} collective-permute-done((bf16[256,4096]{1,0:T(8,128)(2,1)}, bf16[256,4096]{1,0:T(8,128)(2,1)S(1)}, u32[]{:S(2)}, u32[]{:S(2)}) %collective-permute-start.7) | collective-permute-done | bytes 2097184 | tf_op jit(solution)/shard_map/ppermute | solution.py:407
  48.7 2.2 %collective-permute-start.15 = (bf16[256,4096]{1,0:T(8,128)(2,1)S(1)}, bf16[256,4096]{1,0:T(8,128)(2,1)}, u32[]{:S(2)}, u32[]{:S(2)}) collective-permute-start(bf16[256,4096]{1,0:T(8,128)(2,1)S(1)} %collective-permute-done.7.refs_0_.refs_1_.refs_2_), channel_id=1, source_target_pairs={{8,0},{12,4},{16,8},{20,12},{9,1},{13,5},{17,9},{21,13},{10,2},{14... | collective-permute-start | bytes 6291464 | tf_op jit(solution)/shard_map/ppermute | solution.py:407
  50.9 5.7 %collective-permute-start.16 = (bf16[256,4096]{1,0:T(8,128)(2,1)}, bf16[256,4096]{1,0:T(8,128)(2,1)}, u32[]{:S(2)}, u32[]{:S(2)}) collective-permute-start(bf16[256,4096]{1,0:T(8,128)(2,1)} %collective-permute-done.6.refs_1_.refs_2_.refs_3_), channel_id=1, source_target_pairs={{8,16},{12,20},{16,24},{20,28},{9,17},{13,21},{17,25},{21,29},{10,... | collective-permute-start | bytes 6291464 | tf_op jit(solution)/shard_map/ppermute | solution.py:402
  56.6 0.3 add_convert_fusion.2
  56.9 1.3 collective-permute-start.8
  58.2 49.3 %collective-permute-done.8 = bf16[16,128,128]{2,1,0:T(8,128)(2,1)S(1)} collective-permute-done((bf16[16,128,128]{2,1,0:T(8,128)(2,1)S(1)}, bf16[16,128,128]{2,1,0:T(8,128)(2,1)S(1)}, u32[]{:S(2)}, u32[]{:S(2)}) %collective-permute-start.8) | collective-permute-done | bytes 524320 | tf_op jit(solution)/shard_map/ppermute | solution.py:431
  107.5 0.4 add_convert_fusion.1
  107.9 1.3 collective-permute-start.9
  109.3 9.1 %collective-permute-done.9 = bf16[16,128,128]{2,1,0:T(8,128)(2,1)S(1)} collective-permute-done((bf16[16,128,128]{2,1,0:T(8,128)(2,1)S(1)}, bf16[16,128,128]{2,1,0:T(8,128)(2,1)S(1)}, u32[]{:S(2)}, u32[]{:S(2)}) %collective-permute-start.9) | collective-permute-done | bytes 524320 | tf_op jit(solution)/shard_map/ppermute | solution.py:431
  118.4 0.9 add.51
  119.3 5.5 %collective-permute-start.19 = (bf16[256,4096]{1,0:T(8,128)(2,1)}, bf16[256,4096]{1,0:T(8,128)(2,1)}, u32[]{:S(2)}, u32[]{:S(2)}) collective-permute-start(bf16[256,4096]{1,0:T(8,128)(2,1)} %collective-permute-done.15.refs_0_.refs_1_), channel_id=1, source_target_pairs={{8,0},{12,4},{9,1},{13,5},{10,2},{14,6},{11,3},{15,7}} | collective-permute-start | bytes 6291464 | tf_op jit(solution)/shard_map/ppermute | solution.py:434
  124.9 2.0 %collective-permute-start.20 = (bf16[256,4096]{1,0:T(8,128)(2,1)}, bf16[256,4096]{1,0:T(8,128)(2,1)}, u32[]{:S(2)}, u32[]{:S(2)}) collective-permute-start(bf16[256,4096]{1,0:T(8,128)(2,1)} %collective-permute-done.16.refs_3_.refs_2_), channel_id=1, source_target_pairs={{16,24},{20,28},{17,25},{21,29},{18,26},{22,30},{19,27},{23,31}} | collective-permute-start | bytes 6291464 | tf_op jit(solution)/shard_map/ppermute | solution.py:402
  126.9 1.2 collective-permute-start.10
  128.1 15.2 %near.3 = (bf16[512,4096]{1,0:T(8,128)(2,1)}, bf16[32,144,128]{2,1,0:T(8,128)(2,1)}) custom-call(f32[1,32]{1,0:T(1,128)} %gain_ref.3, bf16[512,128]{1,0:T(8,128)(2,1)} %copy-done.4, bf16[512,128]{1,0:T(8,128)(2,1)} %copy-done.10, bf16[128,512]{1,0:T(8,128)(2,1)} %get-tuple-element.46.readst_ref, f32[1,512]{1,0:T(1,128)} %get-tuple-element.47.cntr_ref, ...), custom_call_target="tpu_custom_call" | custom-call | tf_op jit(solution)/shard_map/near/pallas_call | solution.py:230
  143.4 1.8 maximum_select_fusion
  145.4 0.8 fusion
  146.4 1.4 copy-done.1
  147.8 10.7 %far.1.x_ref = bf16[1024,4096]{1,0:T(8,128)(2,1)S(1)} custom-call(bf16[512,4096]{1,0:T(8,128)(2,1)S(1)} %copy-done.1, bf16[512,4096]{1,0:T(8,128)(2,1)} %get-tuple-element.57.refs_1_, bf16[512,128]{1,0:T(8,128)(2,1)S(1)} %bitcast.26, bf16[512,128]{1,0:T(8,128)(2,1)S(1)} %copy-done.5, f32[512,128]{1,0:T(8,128)S(1)} %copy-done.3, f32[512,128]{1,0:T(8,128)S(1)} %copy-done.2, ...), custom_call_target="tpu_custom_call" | custom-call | tf_op jit(solution)/shard_map/far/pallas_call | solution.py:303
  158.4 2.5 %product.4 = (bf16[512,256]{1,0:T(8,128)(2,1)S(1)}, bf16[512,256]{1,0:T(8,128)(2,1)S(1)}) custom-call(s32[1]{0:T(128)} %bitcast.1.slab_ref, bf16[1024,4096]{1,0:T(8,128)(2,1)S(1)} %far.1.x_ref, bf16[256,4096]{1,0:T(8,128)(2,1)S(1)} %bitcast.20, bf16[256,4096]{1,0:T(8,128)(2,1)S(1)} %bitcast.21, bf16[256,4096]{1,0:T(8,128)(2,1)S(1)} %bitcast.22, ...), custom_call_target="tpu_custom_call" | custom-call | tf_op jit(solution)/shard_map/product/pallas_call | solution.py:322
  161.0 3.6 %collective-permute-start.11 = (bf16[512,256]{1,0:T(8,128)(2,1)S(1)}, bf16[512,256]{1,0:T(8,128)(2,1)S(1)}, u32[]{:S(2)}, u32[]{:S(2)}) collective-permute-start(bf16[512,256]{1,0:T(8,128)(2,1)S(1)} %get-tuple-element.60), channel_id=1, source_target_pairs={{0,7},{1,4},{2,5},{3,6},{4,3},{5,0},{6,1},{7,2},{8,15},{9,12},{10,... | collective-permute-start | bytes 786440 | tf_op jit(solution)/shard_map/ppermute | solution.py:459
  164.6 4.0 %product.5 = (bf16[512,256]{1,0:T(8,128)(2,1)S(1)}, bf16[512,256]{1,0:T(8,128)(2,1)S(1)}) custom-call(s32[1]{0:T(128)} %bitcast.1.slab_ref, bf16[1024,4096]{1,0:T(8,128)(2,1)S(1)} %far.1.x_ref, bf16[256,4096]{1,0:T(8,128)(2,1)S(1)} %collective-permute-done.7.refs_0_.refs_1_.refs_2_, bf16[256,4096]{1,0:T(8,128)(2,1)} %collective-permute-done.6.refs_1_.refs_2_.refs_3_, ...), custom_call_target="tpu_custom_call" | custom-call | tf_op jit(solution)/shard_map/product/pallas_call | solution.py:322
  168.6 2.8 %collective-permute-start.13 = (bf16[512,256]{1,0:T(8,128)(2,1)S(1)}, bf16[512,256]{1,0:T(8,128)(2,1)S(1)}, u32[]{:S(2)}, u32[]{:S(2)}) collective-permute-start(bf16[512,256]{1,0:T(8,128)(2,1)S(1)} %get-tuple-element.62), channel_id=1, source_target_pairs={{0,7},{1,4},{2,5},{3,6},{4,3},{5,0},{6,1},{7,2},{8,15},{9,12},{10,... | collective-permute-start | bytes 786440 | tf_op jit(solution)/shard_map/ppermute | solution.py:459
  171.3 2.5 %product.6 = (bf16[512,256]{1,0:T(8,128)(2,1)S(1)}, bf16[512,256]{1,0:T(8,128)(2,1)S(1)}) custom-call(s32[1]{0:T(128)} %bitcast.1.slab_ref, bf16[1024,4096]{1,0:T(8,128)(2,1)S(1)} %far.1.x_ref, bf16[256,4096]{1,0:T(8,128)(2,1)} %collective-permute-done.15.refs_0_.refs_1_, bf16[256,4096]{1,0:T(8,128)(2,1)S(1)} %collective-permute-done.7.refs_0_.refs_1_.refs_2_, ...), custom_call_target="tpu_custom_call" | custom-call | tf_op jit(solution)/shard_map/product/pallas_call | solution.py:322
  174.0 0.7 collective-permute-start.17
  174.7 4.0 %product.7 = (bf16[512,256]{1,0:T(8,128)(2,1)S(1)}, bf16[512,256]{1,0:T(8,128)(2,1)S(1)}) custom-call(s32[1]{0:T(128)} %bitcast.1.slab_ref, bf16[1024,4096]{1,0:T(8,128)(2,1)S(1)} %far.1.x_ref, bf16[256,4096]{1,0:T(8,128)(2,1)} %collective-permute-done.19.refs_0_, bf16[256,4096]{1,0:T(8,128)(2,1)} %collective-permute-done.15.refs_0_.refs_1_, ...), custom_call_target="tpu_custom_call" | custom-call | tf_op jit(solution)/shard_map/product/pallas_call | solution.py:322
  178.8 2.7 %collective-permute-start.21 = (bf16[512,256]{1,0:T(8,128)(2,1)S(1)}, bf16[512,256]{1,0:T(8,128)(2,1)S(1)}, u32[]{:S(2)}, u32[]{:S(2)}) collective-permute-start(bf16[512,256]{1,0:T(8,128)(2,1)S(1)} %get-tuple-element.67), channel_id=1, source_target_pairs={{0,7},{1,4},{2,5},{3,6},{4,3},{5,0},{6,1},{7,2},{8,15},{9,12},{10,... | collective-permute-start | bytes 786440 | tf_op jit(solution)/shard_map/ppermute | solution.py:459
  181.5 1.6 collective-permute-done.17.refs_4_
  183.1 2.6 %collective-permute-done.18.refs_5_ = bf16[512,256]{1,0:T(8,128)(2,1)S(1)} collective-permute-done((bf16[512,256]{1,0:T(8,128)(2,1)S(1)}, bf16[512,256]{1,0:T(8,128)(2,1)S(1)}, u32[]{:S(2)}, u32[]{:S(2)}) %collective-permute-start.18) | collective-permute-done | bytes 262176 | tf_op jit(solution)/shard_map/ppermute | solution.py:459
  185.7 3.0 %collective-permute-done.21.refs_6_ = bf16[512,256]{1,0:T(8,128)(2,1)S(1)} collective-permute-done((bf16[512,256]{1,0:T(8,128)(2,1)S(1)}, bf16[512,256]{1,0:T(8,128)(2,1)S(1)}, u32[]{:S(2)}, u32[]{:S(2)}) %collective-permute-start.21) | collective-permute-done | bytes 262176 | tf_op jit(solution)/shard_map/ppermute | solution.py:459
  188.7 2.4 %collective-permute-done.22.refs_7_ = bf16[512,256]{1,0:T(8,128)(2,1)S(1)} collective-permute-done((bf16[512,256]{1,0:T(8,128)(2,1)S(1)}, bf16[512,256]{1,0:T(8,128)(2,1)S(1)}, u32[]{:S(2)}, u32[]{:S(2)}) %collective-permute-start.22) | collective-permute-done | bytes 262176 | tf_op jit(solution)/shard_map/ppermute | solution.py:459
  191.0 2.2 %assemble.1 = bf16[1,512,2048]{2,1,0:T(8,128)(2,1)} custom-call(s32[1]{0:T(128)} %bitcast.mine_ref, s32[8,8]{1,0:T(8,128)S(1)} %copy-done.7, bf16[512,256]{1,0:T(8,128)(2,1)S(1)} %collective-permute-done.11.refs_0_, bf16[512,256]{1,0:T(8,128)(2,1)S(1)} %collective-permute-done.12.refs_1_, bf16[512,256]{1,0:T(8,128)(2,1)S(1)} %collective-permute-done.13.refs_2_, ...), custom_call_target="tpu_custom_call" | custom-call | tf_op jit(solution)/shard_map/assemble/pallas_call | solution.py:362
  (50 shorter events, 0.6 us)
Async XLA Ops:
  0.0 48.7 %collective-permute-start.7 = (bf16[256,4096]{1,0:T(8,128)(2,1)}, bf16[256,4096]{1,0:T(8,128)(2,1)S(1)}, u32[]{:S(2)}, u32[]{:S(2)}) collective-permute-start(bf16[256,4096]{1,0:T(8,128)(2,1)} %bitcast.18), channel_id=1, source_target_pairs={{8,0},{12,4},{16,8},{20,12},{24,16},{28,20},{9,1},{13,5},{17,9},{2... | collective-permute-start | bytes 6291464 | tf_op jit(solution)/shard_map/ppermute | solution.py:407
  1.9 49.0 %collective-permute-start.6 = (bf16[256,4096]{1,0:T(8,128)(2,1)}, bf16[256,4096]{1,0:T(8,128)(2,1)}, u32[]{:S(2)}, u32[]{:S(2)}) collective-permute-start(bf16[256,4096]{1,0:T(8,128)(2,1)} %bitcast.19), channel_id=1, source_target_pairs={{0,8},{4,12},{8,16},{12,20},{16,24},{20,28},{1,9},{5,13},{9,17},{1... | collective-permute-start | bytes 6291464 | tf_op jit(solution)/shard_map/ppermute | solution.py:402
  5.3 15.9 %collective-permute-start = (bf16[512,128]{1,0:T(8,128)(2,1)}, bf16[512,128]{1,0:T(8,128)(2,1)S(1)}, u32[]{:S(2)}, u32[]{:S(2)}) collective-permute-start(bf16[512,128]{1,0:T(8,128)(2,1)} %bitcast.24), channel_id=1, source_target_pairs={{0,4},{4,0},{8,12},{12,8},{16,20},{20,16},{24,28},{28,24},{1,5},{5... | collective-permute-start | bytes 393224 | tf_op jit(solution)/shard_map/ppermute | solution.py:395
  6.6 14.6 %collective-permute-start.1 = (bf16[512,128]{1,0:T(8,128)(2,1)}, bf16[512,128]{1,0:T(8,128)(2,1)S(1)}, u32[]{:S(2)}, u32[]{:S(2)}) collective-permute-start(bf16[512,128]{1,0:T(8,128)(2,1)} %bitcast.30), channel_id=1, source_target_pairs={{0,4},{4,0},{8,12},{12,8},{16,20},{20,16},{24,28},{28,24},{1,5},{5... | collective-permute-start | bytes 393224 | tf_op jit(solution)/shard_map/ppermute | solution.py:395
  8.4 1.2 copy-start.11
  8.4 12.8 %collective-permute-start.2 = (f32[40,512]{1,0:T(8,128)S(1)}, f32[40,512]{1,0:T(8,128)S(1)}, u32[]{:S(2)}, u32[]{:S(2)}) collective-permute-start(f32[40,512]{1,0:T(8,128)S(1)} %pad_maximum_fusion.ext_ref), channel_id=1, source_target_pairs={{0,4},{4,0},{8,12},{12,8},{16,20},{20,16},{24,28},{28,24},{1,5},{5... | collective-permute-start | bytes 245768 | tf_op jit(solution)/shard_map/ppermute | solution.py:395
  21.1 1.6 copy-start.12
  21.2 14.9 %copy-start.4 = (bf16[512,128]{1,0:T(8,128)(2,1)}, bf16[512,128]{1,0:T(8,128)(2,1)S(1)}, u32[]{:S(2)}) copy-start(bf16[512,128]{1,0:T(8,128)(2,1)S(1)} %collective-permute-done.writes_ref.refs_3_) | copy-start | bytes 393220
  21.2 14.9 %copy-start.10 = (bf16[512,128]{1,0:T(8,128)(2,1)}, bf16[512,128]{1,0:T(8,128)(2,1)S(1)}, u32[]{:S(2)}) copy-start(bf16[512,128]{1,0:T(8,128)(2,1)S(1)} %collective-permute-done.1.reads_ref) | copy-start | bytes 393220
  21.2 17.4 %collective-permute-start.4 = (bf16[16,144,128]{2,1,0:T(8,128)(2,1)}, bf16[16,144,128]{2,1,0:T(8,128)(2,1)}, u32[]{:S(2)}, u32[]{:S(2)}) collective-permute-start(bf16[16,144,128]{2,1,0:T(8,128)(2,1)} %constant_dynamic-slice_fusion), channel_id=1, source_target_pairs={{0,4},{4,0},{8,12},{12,8},{16,20},{20,16},{24,28},{28,24},{1,5},{5... | collective-permute-start | bytes 1769480 | tf_op jit(solution)/shard_map/ppermute | solution.py:395
  21.9 106.3 %collective-permute-start.3 = (bf16[512,4096]{1,0:T(8,128)(2,1)}, bf16[512,4096]{1,0:T(8,128)(2,1)}, u32[]{:S(2)}, u32[]{:S(2)}) collective-permute-start(bf16[512,4096]{1,0:T(8,128)(2,1)} %bitcast.28), channel_id=1, source_target_pairs={{0,4},{4,0},{8,12},{12,8},{16,20},{20,16},{24,28},{28,24},{1,5},{5... | collective-permute-start | bytes 12582920 | tf_op jit(solution)/shard_map/ppermute | solution.py:395
  22.7 15.8 %copy-start.8 = (bf16[32,144,128]{2,1,0:T(8,128)(2,1)S(1)}, bf16[32,144,128]{2,1,0:T(8,128)(2,1)}, u32[]{:S(2)}) copy-start(bf16[32,144,128]{2,1,0:T(8,128)(2,1)} %states.1) | copy-start | bytes 3538948
  40.0 16.7 %collective-permute-start.5 = (bf16[16,128,128]{2,1,0:T(8,128)(2,1)S(1)}, bf16[16,128,128]{2,1,0:T(8,128)(2,1)S(1)}, u32[]{:S(2)}, u32[]{:S(2)}) collective-permute-start(bf16[16,128,128]{2,1,0:T(8,128)(2,1)S(1)} %add_convert_fusion.3), channel_id=1, source_target_pairs={{24,16},{28,20},{25,17},{29,21},{26,18},{30,22},{27,19},{31,23}} | collective-permute-start | bytes 1572872 | tf_op jit(solution)/shard_map/ppermute | solution.py:431
  48.7 70.6 %collective-permute-start.15 = (bf16[256,4096]{1,0:T(8,128)(2,1)S(1)}, bf16[256,4096]{1,0:T(8,128)(2,1)}, u32[]{:S(2)}, u32[]{:S(2)}) collective-permute-start(bf16[256,4096]{1,0:T(8,128)(2,1)S(1)} %collective-permute-done.7.refs_0_.refs_1_.refs_2_), channel_id=1, source_target_pairs={{8,0},{12,4},{16,8},{20,12},{9,1},{13,5},{17,9},{21,13},{10,2},{14... | collective-permute-start | bytes 6291464 | tf_op jit(solution)/shard_map/ppermute | solution.py:407
  50.9 73.9 %collective-permute-start.16 = (bf16[256,4096]{1,0:T(8,128)(2,1)}, bf16[256,4096]{1,0:T(8,128)(2,1)}, u32[]{:S(2)}, u32[]{:S(2)}) collective-permute-start(bf16[256,4096]{1,0:T(8,128)(2,1)} %collective-permute-done.6.refs_1_.refs_2_.refs_3_), channel_id=1, source_target_pairs={{8,16},{12,20},{16,24},{20,28},{9,17},{13,21},{17,25},{21,29},{10,... | collective-permute-start | bytes 6291464 | tf_op jit(solution)/shard_map/ppermute | solution.py:402
  56.9 50.6 %collective-permute-start.8 = (bf16[16,128,128]{2,1,0:T(8,128)(2,1)S(1)}, bf16[16,128,128]{2,1,0:T(8,128)(2,1)S(1)}, u32[]{:S(2)}, u32[]{:S(2)}) collective-permute-start(bf16[16,128,128]{2,1,0:T(8,128)(2,1)S(1)} %add_convert_fusion.2), channel_id=1, source_target_pairs={{16,8},{20,12},{17,9},{21,13},{18,10},{22,14},{19,11},{23,15}} | collective-permute-start | bytes 1572872 | tf_op jit(solution)/shard_map/ppermute | solution.py:431
  107.9 10.4 %collective-permute-start.9 = (bf16[16,128,128]{2,1,0:T(8,128)(2,1)S(1)}, bf16[16,128,128]{2,1,0:T(8,128)(2,1)S(1)}, u32[]{:S(2)}, u32[]{:S(2)}) collective-permute-start(bf16[16,128,128]{2,1,0:T(8,128)(2,1)S(1)} %get-tuple-element.69), channel_id=1, source_target_pairs={{8,0},{12,4},{9,1},{13,5},{10,2},{14,6},{11,3},{15,7}} | collective-permute-start | bytes 1572872 | tf_op jit(solution)/shard_map/ppermute | solution.py:431
  119.3 54.5 %collective-permute-start.19 = (bf16[256,4096]{1,0:T(8,128)(2,1)}, bf16[256,4096]{1,0:T(8,128)(2,1)}, u32[]{:S(2)}, u32[]{:S(2)}) collective-permute-start(bf16[256,4096]{1,0:T(8,128)(2,1)} %collective-permute-done.15.refs_0_.refs_1_), channel_id=1, source_target_pairs={{8,0},{12,4},{9,1},{13,5},{10,2},{14,6},{11,3},{15,7}} | collective-permute-start | bytes 6291464 | tf_op jit(solution)/shard_map/ppermute | solution.py:434
  124.9 49.1 %collective-permute-start.20 = (bf16[256,4096]{1,0:T(8,128)(2,1)}, bf16[256,4096]{1,0:T(8,128)(2,1)}, u32[]{:S(2)}, u32[]{:S(2)}) collective-permute-start(bf16[256,4096]{1,0:T(8,128)(2,1)} %collective-permute-done.16.refs_3_.refs_2_), channel_id=1, source_target_pairs={{16,24},{20,28},{17,25},{21,29},{18,26},{22,30},{19,27},{23,31}} | collective-permute-start | bytes 6291464 | tf_op jit(solution)/shard_map/ppermute | solution.py:402
  126.9 16.5 %collective-permute-start.10 = (bf16[16,128,128]{2,1,0:T(8,128)(2,1)}, bf16[16,128,128]{2,1,0:T(8,128)(2,1)}, u32[]{:S(2)}, u32[]{:S(2)}) collective-permute-start(bf16[16,128,128]{2,1,0:T(8,128)(2,1)} %add.51), channel_id=1, source_target_pairs={{0,4},{4,0},{8,12},{12,8},{16,20},{20,16},{24,28},{28,24},{1,5},{5... | collective-permute-start | bytes 1572872 | tf_op jit(solution)/shard_map/ppermute | solution.py:395
  143.4 1.9 copy-start.9
  145.3 1.0 copy-start.2
  145.3 1.0 copy-start.3
  145.3 1.1 copy-start.5
  145.3 1.1 copy-start.6
  145.4 2.3 %copy-start.1 = (bf16[512,4096]{1,0:T(8,128)(2,1)S(1)}, bf16[512,4096]{1,0:T(8,128)(2,1)}, u32[]{:S(2)}) copy-start(bf16[512,4096]{1,0:T(8,128)(2,1)} %near.2.refs_0_) | copy-start | bytes 12582916
  147.7 10.7 %copy-start = (bf16[1,256,4096]{2,1,0:T(8,128)(2,1)S(1)}, bf16[1,256,4096]{2,1,0:T(8,128)(2,1)}, u32[]{:S(2)}) copy-start(bf16[1,256,4096]{2,1,0:T(8,128)(2,1)} %param.14) | copy-start | bytes 6291460
  161.0 17.7 %collective-permute-start.11 = (bf16[512,256]{1,0:T(8,128)(2,1)S(1)}, bf16[512,256]{1,0:T(8,128)(2,1)S(1)}, u32[]{:S(2)}, u32[]{:S(2)}) collective-permute-start(bf16[512,256]{1,0:T(8,128)(2,1)S(1)} %get-tuple-element.60), channel_id=1, source_target_pairs={{0,7},{1,4},{2,5},{3,6},{4,3},{5,0},{6,1},{7,2},{8,15},{9,12},{10,... | collective-permute-start | bytes 786440 | tf_op jit(solution)/shard_map/ppermute | solution.py:459
  164.6 14.2 %collective-permute-start.12 = (bf16[512,256]{1,0:T(8,128)(2,1)S(1)}, bf16[512,256]{1,0:T(8,128)(2,1)S(1)}, u32[]{:S(2)}, u32[]{:S(2)}) collective-permute-start(bf16[512,256]{1,0:T(8,128)(2,1)S(1)} %get-tuple-element.61), channel_id=1, source_target_pairs={{0,3},{1,0},{2,1},{3,2},{4,7},{5,4},{6,5},{7,6},{8,11},{9,8},{10,9... | collective-permute-start | bytes 786440 | tf_op jit(solution)/shard_map/ppermute | solution.py:459
  168.6 12.9 %collective-permute-start.13 = (bf16[512,256]{1,0:T(8,128)(2,1)S(1)}, bf16[512,256]{1,0:T(8,128)(2,1)S(1)}, u32[]{:S(2)}, u32[]{:S(2)}) collective-permute-start(bf16[512,256]{1,0:T(8,128)(2,1)S(1)} %get-tuple-element.62), channel_id=1, source_target_pairs={{0,7},{1,4},{2,5},{3,6},{4,3},{5,0},{6,1},{7,2},{8,15},{9,12},{10,... | collective-permute-start | bytes 786440 | tf_op jit(solution)/shard_map/ppermute | solution.py:459
  173.9 7.6 %collective-permute-start.14 = (bf16[512,256]{1,0:T(8,128)(2,1)S(1)}, bf16[512,256]{1,0:T(8,128)(2,1)S(1)}, u32[]{:S(2)}, u32[]{:S(2)}) collective-permute-start(bf16[512,256]{1,0:T(8,128)(2,1)S(1)} %get-tuple-element.63), channel_id=1, source_target_pairs={{0,3},{1,0},{2,1},{3,2},{4,7},{5,4},{6,5},{7,6},{8,11},{9,8},{10,9... | collective-permute-start | bytes 786440 | tf_op jit(solution)/shard_map/ppermute | solution.py:459
  173.9 17.1 %copy-start.7 = (s32[8,8]{1,0:T(8,128)S(1)}, s32[8,8]{1,0:T(8,128)}, u32[]{:S(2)}) copy-start(s32[8,8]{1,0:T(8,128)} %constant.41.clone.columns_ref) | copy-start | bytes 772
  174.0 9.1 %collective-permute-start.17 = (bf16[512,256]{1,0:T(8,128)(2,1)S(1)}, bf16[512,256]{1,0:T(8,128)(2,1)S(1)}, u32[]{:S(2)}, u32[]{:S(2)}) collective-permute-start(bf16[512,256]{1,0:T(8,128)(2,1)S(1)} %get-tuple-element.64), channel_id=1, source_target_pairs={{0,7},{1,4},{2,5},{3,6},{4,3},{5,0},{6,1},{7,2},{8,15},{9,12},{10,... | collective-permute-start | bytes 786440 | tf_op jit(solution)/shard_map/ppermute | solution.py:459
  178.7 7.0 %collective-permute-start.18 = (bf16[512,256]{1,0:T(8,128)(2,1)S(1)}, bf16[512,256]{1,0:T(8,128)(2,1)S(1)}, u32[]{:S(2)}, u32[]{:S(2)}) collective-permute-start(bf16[512,256]{1,0:T(8,128)(2,1)S(1)} %get-tuple-element.65), channel_id=1, source_target_pairs={{0,3},{1,0},{2,1},{3,2},{4,7},{5,4},{6,5},{7,6},{8,11},{9,8},{10,9... | collective-permute-start | bytes 786440 | tf_op jit(solution)/shard_map/ppermute | solution.py:459
  178.8 9.9 %collective-permute-start.21 = (bf16[512,256]{1,0:T(8,128)(2,1)S(1)}, bf16[512,256]{1,0:T(8,128)(2,1)S(1)}, u32[]{:S(2)}, u32[]{:S(2)}) collective-permute-start(bf16[512,256]{1,0:T(8,128)(2,1)S(1)} %get-tuple-element.67), channel_id=1, source_target_pairs={{0,7},{1,4},{2,5},{3,6},{4,3},{5,0},{6,1},{7,2},{8,15},{9,12},{10,... | collective-permute-start | bytes 786440 | tf_op jit(solution)/shard_map/ppermute | solution.py:459
  181.5 9.6 %collective-permute-start.22 = (bf16[512,256]{1,0:T(8,128)(2,1)S(1)}, bf16[512,256]{1,0:T(8,128)(2,1)S(1)}, u32[]{:S(2)}, u32[]{:S(2)}) collective-permute-start(bf16[512,256]{1,0:T(8,128)(2,1)S(1)} %get-tuple-element.68), channel_id=1, source_target_pairs={{0,3},{1,0},{2,1},{3,2},{4,7},{5,4},{6,5},{7,6},{8,11},{9,8},{10,9... | collective-permute-start | bytes 786440 | tf_op jit(solution)/shard_map/ppermute | solution.py:459
